TPU v7x, 128 devices: a whole 4x4x4 slice. The times are simulated.
128 devices in a mesh: wall: 16 (over x, z), span: 8 (over y, core).
Axes of the slice: x: 4, y: 4, z: 4, core: 2. Of those that a mesh axis runs over, the one named last changes fastest.
Arguments:
- velocity: float32 [3, 512, 128, 1024], P(None, 'wall', 'span'), may hold values from -6 to 6
- lower: float32 [512], replicated, may hold values from 0.01 to 0.95, as said below
- upper: float32 [512], replicated, may hold values from 0.01 to 0.965
- stencil: float32 [5, 512], P(None, 'wall'), may hold values from -1 to 1
- inv_volume: float32 [512], P('wall'), may hold values from 0.5 to 4
- forces: float32 [3, 524288], P(None, ('wall', 'span')), may hold values from -6 to 6
- owner: int32 [524288, 1], P(('wall', 'span')), may hold values from 0 to 127; in each aligned block of 4096 rows (0 to 4095, 4096 to 8191, ...) at most 64 rows name the same one
- cells: int32 [524288], P(('wall', 'span')), may hold values from 0 to 524287
- counts: int32 [128], P(('wall', 'span')), may hold values from 1 to 4096, 393216 in all
Outputs:
- derivative: float32 [3, 512, 128, 1024], P(None, 'wall', 'span')
- forcing: float32 [3, 512, 128, 1024], P(None, 'wall', 'span')
Inputs may be any that keep to these rules, and one draw needn't show every extreme that they name: Among the 4096 slots of one device no owner is named more than 64 times, a bound that some block reaches. The counts sum to 393216 and some device is full. lower[j] + upper[j] stays below 1 in every row.
All inputs are finite; a program needn't handle non-finite values.
Results may differ from a plain program's by a relative error of at most 0.0003.
Values sent between devices are 32-bit elements; how exact they have to be, the bound alone decides.
A program may use at most 128 MiB of HBM per device.

v0:
```python
import jax
import jax.numpy as jnp
from jax import lax
from jax.sharding import PartitionSpec as P


def with_halo(cells, sides, width):
    for axis, dim in sides:
        count = lax.axis_size(axis)
        ends = count - 1
        head = lax.slice_in_dim(cells, 0, width, axis=dim)
        tail = lax.slice_in_dim(cells, cells.shape[dim] - width, cells.shape[dim], axis=dim)
        cells = jnp.concatenate(
            [
                lax.ppermute(tail, axis, [(i, (i + 1) % count) for i in range(ends)]),
                cells,
                lax.ppermute(head, axis, [((i + 1) % count, i) for i in range(ends)]),
            ],
            axis=dim,
        )
    return cells


def carried_in(value, axis, join, neutral, backward):
    count, mine = (lax.axis_size(axis), lax.axis_index(axis))
    pieces = jax.tree.map(lambda part: lax.all_gather(part, axis), value)
    if backward:
        pieces = jax.tree.map(lambda part: part[::-1], pieces)
        mine = count - 1 - mine
    running = jax.tree.map(
        lambda part, zero: jnp.full_like(part, 0) + jnp.asarray(zero, part.dtype), value, neutral
    )

    def lap(position, running):
        longer = join(running, jax.tree.map(lambda part: part[position], pieces))
        return jax.tree.map(lambda new, old: jnp.where(position < mine, new, old), longer, running)

    return lax.fori_loop(0, count - 1, lap, running)


def pivot_rows(sub_diag, super_diag):

    def advance(carried, row_pair):
        lower_row, upper_row = row_pair
        pivot_now = 1.0 - lower_row * carried
        ratio_now = upper_row / pivot_now
        return (ratio_now, (pivot_now, ratio_now))

    initial = jnp.zeros((), jnp.float32)
    _unused, (pivots, ratios) = lax.scan(advance, initial, (sub_diag, super_diag))
    return (pivots, ratios)


def sweep_solve(sub_diag, pivots, ratios, right_side):

    def forward(previous, row_entry):
        lower_row, pivot_row, value_row = row_entry
        current = (value_row - lower_row * previous) / pivot_row
        return (current, current)

    _unused, reduced = lax.scan(
        forward, jnp.zeros_like(right_side[0]), (sub_diag, pivots, right_side)
    )

    def backward(following, row_entry):
        ratio_row, reduced_row = row_entry
        current = reduced_row - ratio_row * following
        return (current, current)

    _unused2, solved = lax.scan(
        backward, jnp.zeros_like(right_side[0]), (ratios, reduced), reverse=True
    )
    return solved


def pick_entry(values, position):
    return lax.dynamic_index_in_dim(values, position, 0, keepdims=False)


def compose(earlier_map, later_map):
    return (later_map[0] * earlier_map[0], later_map[0] * earlier_map[1] + later_map[1])


def slab_factors(sub_all, super_all):
    depth_rows = sub_all.shape[0]
    local_sub = sub_all.at[0].set(0.0)
    local_super = super_all.at[depth_rows - 1].set(0.0)
    pivots, ratios = pivot_rows(local_sub, local_super)
    below_unit = jnp.zeros((depth_rows,), jnp.float32).at[0].set(-sub_all[0])
    above_unit = (
        jnp.zeros((depth_rows,), jnp.float32).at[depth_rows - 1].set(-super_all[depth_rows - 1])
    )
    from_below = sweep_solve(local_sub, pivots, ratios, below_unit)
    from_above = sweep_solve(local_sub, pivots, ratios, above_unit)
    first_ratio = from_above[0] / from_above[depth_rows - 1]
    last_ratio = from_below[depth_rows - 1] / from_below[0]
    coupling = jnp.stack(
        [
            first_ratio * from_below[depth_rows - 1] - from_below[0],
            -first_ratio,
            -last_ratio,
            last_ratio * from_above[0] - from_above[depth_rows - 1],
        ]
    )
    return (local_sub, pivots, ratios, from_below, from_above, first_ratio, last_ratio, coupling)


def slab_coupling(sub_all, super_all):
    return slab_factors(sub_all, super_all)[7]


def body(velocity, lower, upper, stencil, inv_volume, forces, owner, cells, counts):
    components, depth_rows, span_width, stream_width = velocity.shape
    padded = with_halo(velocity, (("wall", 1),), 2)
    stencil_sum = stencil[0][None, :, None, None] * padded[:, 0:depth_rows]
    for offset in range(1, 5):
        stencil_sum = (
            stencil_sum
            + stencil[offset][None, :, None, None] * padded[:, offset : offset + depth_rows]
        )
    right_side = jnp.moveaxis(stencil_sum, 1, 0).reshape(
        depth_rows, components * span_width, stream_width
    )
    slab_count = lax.axis_size("wall")
    slab_index = lax.axis_index("wall")
    slab_lower = lax.dynamic_slice_in_dim(lower, slab_index * depth_rows, depth_rows)
    slab_upper = lax.dynamic_slice_in_dim(upper, slab_index * depth_rows, depth_rows)
    local_sub, pivots, ratios, from_below, from_above, first_ratio, last_ratio, _own = slab_factors(
        slab_lower, slab_upper
    )
    particular = sweep_solve(local_sub, pivots, ratios, right_side)
    first_row = particular[0] - first_ratio * particular[depth_rows - 1]
    last_row = particular[depth_rows - 1] - last_ratio * particular[0]
    all_coupling = jax.vmap(slab_coupling)(
        lower.reshape(slab_count, depth_rows), upper.reshape(slab_count, depth_rows)
    )
    reduced_sub = all_coupling[:, 0::2].reshape(-1)
    reduced_super = all_coupling[:, 1::2].reshape(-1)
    red_pivots, red_ratios = pivot_rows(reduced_sub, reduced_super)
    sub_first = pick_entry(reduced_sub, 2 * slab_index)
    sub_last = pick_entry(reduced_sub, 2 * slab_index + 1)
    pivot_first = pick_entry(red_pivots, 2 * slab_index)
    pivot_last = pick_entry(red_pivots, 2 * slab_index + 1)
    ratio_first = pick_entry(red_ratios, 2 * slab_index)
    ratio_last = pick_entry(red_ratios, 2 * slab_index + 1)
    ratio_before = pick_entry(jnp.pad(red_ratios, (1, 0)), 2 * slab_index)
    carry_gain = sub_last * sub_first / (pivot_first * pivot_last)
    carry_offset = (last_row - sub_last * first_row / pivot_first) / pivot_last
    identity = (jnp.ones((1, 1), jnp.float32), jnp.zeros_like(first_row))
    _unused_gain, incoming = carried_in(
        (carry_gain.reshape(1, 1), carry_offset), "wall", compose, identity, False
    )
    reduced_first = (first_row - sub_first * incoming) / pivot_first
    reduced_last = (last_row - sub_last * reduced_first) / pivot_last
    back_gain = ratio_first * ratio_last
    back_offset = reduced_first - ratio_first * reduced_last
    _unused_gain2, above_value = carried_in(
        (back_gain.reshape(1, 1), back_offset), "wall", compose, identity, True
    )
    last_value = reduced_last - ratio_last * above_value
    first_value = reduced_first - ratio_first * last_value
    below_value = incoming - ratio_before * first_value
    solved = (
        particular
        + from_below[:, None, None] * below_value[None]
        + from_above[:, None, None] * above_value[None]
    )
    derivative = jnp.moveaxis(
        solved.reshape(depth_rows, components, span_width, stream_width), 0, 1
    )
    highest = lax.Precision.HIGHEST
    count_slots = forces.shape[1]
    devices = lax.axis_size(("wall", "span"))
    capacity = max(2, 2 * count_slots // devices)
    positions = jnp.arange(count_slots, dtype=jnp.int32)
    weighted = jnp.where((positions < counts[0])[None, :], forces, 0.0)
    owners = owner[:, 0]
    device_ids = jnp.arange(devices, dtype=jnp.int32)
    owner_table = (owners[:, None] == device_ids[None, :]).astype(jnp.float32)
    block_len = min(128, count_slots)
    block_count = count_slots // block_len
    owner_blocks = owner_table.reshape(block_count, block_len, devices)
    block_iota = jnp.arange(block_len, dtype=jnp.int32)
    strict_lower = (block_iota[:, None] > block_iota[None, :]).astype(jnp.float32)
    within_block = jnp.einsum("rs,bsd->brd", strict_lower, owner_blocks, precision=highest)
    block_totals = jnp.sum(owner_blocks, axis=1)
    before_block = jnp.cumsum(block_totals, axis=0) - block_totals
    rank_float = jnp.sum((within_block + before_block[:, None, :]) * owner_blocks, axis=2).reshape(
        count_slots
    )
    rank_table = (rank_float[:, None] == jnp.arange(capacity, dtype=jnp.float32)[None, :]).astype(
        jnp.float32
    )
    payload = jnp.concatenate([weighted, cells.astype(jnp.float32)[None, :]], axis=0)
    owner_payload = payload[:, :, None] * owner_table[None]
    outgoing = jnp.einsum("cpd,pr->cdr", owner_payload, rank_table, precision=highest)
    incoming_slots = lax.all_to_all(
        outgoing, ("wall", "span"), split_axis=1, concat_axis=1, tiled=True
    ).reshape(4, -1)
    target = incoming_slots[3].astype(jnp.int32)
    plane_cells = depth_rows * span_width
    arrived = target.shape[0]
    arrive_block = min(1024, arrived)
    arrive_count = arrived // arrive_block
    plane_ids = jnp.arange(plane_cells, dtype=jnp.int32)
    stream_ids = jnp.arange(stream_width, dtype=jnp.int32)
    plane_index = (target // stream_width).reshape(arrive_count, arrive_block)
    stream_index = (target % stream_width).reshape(arrive_count, arrive_block)
    force_blocks = jnp.moveaxis(incoming_slots[:3].reshape(3, arrive_count, arrive_block), 1, 0)

    def deposit_block(total, block_entry):
        plane_now, stream_now, force_now = block_entry
        plane_table = (plane_now[:, None] == plane_ids[None, :]).astype(jnp.float32)
        stream_table = (stream_now[:, None] == stream_ids[None, :]).astype(jnp.float32)
        left_side = force_now[:, :, None] * plane_table[None]
        return (total + jnp.einsum("cka,kb->cab", left_side, stream_table, precision=highest), None)

    summed, _unused3 = lax.scan(
        deposit_block,
        jnp.zeros((3, plane_cells, stream_width), jnp.float32),
        (plane_index, stream_index, force_blocks),
    )
    forcing = -inv_volume[None, :, None, None] * summed.reshape(
        3, depth_rows, span_width, stream_width
    )
    return (derivative, forcing)


def solution(mesh):
    in_specs = (
        P(None, "wall", "span", None),
        P(),
        P(),
        P(None, "wall"),
        P("wall"),
        P(None, ("wall", "span")),
        P(("wall", "span"), None),
        P(("wall", "span")),
        P(("wall", "span")),
    )
    out_specs = (P(None, "wall", "span", None), P(None, "wall", "span", None))
    return jax.shard_map(body, mesh=mesh, in_specs=in_specs, out_specs=out_specs, check_vma=False)
```

profile of v0, /device:TPU:0, one launch (start us, length us, event | category | flops | bytes accessed | tf_op | source)
XLA Modules:
  0.0 1173.9 jit_solution(8277702913154819397)
XLA Ops:
  8.4 3.9 collective-permute-start
  18.3 3.6 while.244
  32.4 86.4 %while.236 = (s32[]{:T(128)}, f32[]{:T(128)}, f32[32]{0:T(128)S(1)}, f32[32]{0:T(128)S(1)}, f32[32]{0:T(128)S(1)}, /*index=5*/f32[32]{0:T(128)S(1)}, s32[]{:T(128)}, f32[]{:T(128)}) while((s32[]{:T(128)}, f32[]{:T(128)}, f32[32]{0:T(128)S(1)}, f32[32]{0:T(128)S(1)}, f32[32]{0:T(128)S(1)}, /*index=5*/f32[32]{0:T(128)S(1)}, s32[]{:T(128)}, ...), condition=%wide.region_1.0_spmd, body=%wide.region_0.0_spmd.sunk | while | flops 5 | bytes 169 | solution.py:50
  119.5 123.0 %while.237 = (s32[]{:T(128)}, f32[]{:T(128)}, f32[32]{0:T(128)S(1)}, f32[32]{0:T(128)S(1)}, f32[32]{0:T(128)S(1)}, /*index=5*/f32[32]{0:T(128)S(1)}, s32[]{:T(128)}) while((s32[]{:T(128)}, f32[]{:T(128)}, f32[32]{0:T(128)S(1)}, f32[32]{0:T(128)S(1)}, f32[32]{0:T(128)S(1)}, /*index=5*/f32[32]{0:T(128)S(1)}, s32[]{:T(128)}) %tuple.494), condition=%wide.region_7.8_spmd, body=%wide.region_6.7_spmd.sunk | while | flops 5 | bytes 161 | solution.py:61
  242.4 89.2 %while.238 = (s32[]{:T(128)}, f32[]{:T(128)}, f32[32]{0:T(128)S(1)}, f32[32]{0:T(128)S(1)}, f32[32]{0:T(128)S(1)}, /*index=5*/s32[]{:T(128)}, s32[]{:T(128)}) while((s32[]{:T(128)}, f32[]{:T(128)}, f32[32]{0:T(128)S(1)}, f32[32]{0:T(128)S(1)}, f32[32]{0:T(128)S(1)}, /*index=5*/s32[]{:T(128)}, s32[]{:T(128)}) %tuple.464), condition=%wide.region_9.10_spmd, body=%wide.region_8.9_spmd.sunk | while | flops 5 | bytes 149 | solution.py:70
  333.0 127.1 %while.240 = (s32[]{:T(128)}, f32[]{:T(128)}, f32[32]{0:T(128)S(1)}, f32[32]{0:T(128)S(1)}, f32[32]{0:T(128)S(1)}, /*index=5*/f32[32]{0:T(128)S(1)}, s32[]{:T(128)}) while((s32[]{:T(128)}, f32[]{:T(128)}, f32[32]{0:T(128)S(1)}, f32[32]{0:T(128)S(1)}, f32[32]{0:T(128)S(1)}, /*index=5*/f32[32]{0:T(128)S(1)}, s32[]{:T(128)}) %tuple.499), condition=%wide.region_24.25_spmd, body=%wide.region_23.24_spmd.sunk | while | flops 5 | bytes 161 | solution.py:61
  460.1 82.9 %while.241 = (s32[]{:T(128)}, f32[]{:T(128)}, f32[32]{0:T(128)S(1)}, f32[32]{0:T(128)S(1)}, f32[32]{0:T(128)S(1)}, /*index=5*/s32[]{:T(128)}, s32[]{:T(128)}) while((s32[]{:T(128)}, f32[]{:T(128)}, f32[32]{0:T(128)S(1)}, f32[32]{0:T(128)S(1)}, f32[32]{0:T(128)S(1)}, /*index=5*/s32[]{:T(128)}, s32[]{:T(128)}) %tuple.501), condition=%wide.region_26.27_spmd, body=%wide.region_25.26_spmd.sunk | while | flops 5 | bytes 149 | solution.py:70
  547.2 89.7 %while.239 = (s32[]{:T(128)}, f32[]{:T(128)}, f32[32]{0:T(128)S(1)}, f32[32]{0:T(128)S(1)}, f32[32]{0:T(128)S(1)}, /*index=5*/f32[32]{0:T(128)S(1)}, s32[]{:T(128)}, f32[]{:T(128)}) while((s32[]{:T(128)}, f32[]{:T(128)}, f32[32]{0:T(128)S(1)}, f32[32]{0:T(128)S(1)}, f32[32]{0:T(128)S(1)}, /*index=5*/f32[32]{0:T(128)S(1)}, s32[]{:T(128)}, ...), condition=%wide.region_22.23_spmd, body=%wide.region_21.22_spmd.sunk | while | flops 5 | bytes 169 | solution.py:50
  639.2 7.3 constant_dynamic-update-slice_fusion
  646.6 7.3 fusion.40
  657.1 3.5 broadcast.235.clone
  660.6 135.3 %while.242 = (s32[]{:T(128)}, f32[48,1024]{1,0:T(8,128)S(1)}, f32[32,48,1024]{2,1,0:T(8,128)}, f32[32,48,1024]{2,1,0:T(8,128)}, f32[32]{0:T(128)S(1)}, /*index=5*/f32[32]{0:T(128)S(1)}, s32[]{:T(128)}, s32[]{:T(128)}) while((s32[]{:T(128)}, f32[48,1024]{1,0:T(8,128)S(1)}, f32[32,48,1024]{2,1,0:T(8,128)}, ...), condition=%wide.region_3.4_spmd.clone, body=%wide.region_2.3_spmd.clone.sunk | while | flops 196611 | bytes 788087 | solution.py:61
  799.5 95.3 %while.243 = (s32[]{:T(128)}, f32[48,1024]{1,0:T(8,128)S(1)}, f32[32,48,1024]{2,1,0:T(8,128)}, f32[32,48,1024]{2,1,0:T(8,128)}, f32[32]{0:T(128)S(1)}, /*index=5*/s32[]{:T(128)}, s32[]{:T(128)}, s32[]{:T(128)}) while((s32[]{:T(128)}, f32[48,1024]{1,0:T(8,128)S(1)}, f32[32,48,1024]{2,1,0:T(8,128)}, f32[32,48,1024]{2,1,0:T(8,128)}, ...), condition=%wide.region_5.6_spmd.clone, body=%wide.region_4.5_spmd.clone.sunk | while | flops 147460 | bytes 787067 | solution.py:70
  894.7 3.6 subtract_divide_fusion
  901.0 4.0 fusion.37
  906.0 11.9 %all-to-all-start = ((f32[128,1,256]{2,1,0:T(1,128)}), f32[128,1,256]{2,1,0:T(1,128)S(1)}, u32[]{:S(2)}, u32[]{:S(2)}) async-start(f32[128,1,256]{2,1,0:T(1,128)} %reshape.339), calls=%async_computation | async-start | bytes 262144 | tf_op jit(solution)/shard_map/all_to_all | solution.py:197
  924.1 40.4 %all-reduce.7 = (f32[16]{0:T(128)S(1)}, f32[16]{0:T(128)S(1)}) all-reduce(f32[16]{0:T(128)S(1)} %dynamic-update-slice.21, f32[16]{0:T(128)S(1)} %dynamic-update-slice.20), channel_id=1, replica_groups=mesh['wall'=16,'span'=8] {'wall'}, use_global_device_ids=true, to_apply=%add.6 | all-reduce | flops 32 | bytes 256
  966.8 34.8 %while.249 = (s32[]{:T(128)}, f32[48,1024]{1,0:T(8,128)S(1)}, s32[]{:T(128)}, f32[16,1,1]{0,2,1:T(1,128)S(1)}, f32[16,48,1024]{2,1,0:T(8,128)}, /*index=5*/s32[]{:T(128)}, s32[]{:T(128)}) while((s32[]{:T(128)}, f32[48,1024]{1,0:T(8,128)S(1)}, s32[]{:T(128)}, f32[16,1,1]{0,2,1:T(1,128)S(1)}, f32[16,48,1024]{2,1,0:T(8,128)}, ...), condition=%wide.region_28.29_spmd.clone, body=%wide.region_27.28_spmd.clone.sunk | while | flops 196612 | bytes 589941 | solution.py:38
  1001.6 4.8 multiply_subtract_fusion.1
  1006.4 117.5 %while.251 = (s32[]{:T(128)}, f32[3,512,1024]{2,1,0:T(8,128)}, f32[8,3,1024]{2,0,1:T(8,128)S(1)}, s32[8,1024]{1,0:T(8,128)S(1)}, s32[8,1024]{1,0:T(8,128)S(1)}, /*index=5*/s32[]{:T(128)}, s32[]{:T(128)}) while((s32[]{:T(128)}, f32[3,512,1024]{2,1,0:T(8,128)}, f32[8,3,1024]{2,0,1:T(8,128)S(1)}, s32[8,1024]{1,0:T(8,128)S(1)}, ...), condition=%wide.region_35.36_spmd.clone, body=%wide.region_34.35_spmd.clone.sunk | while | flops 19334168576 | bytes 16863328 | solution.py:218
  1006.8 13.0 %select_add_fusion.2 = f32[3,512,1024]{2,1,0:T(8,128)} fusion(f32[3,512,1024]{2,1,0:T(8,128)} %get-tuple-element.2495, pred[]{:T(512)S(6)} %compare.93, s32[1024]{0:T(1024)S(1)} %bitcast.318, f32[1024,512]{0,1:T(8,128)S(1)} %fusion.90, f32[3,1024]{1,0:T(4,128)S(1)} %bitcast.316), kind=kOutput, calls=%fused_computation.45.clone.1 | convolution fusion | flops 19333120000 | bytes 14696449 | tf_op jit(solution)/shard_map/while/body/eval_jaxpr/cka,kb->cab/dot_general | solution.py:216
  1020.1 14.6 %select_add_fusion.2 = f32[3,512,1024]{2,1,0:T(8,128)} fusion(f32[3,512,1024]{2,1,0:T(8,128)} %get-tuple-element.2495, pred[]{:T(512)S(6)} %compare.93, s32[1024]{0:T(1024)S(1)} %bitcast.318, f32[1024,512]{0,1:T(8,128)S(1)} %fusion.90, f32[3,1024]{1,0:T(4,128)S(1)} %bitcast.316), kind=kOutput, calls=%fused_computation.45.clone.1 | convolution fusion | flops 19333120000 | bytes 14696449 | tf_op jit(solution)/shard_map/while/body/eval_jaxpr/cka,kb->cab/dot_general | solution.py:216
  1035.0 14.6 %select_add_fusion.2 = f32[3,512,1024]{2,1,0:T(8,128)} fusion(f32[3,512,1024]{2,1,0:T(8,128)} %get-tuple-element.2495, pred[]{:T(512)S(6)} %compare.93, s32[1024]{0:T(1024)S(1)} %bitcast.318, f32[1024,512]{0,1:T(8,128)S(1)} %fusion.90, f32[3,1024]{1,0:T(4,128)S(1)} %bitcast.316), kind=kOutput, calls=%fused_computation.45.clone.1 | convolution fusion | flops 19333120000 | bytes 14696449 | tf_op jit(solution)/shard_map/while/body/eval_jaxpr/cka,kb->cab/dot_general | solution.py:216
  1049.9 14.6 %select_add_fusion.2 = f32[3,512,1024]{2,1,0:T(8,128)} fusion(f32[3,512,1024]{2,1,0:T(8,128)} %get-tuple-element.2495, pred[]{:T(512)S(6)} %compare.93, s32[1024]{0:T(1024)S(1)} %bitcast.318, f32[1024,512]{0,1:T(8,128)S(1)} %fusion.90, f32[3,1024]{1,0:T(4,128)S(1)} %bitcast.316), kind=kOutput, calls=%fused_computation.45.clone.1 | convolution fusion | flops 19333120000 | bytes 14696449 | tf_op jit(solution)/shard_map/while/body/eval_jaxpr/cka,kb->cab/dot_general | solution.py:216
  1064.7 14.6 %select_add_fusion.2 = f32[3,512,1024]{2,1,0:T(8,128)} fusion(f32[3,512,1024]{2,1,0:T(8,128)} %get-tuple-element.2495, pred[]{:T(512)S(6)} %compare.93, s32[1024]{0:T(1024)S(1)} %bitcast.318, f32[1024,512]{0,1:T(8,128)S(1)} %fusion.90, f32[3,1024]{1,0:T(4,128)S(1)} %bitcast.316), kind=kOutput, calls=%fused_computation.45.clone.1 | convolution fusion | flops 19333120000 | bytes 14696449 | tf_op jit(solution)/shard_map/while/body/eval_jaxpr/cka,kb->cab/dot_general | solution.py:216
  1079.6 14.6 %select_add_fusion.2 = f32[3,512,1024]{2,1,0:T(8,128)} fusion(f32[3,512,1024]{2,1,0:T(8,128)} %get-tuple-element.2495, pred[]{:T(512)S(6)} %compare.93, s32[1024]{0:T(1024)S(1)} %bitcast.318, f32[1024,512]{0,1:T(8,128)S(1)} %fusion.90, f32[3,1024]{1,0:T(4,128)S(1)} %bitcast.316), kind=kOutput, calls=%fused_computation.45.clone.1 | convolution fusion | flops 19333120000 | bytes 14696449 | tf_op jit(solution)/shard_map/while/body/eval_jaxpr/cka,kb->cab/dot_general | solution.py:216
  1094.5 14.6 %select_add_fusion.2 = f32[3,512,1024]{2,1,0:T(8,128)} fusion(f32[3,512,1024]{2,1,0:T(8,128)} %get-tuple-element.2495, pred[]{:T(512)S(6)} %compare.93, s32[1024]{0:T(1024)S(1)} %bitcast.318, f32[1024,512]{0,1:T(8,128)S(1)} %fusion.90, f32[3,1024]{1,0:T(4,128)S(1)} %bitcast.316), kind=kOutput, calls=%fused_computation.45.clone.1 | convolution fusion | flops 19333120000 | bytes 14696449 | tf_op jit(solution)/shard_map/while/body/eval_jaxpr/cka,kb->cab/dot_general | solution.py:216
  1109.4 14.6 %select_add_fusion.2 = f32[3,512,1024]{2,1,0:T(8,128)} fusion(f32[3,512,1024]{2,1,0:T(8,128)} %get-tuple-element.2495, pred[]{:T(512)S(6)} %compare.93, s32[1024]{0:T(1024)S(1)} %bitcast.318, f32[1024,512]{0,1:T(8,128)S(1)} %fusion.90, f32[3,1024]{1,0:T(4,128)S(1)} %bitcast.316), kind=kOutput, calls=%fused_computation.45.clone.1 | convolution fusion | flops 19333120000 | bytes 14696449 | tf_op jit(solution)/shard_map/while/body/eval_jaxpr/cka,kb->cab/dot_general | solution.py:216
  1123.9 6.9 broadcast_multiply_fusion
  1132.9 21.2 %while.250 = (s32[]{:T(128)}, f32[48,1024]{1,0:T(8,128)S(1)}, s32[]{:T(128)}, f32[16,1,1]{0,2,1:T(1,128)S(1)}, f32[16,48,1024]{2,1,0:T(8,128)S(1)}, /*index=5*/s32[]{:T(128)}, s32[]{:T(128)}) while((s32[]{:T(128)}, f32[48,1024]{1,0:T(8,128)S(1)}, s32[]{:T(128)}, f32[16,1,1]{0,2,1:T(1,128)S(1)}, f32[16,48,1024]{2,1,0:T(8,128)S(1)}, ...), condition=%wide.region_30.31_spmd.clone, body=%wide.region_29.30_spmd.clone.sunk | while | flops 196612 | bytes 589941 | solution.py:38
  1154.2 5.6 multiply_subtract_fusion
  1159.7 3.9 multiply_add_fusion
  (1432 shorter events, 645.1 us)
Async XLA Ops:
  7.2 959.6 %all-gather.4.cloned.1.call-start = ((), (), s32[]{:S(2)}) async-start(), calls=%async_computation.1 | async-start | bytes 3342336 | tf_op jit(solution)/shard_map/all_gather | solution.py:26
  8.4 630.0 %collective-permute-start = (f32[3,2,16,1024]{3,2,1,0:T(8,128)S(1)}, f32[3,2,16,1024]{3,2,1,0:T(8,128)S(1)}, u32[]{:S(2)}, u32[]{:S(2)}) collective-permute-start(f32[3,2,16,1024]{3,2,1,0:T(8,128)S(1)} %get-tuple-element.1554), channel_id=1, source_target_pairs={{0,8},{8,16},{16,24},{24,32},{32,40},{40,48},{48,56},{56,64},{64,7... | collective-permute-start | bytes 1179656 | tf_op jit(solution)/shard_map/ppermute | solution.py:15
  12.3 634.2 %collective-permute-start.1 = (f32[3,2,16,1024]{3,2,1,0:T(8,128)S(1)}, f32[3,2,16,1024]{3,2,1,0:T(8,128)S(1)}, u32[]{:S(2)}, u32[]{:S(2)}) collective-permute-start(f32[3,2,16,1024]{3,2,1,0:T(8,128)S(1)} %get-tuple-element.1555), channel_id=1, source_target_pairs={{8,0},{16,8},{24,16},{32,24},{40,32},{48,40},{56,48},{64,56},{72,6... | collective-permute-start | bytes 1179656 | tf_op jit(solution)/shard_map/ppermute | solution.py:17
  638.4 8.1 slice-start
  639.2 7.4 slice-start.1
  657.1 3.5 copy-start.1
  660.6 138.8 %copy-start = (f32[48,1024]{1,0:T(8,128)S(1)}, f32[48,1024]{1,0:T(8,128)}, u32[]{:S(2)}) copy-start(f32[48,1024]{1,0:T(8,128)} %custom-call.1) | copy-start | bytes 589828
  795.9 102.4 %copy-start.2 = (s32[4096,1]{0,1:T(1,128)S(1)}, s32[4096,1]{0,1:T(1,128)}, u32[]{:S(2)}) copy-start(s32[4096,1]{0,1:T(1,128)} %param.63) | copy-start | bytes 49156
  795.9 103.5 %copy-start.4 = (s32[4096]{0:T(1024)S(1)}, s32[4096]{0:T(1024)}, u32[]{:S(2)}) copy-start(s32[4096]{0:T(1024)} %param.64) | copy-start | bytes 49156
  796.0 104.4 %copy-start.3 = (f32[3,4096]{1,0:T(4,128)S(1)}, f32[3,4096]{1,0:T(4,128)}, u32[]{:S(2)}) copy-start(f32[3,4096]{1,0:T(4,128)} %param.62) | copy-start | bytes 147460
  894.7 25.8 %copy-start.6 = (u32[128]{0:T(128)S(1)}, u32[128]{0:T(128)}, u32[]{:S(2)}) copy-start(u32[128]{0:T(128)} %constant.547) | copy-start | bytes 1540
  894.7 69.9 %copy-start.5 = (f32[32]{0:T(128)S(1)}, f32[32]{0:T(128)}, u32[]{:S(2)}) copy-start(f32[32]{0:T(128)} %param.61) | copy-start | bytes 388
  906.0 58.5 %all-to-all-start = ((f32[128,1,256]{2,1,0:T(1,128)}), f32[128,1,256]{2,1,0:T(1,128)S(1)}, u32[]{:S(2)}, u32[]{:S(2)}) async-start(f32[128,1,256]{2,1,0:T(1,128)} %reshape.339), calls=%async_computation | async-start | bytes 262144 | tf_op jit(solution)/shard_map/all_to_all | solution.py:197
  918.0 212.8 %all-gather.6.cloned.1.call-start = ((), (), s32[]{:S(2)}) async-start(), calls=%async_computation.2 | async-start | bytes 3342336 | tf_op jit(solution)/shard_map/all_gather | solution.py:26
Sparse Core Ops, SparseCore 0:
  898.5 51.7 all-gather.3
  1006.6 44.3 all-gather.5
where the time goes:
time: 1180 us; the launch traced here: 1170 us
  local copies, waits for them, and re-layouts  429 us (36%)
  loops' own time  298 us (25%)
  other arithmetic  247 us (21%)
  matrix products  120 us (10%)
  blocking collectives  40.4 us (3%)
  between operations  22.6 us (2%)
  starting transfers between devices  17.2 us (1%)
    dynamic_slice x544, local copies, waits for them, and re-layouts, pivot_rows(): lax.scan(advance, initial, (sub_diag, super_diag))  336 us
    dynamic_update_slice x64, other arithmetic, sweep_solve(): lax.scan(forward, jnp.zeros_like(right_side[0]), (sub_diag, pivots, right...  170 us
    another operation x5, loops' own time, sweep_solve(): lax.scan(forward, jnp.zeros_like(right_side[0]), (sub_diag, pivots, right...  126 us
    dot_general x8, matrix products, deposit_block(): jnp.einsum('cka,kb->cab', left_side, stream_table, precision=highest)  115 us
    another operation x5, loops' own time, sweep_solve(): lax.scan(backward, jnp.zeros_like(right_side[0]), (ratios, reduced), reve...  86.8 us
    another operation x3, loops' own time, pivot_rows(): lax.scan(advance, initial, (sub_diag, super_diag))  84.3 us
    unnamed x1, blocking collectives  40.4 us
    select_n x30, other arithmetic, lap(): jnp.where(position < mine, new, old)  35.9 us
  transfers between devices with their start and end apart: 5, of which 0 were waited for; matrix products, arithmetic and copies ran while one was open for 40% of the time, Pallas kernels for 0%

commit v1 on v0

v1 whole, which is shorter than its diff:
```python
import functools

import jax
import jax.numpy as jnp
from jax import lax
from jax.experimental import pallas as pl
from jax.experimental.pallas import tpu as pltpu
from jax.sharding import PartitionSpec as P

F32 = jnp.float32
MESH = pl.DeviceIdType.MESH
NW, NS = 16, 8
RY, SZ, NX = 32, 16, 1024
SLOTS = 64


def exchange_kernel(
    vel, lu, st, forces, owner, cells, counts,
    halo, bound, coef, part_t, rows_out,
    vbuf, send_a, recv_a, send_f, elim, pbuf, tile_out, tile_in,
    pack, recv1, pack2, recv2,
    dmat, cmat, ymat, zmat, wmat, wgt, red,
    vsem, hs, hr, ts, tr, as_, ar, fs, fr, p1s, p1r, p2s, p2r,
):
    me_w = lax.axis_index("wall")
    me_s = lax.axis_index("span")

    def vcopy(c, h):
        part = (c, slice(None), pl.ds(h * 8, 8), slice(None))
        return pltpu.make_async_copy(vel.at[part], vbuf.at[part], vsem.at[c * 2 + h])

    for c in range(3):
        for h in range(2):
            vcopy(c, h).start()

    barrier = pltpu.get_barrier_semaphore()

    @pl.loop(1, NW)
    def _(k):
        pl.semaphore_signal(
            barrier, inc=1, device_id=(lax.rem(me_w + k, NW), me_s), device_id_type=MESH
        )

    @pl.loop(1, NS)
    def _(k):
        pl.semaphore_signal(
            barrier, inc=1, device_id=(me_w, lax.rem(me_s + k, NS)), device_id_type=MESH
        )

    pl.semaphore_wait(barrier, NW - 1 + NS - 1)

    above = lax.rem(me_w + 1, NW)
    under = lax.rem(me_w + NW - 1, NW)

    def hcopy(way):
        return pltpu.make_async_remote_copy(
            src_ref=vel.at[:, RY - 1] if way == 0 else vel.at[:, 0],
            dst_ref=halo.at[way],
            send_sem=hs.at[way],
            recv_sem=hr.at[way],
            device_id=(above if way == 0 else under, me_s),
            device_id_type=MESH,
        )

    hcopy(0).start()
    hcopy(1).start()

    eye = lax.broadcasted_iota(jnp.int32, (RY, RY), 0) == lax.broadcasted_iota(
        jnp.int32, (RY, RY), 1
    )

    def column(row, mask, n):
        full = jnp.broadcast_to(row, (n, n))
        col = jnp.sum(jnp.where(mask, full, 0.0), axis=1, keepdims=True)
        return jnp.broadcast_to(col, (n, 128))

    stc = [column(st[m : m + 1, :], eye, RY) for m in range(5)]
    tile_out[0:1, :] = stc[0][0:1]
    tile_out[1:2, :] = stc[1][0:1]
    tile_out[2:3, :] = stc[4][RY - 1 : RY]
    tile_out[3:4, :] = stc[3][RY - 1 : RY]
    tile_out[4:8, :] = jnp.zeros((4, 128), F32)

    def tcopy(way):
        return pltpu.make_async_remote_copy(
            src_ref=tile_out,
            dst_ref=tile_in.at[way],
            send_sem=ts.at[way],
            recv_sem=tr.at[way],
            device_id=(above if way == 0 else under, me_s),
            device_id_type=MESH,
        )

    tcopy(0).start()
    tcopy(1).start()

    count = counts[0]
    pack[...] = jnp.zeros((2, NW * NS, 128), F32)
    up_i = lax.broadcasted_iota(jnp.int32, (256, 256), 0)
    up_j = lax.broadcasted_iota(jnp.int32, (256, 256), 1)
    before = (up_i < up_j).astype(F32).astype(jnp.bfloat16)
    ones = jnp.ones((256, 256), jnp.bfloat16)
    ids = lax.broadcasted_iota(jnp.int32, (NW * NS, 256), 0)
    ranks = lax.broadcasted_iota(jnp.int32, (SLOTS, 256), 0).astype(F32)
    lanes = lax.broadcasted_iota(jnp.int32, (1, 256), 1)
    nt = (((1,), (1,)), ((), ()))
    nn = (((1,), (0,)), ((), ()))

    def pack_block(i, carry):
        at = pl.ds(pl.multiple_of(i * 256, 256), 256)
        own = owner[:, at]
        key = (own & 7) * NW + (own >> 3)
        key = jnp.where(lanes + i * 256 < count, key, 512)
        hit = ids == key
        hot = jnp.where(hit, 1.0, 0.0)
        hot_b = hot.astype(jnp.bfloat16)
        pre = lax.dot_general(hot_b, before, nn, preferred_element_type=F32)
        tot = lax.dot_general(hot_b, ones, nn, preferred_element_type=F32)
        rank = jnp.sum(jnp.where(hit, pre + carry, 0.0), axis=0, keepdims=True)
        place = ranks == rank
        load = [forces[c : c + 1, at] for c in range(3)] + [cells[:, at].astype(F32)]
        sums = None
        for _part in range(3):
            head = [x.astype(jnp.bfloat16).astype(F32) for x in load]
            load = [x - y for x, y in zip(load, head)]
            right = jnp.concatenate(
                [jnp.where(place, y, 0.0) for y in head], axis=0
            ).astype(jnp.bfloat16)
            term = lax.dot_general(hot_b, right, nt, preferred_element_type=F32)
            sums = term if sums is None else sums + term
        pack[0] += sums[:, 0:128]
        pack[1] += sums[:, 128:256]
        return carry + tot

    lax.fori_loop(
        0, owner.shape[1] // 256, pack_block, jnp.zeros((NW * NS, 256), F32)
    )

    def p1copy(k):
        to = lax.rem(me_s + k, NS)
        return pltpu.make_async_remote_copy(
            src_ref=pack.at[:, pl.ds(pl.multiple_of(to * NW, NW), NW)],
            dst_ref=recv1.at[:, pl.ds(pl.multiple_of(me_s * NW, NW), NW)],
            send_sem=p1s.at[k],
            recv_sem=p1r.at[k],
            device_id=(me_w, to),
            device_id_type=MESH,
        )

    for k in range(1, NS):
        p1copy(k).start()
    mine = pl.ds(pl.multiple_of(me_s * NW, NW), NW)
    recv1[:, mine, :] = pack[:, mine, :]

    zero = jnp.zeros((1, NW), F32)
    carry_c, carry_b = zero, None
    for j in range(RY):
        low, upp = lu[0, j : j + 1, :], lu[1, j : j + 1, :]
        inv = 1.0 / (1.0 - low * carry_c) if j > 0 else jnp.ones((1, NW), F32)
        carry_c = upp * inv
        dmat[j : j + 1, :] = inv
        cmat[j : j + 1, :] = carry_c
    binv = [None] * RY
    for j in range(RY - 1, -1, -1):
        if j == RY - 1:
            binv[j] = jnp.ones((1, NW), F32)
        else:
            binv[j] = 1.0 / (
                1.0 - lu[1, j : j + 1, :] * lu[0, j + 1 : j + 2, :] * binv[j + 1]
            )
    y = binv[0]
    ymat[0:1, :] = y
    for j in range(1, RY):
        y = -(lu[1, j - 1 : j, :] * binv[j]) * y
        ymat[j : j + 1, :] = y
    z = dmat[RY - 1 : RY, :]
    zmat[RY - 1 : RY, :] = z
    for j in range(RY - 2, -1, -1):
        z = -(lu[0, j + 1 : j + 2, :] * dmat[j : j + 1, :]) * z
        zmat[j : j + 1, :] = z

    lane16 = lax.broadcasted_iota(jnp.int32, (RY, NW), 1)

    def at_slab(values, slab):
        n = values.shape[0]
        col = jnp.sum(jnp.where(lane16[0:n] == slab, values, 0.0), axis=1, keepdims=True)
        return jnp.broadcast_to(col, (n, 128))

    low_all, upp_all = lu[0], lu[1]
    inv_own = at_slab(dmat[...], me_w)
    c_own = at_slab(cmat[...], me_w)
    y_own = at_slab(ymat[...], me_w)
    z_own = at_slab(zmat[...], me_w)
    low_own = at_slab(low_all, me_w)
    low_next = at_slab(low_all[0:1], me_w + 1)
    upp_prev = at_slab(upp_all[RY - 1 : RY], me_w - 1)
    has_under = jnp.where(me_w > 0, 1.0, 0.0)
    has_above = jnp.where(me_w < NW - 1, 1.0, 0.0)

    row_i = lax.broadcasted_iota(jnp.int32, (RY, 128), 0)
    kept = [
        jnp.where(row_i == 0, 0.0, jnp.where(row_i == 1, stc[0] * has_under, stc[0])),
        jnp.where(row_i == 0, 0.0, stc[1]),
        stc[2],
        jnp.where(row_i == RY - 1, 0.0, stc[3]),
        jnp.where(
            row_i == RY - 1, 0.0, jnp.where(row_i == RY - 2, stc[4] * has_above, stc[4])
        ),
    ]
    for m in range(5):
        coef[m] = kept[m] * inv_own
    coef[5] = jnp.where(row_i == 0, 0.0, low_own * inv_own)
    coef[6] = c_own
    coef[7] = inv_own

    tcopy(0).wait()
    tcopy(1).wait()
    for way, own, scale in ((0, z_own, low_next), (1, y_own, upp_prev)):
        wmat[...] = jnp.zeros((RY + 8, 128), F32)
        for m in range(5):
            wmat[m + 2 : m + 2 + RY, :] += kept[m] * own
        wgt[way] = wmat[...] * (-scale)
    wgt[0, RY + 2 : RY + 3, :] += tile_in[1, 0:1, :]
    wgt[0, RY + 3 : RY + 4, :] += tile_in[1, 1:2, :]
    wgt[1, 5:6, :] += tile_in[0, 2:3, :]
    wgt[1, 4:5, :] += tile_in[0, 3:4, :]

    eye16 = lax.broadcasted_iota(jnp.int32, (NW, NW), 0) == lax.broadcasted_iota(
        jnp.int32, (NW, NW), 1
    )
    next16 = lax.broadcasted_iota(jnp.int32, (NW, NW), 0) + 1 == lax.broadcasted_iota(
        jnp.int32, (NW, NW), 1
    )
    prev16 = lax.broadcasted_iota(jnp.int32, (NW, NW), 0) - 1 == lax.broadcasted_iota(
        jnp.int32, (NW, NW), 1
    )
    z0 = column(zmat[0:1, :], eye16, NW)
    z1 = column(zmat[RY - 1 : RY, :], eye16, NW)
    y0 = column(ymat[0:1, :], eye16, NW)
    y1 = column(ymat[RY - 1 : RY, :], eye16, NW)
    low_n = column(low_all[0:1], next16, NW)
    upp_p = column(upp_all[RY - 1 : RY], prev16, NW)
    red[0] = upp_p * y0
    red[1] = low_n * z0
    lz1 = low_n * z1
    uy1 = upp_p * y1
    q = -lz1[0:1]
    for s in range(1, NW):
        dinv = 1.0 / (1.0 + red[0, s : s + 1, :] * q)
        c3 = uy1[s : s + 1] * dinv
        red[2, s : s + 1, :] = q * dinv
        red[3, s : s + 1, :] = dinv
        red[4, s : s + 1, :] = c3
        red[5, s : s + 1, :] = q
        q = red[1, s : s + 1, :] * q * c3 - lz1[s : s + 1]

    for c in range(3):
        for h in range(2):
            vcopy(c, h).wait()

            @pl.loop(0, 2)
            def _(x):
                cols = pl.ds(pl.multiple_of(x * 512, 512), 512)
                up = jnp.zeros((8, 512), F32)
                down = jnp.zeros((8, 512), F32)
                for j in range(RY):
                    u = vbuf[c, j, h * 8 : h * 8 + 8, cols]
                    up = up + wgt[0, j + 4 : j + 5, 0:1] * u
                    down = down + wgt[1, j + 4 : j + 5, 0:1] * u
                for b in range(4):
                    send_a[h * 8 + x * 4 + b, 0, c] = up[:, b * 128 : b * 128 + 128]
                    send_a[h * 8 + x * 4 + b, 1, c] = down[:, b * 128 : b * 128 + 128]

    for k in range(1, NS):
        p1copy(k).wait()
    for w in range(NW):
        for b in range(2):
            pack2[w, b] = recv1[b, pl.ds(w, NS, stride=NW), :]

    def p2copy(k):
        to = lax.rem(me_w + k, NW)
        return pltpu.make_async_remote_copy(
            src_ref=pack2.at[to],
            dst_ref=recv2.at[me_w],
            send_sem=p2s.at[k],
            recv_sem=p2r.at[k],
            device_id=(to, me_s),
            device_id_type=MESH,
        )

    for k in range(1, NW):
        p2copy(k).start()
    recv2[me_w] = pack2[me_w]

    hcopy(0).wait()
    hcopy(1).wait()
    for h in range(2):

        @pl.loop(0, 8)
        def _(x):
            cols = pl.ds(pl.multiple_of(x * 128, 128), 128)
            for c in range(3):
                lo = halo[0, c, h * 8 : h * 8 + 8, cols]
                hi = halo[1, c, h * 8 : h * 8 + 8, cols]
                for way in range(2):
                    send_a[h * 8 + x, way, c] += (
                        wgt[way, 3:4, 0:1] * lo + wgt[way, RY + 4 : RY + 5, 0:1] * hi
                    )

    def acopy(k):
        to = lax.rem(me_w + k, NW)
        return pltpu.make_async_remote_copy(
            src_ref=send_a.at[to],
            dst_ref=recv_a.at[me_w],
            send_sem=as_.at[k],
            recv_sem=ar.at[k],
            device_id=(to, me_s),
            device_id_type=MESH,
        )

    for k in range(1, NW):
        acopy(k).start()
    recv_a[me_w] = send_a[me_w]
    for k in range(1, NW):
        acopy(k).wait()

    p = recv_a[0, 0]
    for s in range(1, NW):
        pbuf[s] = p
        e = recv_a[s, 1] - red[0, s : s + 1, :] * p
        elim[s] = e
        if s < NW - 1:
            p = recv_a[s, 0] - red[1, s : s + 1, :] * (p + red[2, s : s + 1, :] * e)
    down = jnp.zeros((3, 8, 128), F32)
    send_f[NW - 1, 1] = down
    for s in range(NW - 1, 0, -1):
        down = red[3, s : s + 1, :] * elim[s] - red[4, s : s + 1, :] * down
        send_f[s - 1, 1] = down
        send_f[s, 0] = pbuf[s] + red[5, s : s + 1, :] * down
    send_f[0, 0] = jnp.zeros((3, 8, 128), F32)

    def fcopy(k):
        to = lax.rem(me_w + k, NW)
        return pltpu.make_async_remote_copy(
            src_ref=send_f.at[to],
            dst_ref=bound.at[me_w],
            send_sem=fs.at[k],
            recv_sem=fr.at[k],
            device_id=(to, me_s),
            device_id_type=MESH,
        )

    for k in range(1, NW):
        fcopy(k).start()
    bound[me_w] = send_f[me_w]

    for k in range(1, NW):
        p2copy(k).wait()
    part_t[0:128, :] = recv2[:, 0].reshape(NW * NS, 128).T
    rest = recv2[:, 1].reshape(NW * NS, 128)
    flipped = rest.T
    part_t[128:192, :] = flipped[0:64]
    part_t[192:256, :] = (flipped[64:128].astype(jnp.int32) & 127).astype(F32)
    rows_out[...] = (rest[:, 64:128].astype(jnp.int32) >> 7) * 4

    for k in range(1, NW):
        fcopy(k).wait()


def exchange(vel, lu, st, forces, owner, cells, counts):
    vm = pl.BlockSpec(memory_space=pltpu.VMEM)
    dma = pltpu.SemaphoreType.DMA
    return pl.pallas_call(
        exchange_kernel,
        out_shape=(
            jax.ShapeDtypeStruct((2, 3, SZ, NX), F32),
            jax.ShapeDtypeStruct((NW, 2, 3, 8, 128), F32),
            jax.ShapeDtypeStruct((8, RY, 128), F32),
            jax.ShapeDtypeStruct((256, 128), F32),
            jax.ShapeDtypeStruct((128, SLOTS), jnp.int32),
        ),
        in_specs=[pl.BlockSpec(memory_space=pl.ANY)] + [vm] * 5
        + [pl.BlockSpec(memory_space=pltpu.SMEM)],
        out_specs=[vm] * 5,
        scratch_shapes=[
            pltpu.VMEM((3, RY, SZ, NX), F32),
            pltpu.VMEM((NW, 2, 3, 8, 128), F32),
            pltpu.VMEM((NW, 2, 3, 8, 128), F32),
            pltpu.VMEM((NW, 2, 3, 8, 128), F32),
            pltpu.VMEM((NW, 3, 8, 128), F32),
            pltpu.VMEM((NW, 3, 8, 128), F32),
            pltpu.VMEM((8, 128), F32),
            pltpu.VMEM((2, 8, 128), F32),
            pltpu.VMEM((2, NW * NS, 128), F32),
            pltpu.VMEM((2, NW * NS, 128), F32),
            pltpu.VMEM((NW, 2, NS, 128), F32),
            pltpu.VMEM((NW, 2, NS, 128), F32),
            pltpu.VMEM((RY, NW), F32),
            pltpu.VMEM((RY, NW), F32),
            pltpu.VMEM((RY, NW), F32),
            pltpu.VMEM((RY, NW), F32),
            pltpu.VMEM((RY + 8, 128), F32),
            pltpu.VMEM((2, RY + 8, 128), F32),
            pltpu.VMEM((6, NW, 128), F32),
            dma((6,)), dma((2,)), dma((2,)), dma((2,)), dma((2,)),
            dma((NW,)), dma((NW,)), dma((NW,)), dma((NW,)),
            dma((NS,)), dma((NS,)), dma((NW,)), dma((NW,)),
        ],
        compiler_params=pltpu.CompilerParams(
            collective_id=0, has_side_effects=True, vmem_limit_bytes=56 << 20
        ),
        name="exchange",
    )(vel, lu, st, forces, owner, cells, counts)


def deposit_kernel(part_t, rows, inv_vol, out, acc0, acc1, acc2, acc3, even, odd, stage, sem):
    accs = (acc0, acc1, acc2, acc3)
    zeros = jnp.zeros((128, 128), F32)

    @pl.loop(0, 128)
    def _(i):
        at = pl.ds(pl.multiple_of(i * 128, 128), 128)
        for acc in accs:
            acc[at, :] = zeros

    lane = lax.broadcasted_iota(jnp.int32, (8, 128), 1).astype(F32)

    def spread(source, to):
        pick = jnp.full((8, 128), source, jnp.int32)
        for g in range(SLOTS // 8):
            xl = jnp.take_along_axis(part_t[192 + g * 8 : 200 + g * 8, :], pick, axis=1)
            hit = xl == lane
            for c in range(3):
                r0 = c * SLOTS + g * 8
                f = jnp.take_along_axis(part_t[r0 : r0 + 8, :], pick, axis=1)
                to[r0 : r0 + 8, :] = jnp.where(hit, f, 0.0)

    def add(source, frm):
        for r in range(SLOTS):
            at = pl.ds(pl.multiple_of(rows[source, r], 4), 4)
            accs[r % 4][at, :] += frm[pl.ds(r, 4, stride=SLOTS), :]

    spread(0, even)

    @pl.loop(0, 64)
    def _(i):
        spread(2 * i + 1, odd)
        add(2 * i, even)
        spread(jnp.minimum(2 * i + 2, 127), even)
        add(2 * i + 1, odd)

    def put(b):
        part = (slice(None), pl.ds(b * 4, 4))
        return pltpu.make_async_copy(stage.at[part], out.at[part], sem.at[b])

    @pl.loop(0, 8)
    def _(b):
        @pl.loop(0, 4)
        def _(jj):
            j = b * 4 + jj
            scale = -inv_vol[j]
            for h in range(2):
                for x in range(8):
                    for c in range(3):
                        at = pl.ds(((j * SZ + h * 8) * 8 + x) * 4 + c, 8, stride=32)
                        t = (acc0[at, :] + acc1[at, :]) + (acc2[at, :] + acc3[at, :])
                        stage[c, j, h * 8 : h * 8 + 8, x * 128 : x * 128 + 128] = scale * t

        put(b).start()

    @pl.loop(0, 8)
    def _(b):
        put(b).wait()


def deposit(part_t, rows, inv_vol):
    sm = pl.BlockSpec(memory_space=pltpu.SMEM)
    cells = RY * SZ * NX // 128 * 4
    return pl.pallas_call(
        deposit_kernel,
        out_shape=jax.ShapeDtypeStruct((3, RY, SZ, NX), F32),
        in_specs=[pl.BlockSpec(memory_space=pltpu.VMEM), sm, sm],
        out_specs=pl.BlockSpec(memory_space=pl.ANY),
        scratch_shapes=[pltpu.VMEM((cells, 128), F32)] * 4
        + [pltpu.VMEM((256, 128), F32)] * 2
        + [pltpu.VMEM((3, RY, SZ, NX), F32), pltpu.SemaphoreType.DMA((8,))],
        compiler_params=pltpu.CompilerParams(vmem_limit_bytes=56 << 20),
        name="deposit",
    )(part_t, rows, inv_vol)


def sweep_kernel(vel, halo, bound, coef, out):
    for b in range(2):
        for h in range(2):
            cells = (slice(h * 8, h * 8 + 8), slice(b * 128, b * 128 + 128))

            def row(j):
                if j == -1:
                    return halo[0, 0, *cells]
                if j == RY:
                    return halo[1, 0, *cells]
                return vel[0, j, *cells]

            prev = None
            for j in range(RY):
                total = None
                for m in range(5):
                    i = j + m - 2
                    if i < -1 or i > RY or (i == -1 and j == 0) or (i == RY and j == RY - 1):
                        continue
                    term = coef[m, j : j + 1, :] * row(i)
                    total = term if total is None else total + term
                if j == 0:
                    total = total + coef[7, 0:1, :] * bound[h, b, 0, 0]
                if j == RY - 1:
                    total = total + coef[7, RY - 1 : RY, :] * bound[h, b, 1, 0]
                if j > 0:
                    total = total - coef[5, j : j + 1, :] * prev
                prev = total
                out[0, j, *cells] = total
            for j in range(RY - 2, -1, -1):
                prev = out[0, j, *cells] - coef[6, j : j + 1, :] * prev
                out[0, j, *cells] = prev


def sweep(vel, halo, bound, coef):
    return pl.pallas_call(
        sweep_kernel,
        grid=(3, 4),
        out_shape=jax.ShapeDtypeStruct((3, RY, SZ, NX), F32),
        in_specs=[
            pl.BlockSpec((1, RY, SZ, 256), lambda c, x: (c, 0, 0, x)),
            pl.BlockSpec((2, 1, SZ, 256), lambda c, x: (0, c, 0, x)),
            pl.BlockSpec((2, 2, 2, 1, 8, 128), lambda c, x: (0, x, 0, c, 0, 0)),
            pl.BlockSpec((8, RY, 128), lambda c, x: (0, 0, 0)),
        ],
        out_specs=pl.BlockSpec((1, RY, SZ, 256), lambda c, x: (c, 0, 0, x)),
        compiler_params=pltpu.CompilerParams(vmem_limit_bytes=56 << 20),
        name="sweep",
    )(vel, halo, bound.reshape(2, 8, 2, 3, 8, 128), coef)


def body(velocity, lower, upper, stencil, inv_volume, forces, owner, cells, counts):
    lu = jnp.stack([lower, upper]).reshape(2, NW, RY).transpose(0, 2, 1)
    halo, bound, coef, part_t, rows = exchange(
        velocity, lu, stencil, forces, owner.reshape(1, -1), cells.reshape(1, -1), counts
    )
    forcing = deposit(part_t, rows, inv_volume)
    derivative = sweep(velocity, halo, bound, coef)
    return derivative, forcing


def solution(mesh):
    in_specs = (
        P(None, "wall", "span", None),
        P(),
        P(),
        P(None, "wall"),
        P("wall"),
        P(None, ("wall", "span")),
        P(("wall", "span"), None),
        P(("wall", "span")),
        P(("wall", "span")),
    )
    out_specs = (P(None, "wall", "span", None), P(None, "wall", "span", None))
    return jax.shard_map(body, mesh=mesh, in_specs=in_specs, out_specs=out_specs, check_vma=False)
```

time: 1180 us -> 90.8 us (0.08)
  local copies, waits for them, and re-layouts: 429 us -> 1.67 us
  loops' own time: 298 us -> 0 us
  other arithmetic: 247 us -> 0.62 us
  matrix products: 120 us -> 0 us
  Pallas kernels: 0 us -> 86.7 us
  blocking collectives: 40.4 us -> 0 us
  between operations: 22.6 us -> 1.29 us
  starting transfers between devices: 17.2 us -> 0 us
    dynamic_slice x602 -> x0, local copies, waits for them, and re-layouts: 358 us -> none  [the longest x544 336 us: pivot_rows(): lax.scan(advance, initial, (sub_diag, super_diag))]
    another operation x16 -> x0, loops' own time: 298 us -> none  [the longest x5 126 us: sweep_solve(): lax.scan(forward, jnp.zeros_like(right_side[0]), (sub_diag, pivots, right...]
    dynamic_update_slice x64 -> x0, other arithmetic: 170 us -> none  [sweep_solve(): lax.scan(forward, jnp.zeros_like(right_side[0]), (sub_diag, pivots, right...]
    dot_general x10 -> x0, matrix products: 120 us -> none  [the longest x8 115 us: deposit_block(): jnp.einsum('cka,kb->cab', left_side, stream_table, precision=highest)]
    pallas_call x0 -> x3, Pallas kernels: none -> 86.7 us  [the longest x1 39.9 us: exchange(): pl.pallas_call(exchange_kernel, out_shape=(jax.ShapeDtypeStruct((2, 3, SZ...]
    unnamed x1 -> x0, blocking collectives: 40.4 us -> none
    select_n x32 -> x0, other arithmetic: 36 us -> none  [the longest x30 35.9 us: lap(): jnp.where(position < mine, new, old)]
    dynamic_update_slice x448 -> x0, local copies, waits for them, and re-layouts: 35.9 us -> none  [pivot_rows(): lax.scan(advance, initial, (sub_diag, super_diag))]
  transfers between devices with their start and end apart: 5 -> 0, of which waited for: 0 -> 0; matrix products, arithmetic and copies ran while one was open for 40% -> 0% of each run, Pallas kernels for 0% -> 0%
where the time goes in v1:
time: 90.8 us; the launch traced here: 90.3 us
  Pallas kernels  86.7 us (95%)
  local copies, waits for them, and re-layouts  1.67 us (2%)
  between operations  1.29 us (1%)
    pallas_call x1, Pallas kernels, exchange(): pl.pallas_call(exchange_kernel, out_shape=(jax.ShapeDtypeStruct((2, 3, SZ...  39.9 us
    pallas_call x1, Pallas kernels, deposit(): pl.pallas_call(deposit_kernel, out_shape=jax.ShapeDtypeStruct((3, RY, SZ,...  35.6 us
    pallas_call x1, Pallas kernels, sweep(): pl.pallas_call(sweep_kernel, grid=(3, 4), out_shape=jax.ShapeDtypeStruct(...  11.2 us

profile of v1, /device:TPU:0, one launch (start us, length us, event | category | flops | bytes accessed | tf_op | source)
XLA Modules:
  0.0 90.3 jit_solution(5001169416427029221)
XLA Ops:
  1.3 0.8 stack.9
  2.0 0.1 copy.11
  2.1 0.8 stack.10
  2.9 0.1 copy.12
  2.9 0.6 maximum_bitcast_fusion.lu
  3.6 39.9 %exchange.1 = (f32[2,3,16,1024]{3,2,1,0:T(8,128)}, f32[16,2,3,8,128]{4,3,2,1,0:T(8,128)}, f32[8,32,128]{2,1,0:T(8,128)}, f32[256,128]{1,0:T(8,128)}, s32[128,64]{1,0:T(8,128)}) custom-call(f32[3,32,16,1024]{3,2,1,0:T(8,128)} %vel.3, f32[2,32,16]{2,1,0:T(8,128)} %maximum_bitcast_fusion.lu, f32[5,32]{1,0:T(8,128)} %st.1, f32[3,4096]{1,0:T(4,128)} %forces.1, ...), custom_call_target="tpu_custom_call" | custom-call | tf_op jit(solution)/shard_map/exchange/pallas_call | solution.py:373
  43.4 11.2 %sweep.1 = f32[3,32,16,1024]{3,2,1,0:T(8,128)} custom-call(f32[3,32,16,1024]{3,2,1,0:T(8,128)} %vel.3, f32[2,3,16,1024]{3,2,1,0:T(8,128)} %get-tuple-element.7.halo, f32[2,8,2,3,8,128]{5,4,3,2,1,0:T(8,128)} %bitcast.5, f32[8,32,128]{2,1,0:T(8,128)} %get-tuple-element.9.coef), custom_call_target="tpu_custom_call" | custom-call | tf_op jit(solution)/shard_map/sweep/pallas_call | solution.py:527
  54.7 35.6 %deposit.1 = f32[3,32,16,1024]{3,2,1,0:T(8,128)} custom-call(f32[256,128]{1,0:T(8,128)} %get-tuple-element.10.part_t, s32[128,64]{1,0:T(8,128)} %get-tuple-element.11.rows, f32[32]{0:T(128)} %inv_vol.1), custom_call_target="tpu_custom_call" | custom-call | tf_op jit(solution)/shard_map/deposit/pallas_call | solution.py:479

commit v2 on v1

v2 whole, which is shorter than its diff:
```python
import functools

import jax
import jax.numpy as jnp
from jax import lax
from jax.experimental import pallas as pl
from jax.experimental.pallas import tpu as pltpu
from jax.sharding import PartitionSpec as P

F32 = jnp.float32
MESH = pl.DeviceIdType.MESH
NW, NS = 16, 8
RY, SZ, NX = 32, 16, 1024
SLOTS = 64


def exchange_kernel(
    vel, lower, upper, st, forces, owner, cells, counts,
    halo, bound, coef, part_t, rows_out,
    vbuf, send_a, recv_a, send_f, elim, pbuf, tile_out, tile_in,
    pack, recv1, pack2, recv2,
    lmat, umat, dmat, cmat, ymat, zmat, wmat, wgt, red,
    vsem, hs, hr, ts, tr, as_, ar, fs, fr, p1s, p1r, p2s, p2r,
):
    me_w = lax.axis_index("wall")
    me_s = lax.axis_index("span")

    def vcopy(c, h):
        part = (c, slice(None), pl.ds(h * 8, 8), slice(None))
        return pltpu.make_async_copy(vel.at[part], vbuf.at[part], vsem.at[c * 2 + h])

    for c in range(3):
        for h in range(2):
            vcopy(c, h).start()

    barrier = pltpu.get_barrier_semaphore()

    @pl.loop(1, NW)
    def _(k):
        pl.semaphore_signal(
            barrier, inc=1, device_id=(lax.rem(me_w + k, NW), me_s), device_id_type=MESH
        )

    @pl.loop(1, NS)
    def _(k):
        pl.semaphore_signal(
            barrier, inc=1, device_id=(me_w, lax.rem(me_s + k, NS)), device_id_type=MESH
        )

    pl.semaphore_wait(barrier, NW - 1 + NS - 1)

    above = lax.rem(me_w + 1, NW)
    under = lax.rem(me_w + NW - 1, NW)

    def hcopy(way):
        return pltpu.make_async_remote_copy(
            src_ref=vel.at[:, RY - 1] if way == 0 else vel.at[:, 0],
            dst_ref=halo.at[way],
            send_sem=hs.at[way],
            recv_sem=hr.at[way],
            device_id=(above if way == 0 else under, me_s),
            device_id_type=MESH,
        )

    hcopy(0).start()
    hcopy(1).start()

    eye = lax.broadcasted_iota(jnp.int32, (RY, RY), 0) == lax.broadcasted_iota(
        jnp.int32, (RY, RY), 1
    )

    def column(row, mask, n):
        full = jnp.broadcast_to(row, (n, n))
        col = jnp.sum(jnp.where(mask, full, 0.0), axis=1, keepdims=True)
        return jnp.broadcast_to(col, (n, 128))

    stc = [column(st[m : m + 1, :], eye, RY) for m in range(5)]
    tile_out[0:1, :] = stc[0][0:1]
    tile_out[1:2, :] = stc[1][0:1]
    tile_out[2:3, :] = stc[4][RY - 1 : RY]
    tile_out[3:4, :] = stc[3][RY - 1 : RY]
    tile_out[4:8, :] = jnp.zeros((4, 128), F32)

    def tcopy(way):
        return pltpu.make_async_remote_copy(
            src_ref=tile_out,
            dst_ref=tile_in.at[way],
            send_sem=ts.at[way],
            recv_sem=tr.at[way],
            device_id=(above if way == 0 else under, me_s),
            device_id_type=MESH,
        )

    tcopy(0).start()
    tcopy(1).start()

    nn = (((1,), (0,)), ((), ()))
    lane_i = lax.broadcasted_iota(jnp.int32, (RY, NW * RY), 1)
    in_row = (lane_i & (RY - 1)) == lax.broadcasted_iota(jnp.int32, (RY, NW * RY), 0)
    to_slab = (
        lax.broadcasted_iota(jnp.int32, (NW * RY, 128), 0) // RY
        == lax.broadcasted_iota(jnp.int32, (NW * RY, 128), 1)
    ).astype(F32).astype(jnp.bfloat16)
    both = jnp.concatenate(
        [
            jnp.where(in_row, jnp.broadcast_to(v[0:1, :], (RY, NW * RY)), 0.0)
            for v in (lower, upper)
        ],
        axis=0,
    )
    tall = None
    for _part in range(3):
        head = both.astype(jnp.bfloat16)
        both = both - head.astype(F32)
        term = lax.dot_general(head, to_slab, nn, preferred_element_type=F32)
        tall = term if tall is None else tall + term
    lmat[...] = tall[0:RY]
    umat[...] = tall[RY : 2 * RY]

    zero = jnp.zeros((1, 128), F32)
    carry_c, carry_b = zero, None
    for j in range(RY):
        low, upp = lmat[j : j + 1, :], umat[j : j + 1, :]
        inv = 1.0 / (1.0 - low * carry_c) if j > 0 else jnp.ones((1, 128), F32)
        carry_c = upp * inv
        dmat[j : j + 1, :] = inv
        cmat[j : j + 1, :] = carry_c
    binv = [None] * RY
    for j in range(RY - 1, -1, -1):
        if j == RY - 1:
            binv[j] = jnp.ones((1, 128), F32)
        else:
            binv[j] = 1.0 / (
                1.0 - umat[j : j + 1, :] * lmat[j + 1 : j + 2, :] * binv[j + 1]
            )
    y = binv[0]
    ymat[0:1, :] = y
    for j in range(1, RY):
        y = -(umat[j - 1 : j, :] * binv[j]) * y
        ymat[j : j + 1, :] = y
    z = dmat[RY - 1 : RY, :]
    zmat[RY - 1 : RY, :] = z
    for j in range(RY - 2, -1, -1):
        z = -(lmat[j + 1 : j + 2, :] * dmat[j : j + 1, :]) * z
        zmat[j : j + 1, :] = z

    lane16 = lax.broadcasted_iota(jnp.int32, (RY, 128), 1)

    def at_slab(values, slab):
        n = values.shape[0]
        col = jnp.sum(jnp.where(lane16[0:n] == slab, values, 0.0), axis=1, keepdims=True)
        return jnp.broadcast_to(col, (n, 128))

    low_all, upp_all = lmat[...], umat[...]
    inv_own = at_slab(dmat[...], me_w)
    c_own = at_slab(cmat[...], me_w)
    y_own = at_slab(ymat[...], me_w)
    z_own = at_slab(zmat[...], me_w)
    low_own = at_slab(low_all, me_w)
    low_next = at_slab(low_all[0:1], me_w + 1)
    upp_prev = at_slab(upp_all[RY - 1 : RY], me_w - 1)
    has_under = jnp.where(me_w > 0, 1.0, 0.0)
    has_above = jnp.where(me_w < NW - 1, 1.0, 0.0)

    row_i = lax.broadcasted_iota(jnp.int32, (RY, 128), 0)
    kept = [
        jnp.where(row_i == 0, 0.0, jnp.where(row_i == 1, stc[0] * has_under, stc[0])),
        jnp.where(row_i == 0, 0.0, stc[1]),
        stc[2],
        jnp.where(row_i == RY - 1, 0.0, stc[3]),
        jnp.where(
            row_i == RY - 1, 0.0, jnp.where(row_i == RY - 2, stc[4] * has_above, stc[4])
        ),
    ]
    for m in range(5):
        coef[m] = kept[m] * inv_own
    coef[5] = jnp.where(row_i == 0, 0.0, low_own * inv_own)
    coef[6] = c_own
    coef[7] = inv_own

    tcopy(0).wait()
    tcopy(1).wait()
    for way, own, scale in ((0, z_own, low_next), (1, y_own, upp_prev)):
        wmat[...] = jnp.zeros((RY + 8, 128), F32)
        for m in range(5):
            wmat[m + 2 : m + 2 + RY, :] += kept[m] * own
        wgt[way] = wmat[...] * (-scale)
    wgt[0, RY + 2 : RY + 3, :] += tile_in[1, 0:1, :]
    wgt[0, RY + 3 : RY + 4, :] += tile_in[1, 1:2, :]
    wgt[1, 5:6, :] += tile_in[0, 2:3, :]
    wgt[1, 4:5, :] += tile_in[0, 3:4, :]

    eye16 = lax.broadcasted_iota(jnp.int32, (NW, NW), 0) == lax.broadcasted_iota(
        jnp.int32, (NW, NW), 1
    )
    next16 = lax.broadcasted_iota(jnp.int32, (NW, NW), 0) + 1 == lax.broadcasted_iota(
        jnp.int32, (NW, NW), 1
    )
    prev16 = lax.broadcasted_iota(jnp.int32, (NW, NW), 0) - 1 == lax.broadcasted_iota(
        jnp.int32, (NW, NW), 1
    )
    z0 = column(zmat[0:1, 0:NW], eye16, NW)
    z1 = column(zmat[RY - 1 : RY, 0:NW], eye16, NW)
    y0 = column(ymat[0:1, 0:NW], eye16, NW)
    y1 = column(ymat[RY - 1 : RY, 0:NW], eye16, NW)
    low_n = column(low_all[0:1, 0:NW], next16, NW)
    upp_p = column(upp_all[RY - 1 : RY, 0:NW], prev16, NW)
    red[0] = upp_p * y0
    red[1] = low_n * z0
    lz1 = low_n * z1
    uy1 = upp_p * y1
    q = -lz1[0:1]
    for s in range(1, NW):
        dinv = 1.0 / (1.0 + red[0, s : s + 1, :] * q)
        c3 = uy1[s : s + 1] * dinv
        red[2, s : s + 1, :] = q * dinv
        red[3, s : s + 1, :] = dinv
        red[4, s : s + 1, :] = c3
        red[5, s : s + 1, :] = q
        q = red[1, s : s + 1, :] * q * c3 - lz1[s : s + 1]

    for c in range(3):
        for h in range(2):
            vcopy(c, h).wait()

            @pl.loop(0, 2)
            def _(x):
                cols = pl.ds(pl.multiple_of(x * 512, 512), 512)
                up = jnp.zeros((8, 512), F32)
                down = jnp.zeros((8, 512), F32)
                for j in range(RY):
                    u = vbuf[c, j, h * 8 : h * 8 + 8, cols]
                    up = up + wgt[0, j + 4 : j + 5, 0:1] * u
                    down = down + wgt[1, j + 4 : j + 5, 0:1] * u
                for b in range(4):
                    send_a[h * 8 + x * 4 + b, 0, c] = up[:, b * 128 : b * 128 + 128]
                    send_a[h * 8 + x * 4 + b, 1, c] = down[:, b * 128 : b * 128 + 128]

    hcopy(0).wait()
    hcopy(1).wait()
    for h in range(2):

        @pl.loop(0, 8)
        def _(x):
            cols = pl.ds(pl.multiple_of(x * 128, 128), 128)
            for c in range(3):
                lo = halo[0, c, h * 8 : h * 8 + 8, cols]
                hi = halo[1, c, h * 8 : h * 8 + 8, cols]
                for way in range(2):
                    send_a[h * 8 + x, way, c] += (
                        wgt[way, 3:4, 0:1] * lo + wgt[way, RY + 4 : RY + 5, 0:1] * hi
                    )

    def acopy(k):
        to = lax.rem(me_w + k, NW)
        return pltpu.make_async_remote_copy(
            src_ref=send_a.at[to],
            dst_ref=recv_a.at[me_w],
            send_sem=as_.at[k],
            recv_sem=ar.at[k],
            device_id=(to, me_s),
            device_id_type=MESH,
        )

    for k in range(1, NW):
        acopy(k).start()
    recv_a[me_w] = send_a[me_w]

    count = counts[0]
    pack[...] = jnp.zeros((2, NW * NS, 128), F32)
    up_i = lax.broadcasted_iota(jnp.int32, (256, 256), 0)
    up_j = lax.broadcasted_iota(jnp.int32, (256, 256), 1)
    before = (up_i < up_j).astype(F32).astype(jnp.bfloat16)
    ones = jnp.ones((256, 256), jnp.bfloat16)
    ids = lax.broadcasted_iota(jnp.int32, (NW * NS, 256), 0)
    ranks = lax.broadcasted_iota(jnp.int32, (SLOTS, 256), 0).astype(F32)
    lanes = lax.broadcasted_iota(jnp.int32, (1, 256), 1)
    nt = (((1,), (1,)), ((), ()))

    def pack_block(i, carry):
        at = pl.ds(pl.multiple_of(i * 256, 256), 256)
        own = owner[:, at]
        key = (own & 7) * NW + (own >> 3)
        key = jnp.where(lanes + i * 256 < count, key, 512)
        hit = ids == key
        hot = jnp.where(hit, 1.0, 0.0)
        hot_b = hot.astype(jnp.bfloat16)
        pre = lax.dot_general(hot_b, before, nn, preferred_element_type=F32)
        tot = lax.dot_general(hot_b, ones, nn, preferred_element_type=F32)
        rank = jnp.sum(jnp.where(hit, pre + carry, 0.0), axis=0, keepdims=True)
        place = ranks == rank
        load = [forces[c : c + 1, at] for c in range(3)] + [cells[:, at].astype(F32)]
        sums = None
        for _part in range(3):
            head = [x.astype(jnp.bfloat16).astype(F32) for x in load]
            load = [x - y for x, y in zip(load, head)]
            right = jnp.concatenate(
                [jnp.where(place, y, 0.0) for y in head], axis=0
            ).astype(jnp.bfloat16)
            term = lax.dot_general(hot_b, right, nt, preferred_element_type=F32)
            sums = term if sums is None else sums + term
        pack[0] += sums[:, 0:128]
        pack[1] += sums[:, 128:256]
        return carry + tot

    lax.fori_loop(
        0, owner.shape[1] // 256, pack_block, jnp.zeros((NW * NS, 256), F32)
    )

    def p1copy(k):
        to = lax.rem(me_s + k, NS)
        return pltpu.make_async_remote_copy(
            src_ref=pack.at[:, pl.ds(pl.multiple_of(to * NW, NW), NW)],
            dst_ref=recv1.at[:, pl.ds(pl.multiple_of(me_s * NW, NW), NW)],
            send_sem=p1s.at[k],
            recv_sem=p1r.at[k],
            device_id=(me_w, to),
            device_id_type=MESH,
        )

    for k in range(1, NS):
        p1copy(k).start()
    mine = pl.ds(pl.multiple_of(me_s * NW, NW), NW)
    recv1[:, mine, :] = pack[:, mine, :]

    for k in range(1, NW):
        acopy(k).wait()

    p = recv_a[0, 0]
    for s in range(1, NW):
        pbuf[s] = p
        e = recv_a[s, 1] - red[0, s : s + 1, :] * p
        elim[s] = e
        if s < NW - 1:
            p = recv_a[s, 0] - red[1, s : s + 1, :] * (p + red[2, s : s + 1, :] * e)
    down = jnp.zeros((3, 8, 128), F32)
    send_f[NW - 1, 1] = down
    for s in range(NW - 1, 0, -1):
        down = red[3, s : s + 1, :] * elim[s] - red[4, s : s + 1, :] * down
        send_f[s - 1, 1] = down
        send_f[s, 0] = pbuf[s] + red[5, s : s + 1, :] * down
    send_f[0, 0] = jnp.zeros((3, 8, 128), F32)

    def fcopy(k):
        to = lax.rem(me_w + k, NW)
        return pltpu.make_async_remote_copy(
            src_ref=send_f.at[to],
            dst_ref=bound.at[me_w],
            send_sem=fs.at[k],
            recv_sem=fr.at[k],
            device_id=(to, me_s),
            device_id_type=MESH,
        )

    for k in range(1, NW):
        fcopy(k).start()
    bound[me_w] = send_f[me_w]

    for k in range(1, NS):
        p1copy(k).wait()
    for w in range(NW):
        for b in range(2):
            pack2[w, b] = recv1[b, pl.ds(w, NS, stride=NW), :]

    def p2copy(k):
        to = lax.rem(me_w + k, NW)
        return pltpu.make_async_remote_copy(
            src_ref=pack2.at[to],
            dst_ref=recv2.at[me_w],
            send_sem=p2s.at[k],
            recv_sem=p2r.at[k],
            device_id=(to, me_s),
            device_id_type=MESH,
        )

    for k in range(1, NW):
        p2copy(k).start()
    recv2[me_w] = pack2[me_w]

    for k in range(1, NW):
        p2copy(k).wait()
    part_t[0:128, :] = recv2[:, 0].reshape(NW * NS, 128).T
    rest = recv2[:, 1].reshape(NW * NS, 128)
    flipped = rest.T
    part_t[128:192, :] = flipped[0:64]
    part_t[192:256, :] = (flipped[64:128].astype(jnp.int32) & 127).astype(F32)
    place = rest[:, 64:128].astype(jnp.int32)
    rows_out[...] = (
        (place >> 13) * 64 + ((place >> 7) & 7) * 8 + ((place >> 10) & 7)
    ) * 4

    for k in range(1, NW):
        fcopy(k).wait()


def exchange(vel, lower, upper, st, forces, owner, cells, counts):
    vm = pl.BlockSpec(memory_space=pltpu.VMEM)
    dma = pltpu.SemaphoreType.DMA
    return pl.pallas_call(
        exchange_kernel,
        out_shape=(
            jax.ShapeDtypeStruct((2, 3, SZ, NX), F32),
            jax.ShapeDtypeStruct((NW, 2, 3, 8, 128), F32),
            jax.ShapeDtypeStruct((8, RY, 128), F32),
            jax.ShapeDtypeStruct((256, 128), F32),
            jax.ShapeDtypeStruct((128, SLOTS), jnp.int32),
        ),
        in_specs=[pl.BlockSpec(memory_space=pl.ANY)] + [vm] * 6
        + [pl.BlockSpec(memory_space=pltpu.SMEM)],
        out_specs=[vm] * 5,
        scratch_shapes=[
            pltpu.VMEM((3, RY, SZ, NX), F32),
            pltpu.VMEM((NW, 2, 3, 8, 128), F32),
            pltpu.VMEM((NW, 2, 3, 8, 128), F32),
            pltpu.VMEM((NW, 2, 3, 8, 128), F32),
            pltpu.VMEM((NW, 3, 8, 128), F32),
            pltpu.VMEM((NW, 3, 8, 128), F32),
            pltpu.VMEM((8, 128), F32),
            pltpu.VMEM((2, 8, 128), F32),
            pltpu.VMEM((2, NW * NS, 128), F32),
            pltpu.VMEM((2, NW * NS, 128), F32),
            pltpu.VMEM((NW, 2, NS, 128), F32),
            pltpu.VMEM((NW, 2, NS, 128), F32),
            pltpu.VMEM((RY, 128), F32),
            pltpu.VMEM((RY, 128), F32),
            pltpu.VMEM((RY, 128), F32),
            pltpu.VMEM((RY, 128), F32),
            pltpu.VMEM((RY, 128), F32),
            pltpu.VMEM((RY, 128), F32),
            pltpu.VMEM((RY + 8, 128), F32),
            pltpu.VMEM((2, RY + 8, 128), F32),
            pltpu.VMEM((6, NW, 128), F32),
            dma((6,)), dma((2,)), dma((2,)), dma((2,)), dma((2,)),
            dma((NW,)), dma((NW,)), dma((NW,)), dma((NW,)),
            dma((NS,)), dma((NS,)), dma((NW,)), dma((NW,)),
        ],
        compiler_params=pltpu.CompilerParams(
            collective_id=0, has_side_effects=True, vmem_limit_bytes=56 << 20
        ),
        name="exchange",
    )(vel, lower, upper, st, forces, owner, cells, counts)


def local_kernel(
    vel, halo, bound, coef, part_t, rows, inv_vol,
    derivative, forcing,
    acc0, acc1, acc2, acc3, even, odd, mixed, vbuf, stage, vsem, dsem, fsem,
):
    def take(c):
        return pltpu.make_async_copy(vel.at[c], vbuf.at[c], vsem.at[c])

    for c in range(3):
        take(c).start()

    accs = (acc0, acc1, acc2, acc3)
    zeros = jnp.zeros((128, 128), F32)

    @pl.loop(0, 128)
    def _(i):
        at = pl.ds(pl.multiple_of(i * 128, 128), 128)
        for acc in accs:
            acc[at, :] = zeros

    lane = lax.broadcasted_iota(jnp.int32, (8, 128), 1).astype(F32)

    def spread(source, to):
        pick = jnp.full((8, 128), source, jnp.int32)
        for g in range(SLOTS // 8):
            xl = jnp.take_along_axis(part_t[192 + g * 8 : 200 + g * 8, :], pick, axis=1)
            hit = xl == lane
            for c in range(3):
                r0 = c * SLOTS + g * 8
                f = jnp.take_along_axis(part_t[r0 : r0 + 8, :], pick, axis=1)
                to[r0 : r0 + 8, :] = jnp.where(hit, f, 0.0)

    def add(source, frm):
        for r in range(SLOTS):
            at = pl.ds(pl.multiple_of(rows[source, r], 4), 4)
            accs[r % 4][at, :] += frm[pl.ds(r, 4, stride=SLOTS), :]

    even[192:256, :] = jnp.zeros((64, 128), F32)
    odd[192:256, :] = jnp.zeros((64, 128), F32)
    spread(0, even)

    @pl.loop(0, 64)
    def _(i):
        spread(2 * i + 1, odd)
        add(2 * i, even)
        spread(jnp.minimum(2 * i + 2, 127), even)
        add(2 * i + 1, odd)

    def put_f(b):
        part = (slice(None), pl.ds(b * 4, 4))
        return pltpu.make_async_copy(stage.at[part], forcing.at[part], fsem.at[b])

    @pl.loop(0, 8)
    def _(b):
        @pl.loop(0, 8)
        def _(jh):
            j, h = b * 4 + jh // 2, jh % 2
            scale = -inv_vol[j]
            cells = pl.ds(pl.multiple_of(h * 8, 8), 8)
            for x in range(8):
                at = pl.ds(pl.multiple_of(((j * 2 + h) * 8 + x) * 32, 32), 32)
                mixed[x * 32 : x * 32 + 32, :] = scale * (
                    (acc0[at, :] + acc1[at, :]) + (acc2[at, :] + acc3[at, :])
                )
            for x in range(8):
                for c in range(3):
                    stage[c, j, cells, x * 128 : x * 128 + 128] = mixed[
                        pl.ds(x * 32 + c, 8, stride=4), :
                    ]

        put_f(b).start()

    def put_d(c, x):
        part = (c, slice(None), slice(None), pl.ds(x * 512, 512))
        return pltpu.make_async_copy(vbuf.at[part], derivative.at[part], dsem.at[c * 2 + x])

    for c in range(3):
        take(c).wait()
        for half in range(2):

            @pl.loop(0, 4)
            def _(xx):
                x = half * 4 + xx
                cols = pl.ds(pl.multiple_of(x * 128, 128), 128)

                def row(i):
                    if i < -1 or i > RY:
                        return None
                    if i == -1:
                        return halo[0, c, :, cols]
                    if i == RY:
                        return halo[1, c, :, cols]
                    return vbuf[c, i, :, cols]

                def edge(way):
                    return jnp.concatenate([bound[x, way, c], bound[8 + x, way, c]], axis=0)

                window = [row(i) for i in range(-2, 3)]
                prev = None
                for j in range(RY):
                    total = None
                    for m in range(5):
                        if window[m] is None or j + m - 2 == -1 and j == 0:
                            continue
                        if j + m - 2 == RY and j == RY - 1:
                            continue
                        term = coef[m, j : j + 1, :] * window[m]
                        total = term if total is None else total + term
                    if j == 0:
                        total = total + coef[7, 0:1, :] * edge(0)
                    if j == RY - 1:
                        total = total + coef[7, RY - 1 : RY, :] * edge(1)
                    if j > 0:
                        total = total - coef[5, j : j + 1, :] * prev
                    prev = total
                    window = window[1:] + [row(j + 3)]
                    vbuf[c, j, :, cols] = total
                for j in range(RY - 2, -1, -1):
                    prev = vbuf[c, j, :, cols] - coef[6, j : j + 1, :] * prev
                    vbuf[c, j, :, cols] = prev

            put_d(c, half).start()

    for c in range(3):
        for half in range(2):
            put_d(c, half).wait()

    @pl.loop(0, 8)
    def _(b):
        put_f(b).wait()


def local(vel, halo, bound, coef, part_t, rows, inv_vol):
    sm = pl.BlockSpec(memory_space=pltpu.SMEM)
    vm = pl.BlockSpec(memory_space=pltpu.VMEM)
    hbm = pl.BlockSpec(memory_space=pl.ANY)
    depth = RY * SZ * NX // 128 * 4
    whole = (3, RY, SZ, NX)
    return pl.pallas_call(
        local_kernel,
        out_shape=(jax.ShapeDtypeStruct(whole, F32), jax.ShapeDtypeStruct(whole, F32)),
        in_specs=[hbm, vm, vm, vm, vm, sm, sm],
        out_specs=(hbm, hbm),
        scratch_shapes=[pltpu.VMEM((depth, 128), F32)] * 4
        + [pltpu.VMEM((256, 128), F32)] * 3
        + [pltpu.VMEM(whole, F32)] * 2
        + [pltpu.SemaphoreType.DMA((n,)) for n in (3, 6, 8)],
        compiler_params=pltpu.CompilerParams(vmem_limit_bytes=58 << 20),
        name="local",
    )(vel, halo, bound, coef, part_t, rows, inv_vol)


def body(velocity, lower, upper, stencil, inv_volume, forces, owner, cells, counts):
    halo, bound, coef, part_t, rows = exchange(
        velocity, lower.reshape(1, -1), upper.reshape(1, -1), stencil, forces,
        owner.reshape(1, -1), cells.reshape(1, -1), counts,
    )
    derivative, forcing = local(velocity, halo, bound, coef, part_t, rows, inv_volume)
    return derivative, forcing


def solution(mesh):
    in_specs = (
        P(None, "wall", "span", None),
        P(),
        P(),
        P(None, "wall"),
        P("wall"),
        P(None, ("wall", "span")),
        P(("wall", "span"), None),
        P(("wall", "span")),
        P(("wall", "span")),
    )
    out_specs = (P(None, "wall", "span", None), P(None, "wall", "span", None))
    return jax.shard_map(body, mesh=mesh, in_specs=in_specs, out_specs=out_specs, check_vma=False)
```

time: 90.8 us -> 69.8 us (0.77)
  Pallas kernels: 86.7 us -> 67.8 us
  local copies, waits for them, and re-layouts: 1.67 us -> 0 us
    pallas_call x2 -> x1, Pallas kernels: 46.9 us -> 29.4 us  [local(): pl.pallas_call(local_kernel, out_shape=(jax.ShapeDtypeStruct(whole, F32),...]
    another operation x4 -> x0, local copies, waits for them, and re-layouts: 1.67 us -> none  [body(): lu = jnp.stack([lower, upper]).reshape(2, NW, RY).transpose(0, 2, 1)]
    pallas_call x1, Pallas kernels: 39.9 us -> 38.4 us  [exchange(): pl.pallas_call(exchange_kernel, out_shape=(jax.ShapeDtypeStruct((2, 3, SZ...]
where the time goes in v2:
time: 69.8 us; the launch traced here: 69.1 us
  Pallas kernels  67.8 us (97%)
  between operations  1.29 us (2%)
    pallas_call x1, Pallas kernels, exchange(): pl.pallas_call(exchange_kernel, out_shape=(jax.ShapeDtypeStruct((2, 3, SZ...  38.4 us
    pallas_call x1, Pallas kernels, local(): pl.pallas_call(local_kernel, out_shape=(jax.ShapeDtypeStruct(whole, F32),...  29.4 us

profile of v2, /device:TPU:0, one launch (start us, length us, event | category | flops | bytes accessed | tf_op | source)
XLA Modules:
  0.0 69.1 jit_solution(4564260342278042632)
XLA Ops:
  1.3 38.4 %exchange.1 = (f32[2,3,16,1024]{3,2,1,0:T(8,128)}, f32[16,2,3,8,128]{4,3,2,1,0:T(8,128)}, f32[8,32,128]{2,1,0:T(8,128)}, f32[256,128]{1,0:T(8,128)}, s32[128,64]{1,0:T(8,128)}) custom-call(f32[3,32,16,1024]{3,2,1,0:T(8,128)} %vel.3, f32[1,512]{1,0:T(1,128)} %bitcast.6, f32[1,512]{1,0:T(1,128)} %bitcast.7, f32[5,32]{1,0:T(8,128)} %st.1, f32[3,4096]{1,0:T(4,128)} %forces.1, ...), custom_call_target="tpu_custom_call" | custom-call | tf_op jit(solution)/shard_map/exchange/pallas_call | solution.py:399
  39.7 29.4 %local.1 = (f32[3,32,16,1024]{3,2,1,0:T(8,128)}, f32[3,32,16,1024]{3,2,1,0:T(8,128)}) custom-call(f32[3,32,16,1024]{3,2,1,0:T(8,128)} %vel.3, f32[2,3,16,1024]{3,2,1,0:T(8,128)} %get-tuple-element.7.halo, f32[16,2,3,8,128]{4,3,2,1,0:T(8,128)} %get-tuple-element.8.bound, f32[8,32,128]{2,1,0:T(8,128)} %get-tuple-element.9.coef, ...), custom_call_target="tpu_custom_call" | custom-call | tf_op jit(solution)/shard_map/local/pallas_call | solution.py:582

commit v3 on v2

--- a/solution.py
+++ b/solution.py
@@ -15,12 +15,13 @@
 
 
 def exchange_kernel(
-    vel, lower, upper, st, forces, owner, cells, counts,
-    halo, bound, coef, part_t, rows_out,
+    vel, lower_h, upper_h, st_h, forces_h, owner_h, cells_h, counts_h,
+    halo_h, bound, coef_h, part_h, rows_h,
+    lower, upper, st, forces, owner, cells, counts, halo, coef, part_t, rows_v,
     vbuf, send_a, recv_a, send_f, elim, pbuf, tile_out, tile_in,
     pack, recv1, pack2, recv2,
     lmat, umat, dmat, cmat, ymat, zmat, wmat, wgt, red,
-    vsem, hs, hr, ts, tr, as_, ar, fs, fr, p1s, p1r, p2s, p2r,
+    isem, osem, vsem, hs, hr, ts, tr, as_, ar, fs, fr, p1s, p1r, p2s, p2r,
 ):
     me_w = lax.axis_index("wall")
     me_s = lax.axis_index("span")
@@ -28,10 +29,6 @@
     def vcopy(c, h):
         part = (c, slice(None), pl.ds(h * 8, 8), slice(None))
         return pltpu.make_async_copy(vel.at[part], vbuf.at[part], vsem.at[c * 2 + h])
-
-    for c in range(3):
-        for h in range(2):
-            vcopy(c, h).start()
 
     barrier = pltpu.get_barrier_semaphore()
 
@@ -47,6 +44,20 @@
             barrier, inc=1, device_id=(me_w, lax.rem(me_s + k, NS)), device_id_type=MESH
         )
 
+    staged = (
+        (st_h, st), (lower_h, lower), (upper_h, upper),
+        (forces_h, forces), (owner_h, owner), (cells_h, cells), (counts_h, counts),
+    )
+    loads = [
+        pltpu.make_async_copy(src, dst, isem.at[i]) for i, (src, dst) in enumerate(staged)
+    ]
+    for i in range(3):
+        loads[i].start()
+    for c in range(3):
+        for h in range(2):
+            vcopy(c, h).start()
+    for i in range(3, 7):
+        loads[i].start()
     pl.semaphore_wait(barrier, NW - 1 + NS - 1)
 
     above = lax.rem(me_w + 1, NW)
@@ -65,6 +76,8 @@
     hcopy(0).start()
     hcopy(1).start()
 
+    for i in range(3):
+        loads[i].wait()
     eye = lax.broadcasted_iota(jnp.int32, (RY, RY), 0) == lax.broadcasted_iota(
         jnp.int32, (RY, RY), 1
     )
@@ -177,6 +190,8 @@
     coef[5] = jnp.where(row_i == 0, 0.0, low_own * inv_own)
     coef[6] = c_own
     coef[7] = inv_own
+    keep_coef = pltpu.make_async_copy(coef, coef_h, osem.at[0])
+    keep_coef.start()
 
     tcopy(0).wait()
     tcopy(1).wait()
@@ -225,19 +240,24 @@
 
             @pl.loop(0, 2)
             def _(x):
-                cols = pl.ds(pl.multiple_of(x * 512, 512), 512)
-                up = jnp.zeros((8, 512), F32)
-                down = jnp.zeros((8, 512), F32)
+                cols = [
+                    pl.ds(pl.multiple_of(x * 512 + b * 128, 128), 128) for b in range(4)
+                ]
+                up, down = [None] * 4, [None] * 4
                 for j in range(RY):
-                    u = vbuf[c, j, h * 8 : h * 8 + 8, cols]
-                    up = up + wgt[0, j + 4 : j + 5, 0:1] * u
-                    down = down + wgt[1, j + 4 : j + 5, 0:1] * u
+                    wu, wd = wgt[0, j + 4 : j + 5, :], wgt[1, j + 4 : j + 5, :]
+                    for b in range(4):
+                        u = vbuf[c, j, h * 8 : h * 8 + 8, cols[b]]
+                        up[b] = wu * u if j == 0 else up[b] + wu * u
+                        down[b] = wd * u if j == 0 else down[b] + wd * u
                 for b in range(4):
-                    send_a[h * 8 + x * 4 + b, 0, c] = up[:, b * 128 : b * 128 + 128]
-                    send_a[h * 8 + x * 4 + b, 1, c] = down[:, b * 128 : b * 128 + 128]
+                    send_a[h * 8 + x * 4 + b, 0, c] = up[b]
+                    send_a[h * 8 + x * 4 + b, 1, c] = down[b]
 
     hcopy(0).wait()
     hcopy(1).wait()
+    keep_halo = pltpu.make_async_copy(halo, halo_h, osem.at[1])
+    keep_halo.start()
     for h in range(2):
 
         @pl.loop(0, 8)
@@ -248,7 +268,7 @@
                 hi = halo[1, c, h * 8 : h * 8 + 8, cols]
                 for way in range(2):
                     send_a[h * 8 + x, way, c] += (
-                        wgt[way, 3:4, 0:1] * lo + wgt[way, RY + 4 : RY + 5, 0:1] * hi
+                        wgt[way, 3:4, :] * lo + wgt[way, RY + 4 : RY + 5, :] * hi
                     )
 
     def acopy(k):
@@ -266,6 +286,8 @@
         acopy(k).start()
     recv_a[me_w] = send_a[me_w]
 
+    for i in range(3, 7):
+        loads[i].wait()
     count = counts[0]
     pack[...] = jnp.zeros((2, NW * NS, 128), F32)
     up_i = lax.broadcasted_iota(jnp.int32, (256, 256), 0)
@@ -304,7 +326,7 @@
         return carry + tot
 
     lax.fori_loop(
-        0, owner.shape[1] // 256, pack_block, jnp.zeros((NW * NS, 256), F32)
+        0, owner.shape[1] // 256, pack_block, jnp.zeros((NW * NS, 256), F32), unroll=4
     )
 
     def p1copy(k):
@@ -322,6 +344,27 @@
         p1copy(k).start()
     mine = pl.ds(pl.multiple_of(me_s * NW, NW), NW)
     recv1[:, mine, :] = pack[:, mine, :]
+
+    for k in range(1, NS):
+        p1copy(k).wait()
+    for w in range(NW):
+        for b in range(2):
+            pack2[w, b] = recv1[b, pl.ds(w, NS, stride=NW), :]
+
+    def p2copy(k):
+        to = lax.rem(me_w + k, NW)
+        return pltpu.make_async_remote_copy(
+            src_ref=pack2.at[to],
+            dst_ref=recv2.at[me_w],
+            send_sem=p2s.at[k],
+            recv_sem=p2r.at[k],
+            device_id=(to, me_s),
+            device_id_type=MESH,
+        )
+
+    for k in range(1, NW):
+        p2copy(k).start()
+    recv2[me_w] = pack2[me_w]
 
     for k in range(1, NW):
         acopy(k).wait()
@@ -354,28 +397,8 @@
 
     for k in range(1, NW):
         fcopy(k).start()
-    bound[me_w] = send_f[me_w]
-
-    for k in range(1, NS):
-        p1copy(k).wait()
-    for w in range(NW):
-        for b in range(2):
-            pack2[w, b] = recv1[b, pl.ds(w, NS, stride=NW), :]
-
-    def p2copy(k):
-        to = lax.rem(me_w + k, NW)
-        return pltpu.make_async_remote_copy(
-            src_ref=pack2.at[to],
-            dst_ref=recv2.at[me_w],
-            send_sem=p2s.at[k],
-            recv_sem=p2r.at[k],
-            device_id=(to, me_s),
-            device_id_type=MESH,
-        )
-
-    for k in range(1, NW):
-        p2copy(k).start()
-    recv2[me_w] = pack2[me_w]
+    keep_own = pltpu.make_async_copy(send_f.at[me_w], bound.at[me_w], osem.at[2])
+    keep_own.start()
 
     for k in range(1, NW):
         p2copy(k).wait()
@@ -384,17 +407,23 @@
     flipped = rest.T
     part_t[128:192, :] = flipped[0:64]
     part_t[192:256, :] = (flipped[64:128].astype(jnp.int32) & 127).astype(F32)
-    place = rest[:, 64:128].astype(jnp.int32)
-    rows_out[...] = (
+    place = rest.astype(jnp.int32)
+    rows_v[...] = (
         (place >> 13) * 64 + ((place >> 7) & 7) * 8 + ((place >> 10) & 7)
     ) * 4
+    keep_part = pltpu.make_async_copy(part_t, part_h, osem.at[3])
+    keep_part.start()
+    keep_rows = pltpu.make_async_copy(rows_v, rows_h, osem.at[4])
+    keep_rows.start()
 
     for k in range(1, NW):
         fcopy(k).wait()
+    for keep in (keep_coef, keep_halo, keep_own, keep_part, keep_rows):
+        keep.wait()
 
 
 def exchange(vel, lower, upper, st, forces, owner, cells, counts):
-    vm = pl.BlockSpec(memory_space=pltpu.VMEM)
+    hbm = pl.BlockSpec(memory_space=pl.ANY)
     dma = pltpu.SemaphoreType.DMA
     return pl.pallas_call(
         exchange_kernel,
@@ -403,12 +432,22 @@
             jax.ShapeDtypeStruct((NW, 2, 3, 8, 128), F32),
             jax.ShapeDtypeStruct((8, RY, 128), F32),
             jax.ShapeDtypeStruct((256, 128), F32),
-            jax.ShapeDtypeStruct((128, SLOTS), jnp.int32),
+            jax.ShapeDtypeStruct((128, 128), jnp.int32),
         ),
-        in_specs=[pl.BlockSpec(memory_space=pl.ANY)] + [vm] * 6
-        + [pl.BlockSpec(memory_space=pltpu.SMEM)],
-        out_specs=[vm] * 5,
+        in_specs=[hbm] * 8,
+        out_specs=[hbm] * 5,
         scratch_shapes=[
+            pltpu.VMEM((1, NW * RY), F32),
+            pltpu.VMEM((1, NW * RY), F32),
+            pltpu.VMEM(st.shape, F32),
+            pltpu.VMEM(forces.shape, F32),
+            pltpu.VMEM(owner.shape, jnp.int32),
+            pltpu.VMEM(cells.shape, jnp.int32),
+            pltpu.SMEM((1,), jnp.int32),
+            pltpu.VMEM((2, 3, SZ, NX), F32),
+            pltpu.VMEM((8, RY, 128), F32),
+            pltpu.VMEM((256, 128), F32),
+            pltpu.VMEM((128, 128), jnp.int32),
             pltpu.VMEM((3, RY, SZ, NX), F32),
             pltpu.VMEM((NW, 2, 3, 8, 128), F32),
             pltpu.VMEM((NW, 2, 3, 8, 128), F32),
@@ -430,7 +469,7 @@
             pltpu.VMEM((RY + 8, 128), F32),
             pltpu.VMEM((2, RY + 8, 128), F32),
             pltpu.VMEM((6, NW, 128), F32),
-            dma((6,)), dma((2,)), dma((2,)), dma((2,)), dma((2,)),
+            dma((7,)), dma((5,)), dma((6,)), dma((2,)), dma((2,)), dma((2,)), dma((2,)),
             dma((NW,)), dma((NW,)), dma((NW,)), dma((NW,)),
             dma((NS,)), dma((NS,)), dma((NW,)), dma((NW,)),
         ],
@@ -442,15 +481,24 @@
 
 
 def local_kernel(
-    vel, halo, bound, coef, part_t, rows, inv_vol,
+    vel, halo_h, bound_h, coef_h, part_h, rows_h, inv_vol,
     derivative, forcing,
-    acc0, acc1, acc2, acc3, even, odd, mixed, vbuf, stage, vsem, dsem, fsem,
+    halo, bound, coef, part_t, rows,
+    acc0, acc1, acc2, acc3, even, odd, mixed, vbuf, stage, isem, vsem, dsem, fsem,
 ):
     def take(c):
         return pltpu.make_async_copy(vel.at[c], vbuf.at[c], vsem.at[c])
 
+    staged = ((coef_h, coef), (bound_h, bound), (halo_h, halo), (part_h, part_t), (rows_h, rows))
+    loads = [
+        pltpu.make_async_copy(src, dst, isem.at[i]) for i, (src, dst) in enumerate(staged)
+    ]
+    for i in range(3):
+        loads[i].start()
     for c in range(3):
         take(c).start()
+    loads[3].start()
+    loads[4].start()
 
     accs = (acc0, acc1, acc2, acc3)
     zeros = jnp.zeros((128, 128), F32)
@@ -461,62 +509,12 @@
         for acc in accs:
             acc[at, :] = zeros
 
-    lane = lax.broadcasted_iota(jnp.int32, (8, 128), 1).astype(F32)
-
-    def spread(source, to):
-        pick = jnp.full((8, 128), source, jnp.int32)
-        for g in range(SLOTS // 8):
-            xl = jnp.take_along_axis(part_t[192 + g * 8 : 200 + g * 8, :], pick, axis=1)
-            hit = xl == lane
-            for c in range(3):
-                r0 = c * SLOTS + g * 8
-                f = jnp.take_along_axis(part_t[r0 : r0 + 8, :], pick, axis=1)
-                to[r0 : r0 + 8, :] = jnp.where(hit, f, 0.0)
-
-    def add(source, frm):
-        for r in range(SLOTS):
-            at = pl.ds(pl.multiple_of(rows[source, r], 4), 4)
-            accs[r % 4][at, :] += frm[pl.ds(r, 4, stride=SLOTS), :]
-
-    even[192:256, :] = jnp.zeros((64, 128), F32)
-    odd[192:256, :] = jnp.zeros((64, 128), F32)
-    spread(0, even)
-
-    @pl.loop(0, 64)
-    def _(i):
-        spread(2 * i + 1, odd)
-        add(2 * i, even)
-        spread(jnp.minimum(2 * i + 2, 127), even)
-        add(2 * i + 1, odd)
-
-    def put_f(b):
-        part = (slice(None), pl.ds(b * 4, 4))
-        return pltpu.make_async_copy(stage.at[part], forcing.at[part], fsem.at[b])
-
-    @pl.loop(0, 8)
-    def _(b):
-        @pl.loop(0, 8)
-        def _(jh):
-            j, h = b * 4 + jh // 2, jh % 2
-            scale = -inv_vol[j]
-            cells = pl.ds(pl.multiple_of(h * 8, 8), 8)
-            for x in range(8):
-                at = pl.ds(pl.multiple_of(((j * 2 + h) * 8 + x) * 32, 32), 32)
-                mixed[x * 32 : x * 32 + 32, :] = scale * (
-                    (acc0[at, :] + acc1[at, :]) + (acc2[at, :] + acc3[at, :])
-                )
-            for x in range(8):
-                for c in range(3):
-                    stage[c, j, cells, x * 128 : x * 128 + 128] = mixed[
-                        pl.ds(x * 32 + c, 8, stride=4), :
-                    ]
-
-        put_f(b).start()
-
     def put_d(c, x):
         part = (c, slice(None), slice(None), pl.ds(x * 512, 512))
         return pltpu.make_async_copy(vbuf.at[part], derivative.at[part], dsem.at[c * 2 + x])
 
+    for i in range(3):
+        loads[i].wait()
     for c in range(3):
         take(c).wait()
         for half in range(2):
@@ -564,6 +562,61 @@
 
             put_d(c, half).start()
 
+    lane = lax.broadcasted_iota(jnp.int32, (8, 128), 1).astype(F32)
+
+    def spread(source, to):
+        pick = jnp.full((8, 128), source, jnp.int32)
+        for g in range(SLOTS // 8):
+            xl = jnp.take_along_axis(part_t[192 + g * 8 : 200 + g * 8, :], pick, axis=1)
+            hit = xl == lane
+            for c in range(3):
+                r0 = c * SLOTS + g * 8
+                f = jnp.take_along_axis(part_t[r0 : r0 + 8, :], pick, axis=1)
+                to[pl.ds(g * 32 + c, 8, stride=4), :] = jnp.where(hit, f, 0.0)
+
+    def add(source, frm):
+        base = source * 128 + SLOTS
+        for r in range(SLOTS):
+            at = pl.ds(pl.multiple_of(rows[base + r], 4), 4)
+            accs[r % 4][at, :] += frm[r * 4 : r * 4 + 4, :]
+
+    even[...] = jnp.zeros((256, 128), F32)
+    odd[...] = jnp.zeros((256, 128), F32)
+    loads[3].wait()
+    loads[4].wait()
+    spread(0, even)
+
+    @pl.loop(0, 64)
+    def _(i):
+        spread(2 * i + 1, odd)
+        add(2 * i, even)
+        spread(jnp.minimum(2 * i + 2, 127), even)
+        add(2 * i + 1, odd)
+
+    def put_f(b):
+        part = (slice(None), pl.ds(b * 4, 4))
+        return pltpu.make_async_copy(stage.at[part], forcing.at[part], fsem.at[b])
+
+    @pl.loop(0, 8)
+    def _(b):
+        @pl.loop(0, 8)
+        def _(jh):
+            j, h = b * 4 + jh // 2, jh % 2
+            scale = -inv_vol[j]
+            cells = pl.ds(pl.multiple_of(h * 8, 8), 8)
+            for x in range(8):
+                at = pl.ds(pl.multiple_of(((j * 2 + h) * 8 + x) * 32, 32), 32)
+                mixed[x * 32 : x * 32 + 32, :] = scale * (
+                    (acc0[at, :] + acc1[at, :]) + (acc2[at, :] + acc3[at, :])
+                )
+            for x in range(8):
+                for c in range(3):
+                    stage[c, j, cells, x * 128 : x * 128 + 128] = mixed[
+                        pl.ds(x * 32 + c, 8, stride=4), :
+                    ]
+
+        put_f(b).start()
+
     for c in range(3):
         for half in range(2):
             put_d(c, half).wait()
@@ -575,19 +628,25 @@
 
 def local(vel, halo, bound, coef, part_t, rows, inv_vol):
     sm = pl.BlockSpec(memory_space=pltpu.SMEM)
-    vm = pl.BlockSpec(memory_space=pltpu.VMEM)
     hbm = pl.BlockSpec(memory_space=pl.ANY)
     depth = RY * SZ * NX // 128 * 4
     whole = (3, RY, SZ, NX)
     return pl.pallas_call(
         local_kernel,
         out_shape=(jax.ShapeDtypeStruct(whole, F32), jax.ShapeDtypeStruct(whole, F32)),
-        in_specs=[hbm, vm, vm, vm, vm, sm, sm],
+        in_specs=[hbm] * 6 + [sm],
         out_specs=(hbm, hbm),
-        scratch_shapes=[pltpu.VMEM((depth, 128), F32)] * 4
+        scratch_shapes=[
+            pltpu.VMEM(halo.shape, F32),
+            pltpu.VMEM(bound.shape, F32),
+            pltpu.VMEM(coef.shape, F32),
+            pltpu.VMEM(part_t.shape, F32),
+            pltpu.SMEM(rows.shape, jnp.int32),
+        ]
+        + [pltpu.VMEM((depth, 128), F32)] * 4
         + [pltpu.VMEM((256, 128), F32)] * 3
         + [pltpu.VMEM(whole, F32)] * 2
-        + [pltpu.SemaphoreType.DMA((n,)) for n in (3, 6, 8)],
+        + [pltpu.SemaphoreType.DMA((n,)) for n in (5, 3, 6, 8)],
         compiler_params=pltpu.CompilerParams(vmem_limit_bytes=58 << 20),
         name="local",
     )(vel, halo, bound, coef, part_t, rows, inv_vol)
@@ -598,7 +657,9 @@
         velocity, lower.reshape(1, -1), upper.reshape(1, -1), stencil, forces,
         owner.reshape(1, -1), cells.reshape(1, -1), counts,
     )
-    derivative, forcing = local(velocity, halo, bound, coef, part_t, rows, inv_volume)
+    derivative, forcing = local(
+        velocity, halo, bound, coef, part_t, rows.reshape(-1), inv_volume
+    )
     return derivative, forcing
 
 

time: 69.8 us -> 63.9 us (0.915)
  Pallas kernels: 67.8 us -> 62.5 us
    pallas_call x1, Pallas kernels: 29.4 us -> 25.6 us  [local(): pl.pallas_call(local_kernel, out_shape=(jax.ShapeDtypeStruct(whole, F32),...]
    pallas_call x1, Pallas kernels: 38.4 us -> 36.9 us  [exchange(): pl.pallas_call(exchange_kernel, out_shape=(jax.ShapeDtypeStruct((2, 3, SZ...]
where the time goes in v3:
time: 63.9 us; the launch traced here: 63.8 us
  Pallas kernels  62.5 us (98%)
  between operations  1.29 us (2%)
    pallas_call x1, Pallas kernels, exchange(): pl.pallas_call(exchange_kernel, out_shape=(jax.ShapeDtypeStruct((2, 3, SZ...  36.9 us
    pallas_call x1, Pallas kernels, local(): pl.pallas_call(local_kernel, out_shape=(jax.ShapeDtypeStruct(whole, F32),...  25.6 us

profile of v3, /device:TPU:0, one launch (start us, length us, event | category | flops | bytes accessed | tf_op | source)
XLA Modules:
  0.0 63.8 jit_solution(13948254648459270813)
XLA Ops:
  1.3 36.9 %exchange.1 = (f32[2,3,16,1024]{3,2,1,0:T(8,128)}, f32[16,2,3,8,128]{4,3,2,1,0:T(8,128)}, f32[8,32,128]{2,1,0:T(8,128)}, f32[256,128]{1,0:T(8,128)}, s32[128,128]{1,0:T(8,128)}) custom-call(f32[3,32,16,1024]{3,2,1,0:T(8,128)} %vel.3, f32[1,512]{1,0:T(1,128)} %bitcast.8, f32[1,512]{1,0:T(1,128)} %bitcast.9, f32[5,32]{1,0:T(8,128)} %st_h.1, ...), custom_call_target="tpu_custom_call" | custom-call | tf_op jit(solution)/shard_map/exchange/pallas_call | solution.py:428
  38.2 25.6 %local.1 = (f32[3,32,16,1024]{3,2,1,0:T(8,128)}, f32[3,32,16,1024]{3,2,1,0:T(8,128)}) custom-call(f32[3,32,16,1024]{3,2,1,0:T(8,128)} %vel.3, f32[2,3,16,1024]{3,2,1,0:T(8,128)} %get-tuple-element.7.halo_h, f32[16,2,3,8,128]{4,3,2,1,0:T(8,128)} %get-tuple-element.8.bound_h, f32[8,32,128]{2,1,0:T(8,128)} %get-tuple-element.9.coef_h, ...), custom_call_target="tpu_custom_call" | custom-call | tf_op jit(solution)/shard_map/local/pallas_call | solution.py:634

commit v4 on v3

--- a/solution.py
+++ b/solution.py
@@ -18,13 +18,25 @@
     vel, lower_h, upper_h, st_h, forces_h, owner_h, cells_h, counts_h,
     halo_h, bound, coef_h, part_h, rows_h,
     lower, upper, st, forces, owner, cells, counts, halo, coef, part_t, rows_v,
-    vbuf, send_a, recv_a, send_f, elim, pbuf, tile_out, tile_in,
+    key_row, left, right, vbuf, send_a, recv_a, send_f, elim, pbuf, tile_out, tile_in,
     pack, recv1, pack2, recv2,
     lmat, umat, dmat, cmat, ymat, zmat, wmat, wgt, red,
     isem, osem, vsem, hs, hr, ts, tr, as_, ar, fs, fr, p1s, p1r, p2s, p2r,
 ):
     me_w = lax.axis_index("wall")
     me_s = lax.axis_index("span")
+
+    def wait_all(src, dst, sent, got):
+        group = pltpu.make_async_remote_copy(
+            src_ref=src,
+            dst_ref=dst,
+            send_sem=sent.at[0],
+            recv_sem=got.at[0],
+            device_id=(me_w, me_s),
+            device_id_type=MESH,
+        )
+        group.wait_send()
+        group.wait_recv()
 
     def vcopy(c, h):
         part = (c, slice(None), pl.ds(h * 8, 8), slice(None))
@@ -58,10 +70,41 @@
             vcopy(c, h).start()
     for i in range(3, 7):
         loads[i].start()
+    for i in range(3):
+        loads[i].wait()
+    eye = lax.broadcasted_iota(jnp.int32, (RY, RY), 0) == lax.broadcasted_iota(
+        jnp.int32, (RY, RY), 1
+    )
+
+    def column(row, mask, n):
+        full = jnp.broadcast_to(row, (n, n))
+        col = jnp.sum(jnp.where(mask, full, 0.0), axis=1, keepdims=True)
+        return jnp.broadcast_to(col, (n, 128))
+
+    stc = [column(st[m : m + 1, :], eye, RY) for m in range(5)]
+    tile_out[0:1, :] = stc[0][0:1]
+    tile_out[1:2, :] = stc[1][0:1]
+    tile_out[2:3, :] = stc[4][RY - 1 : RY]
+    tile_out[3:4, :] = stc[3][RY - 1 : RY]
+    tile_out[4:8, :] = jnp.zeros((4, 128), F32)
+
     pl.semaphore_wait(barrier, NW - 1 + NS - 1)
 
     above = lax.rem(me_w + 1, NW)
     under = lax.rem(me_w + NW - 1, NW)
+
+    def tcopy(way):
+        return pltpu.make_async_remote_copy(
+            src_ref=tile_out,
+            dst_ref=tile_in.at[way],
+            send_sem=ts.at[way],
+            recv_sem=tr.at[way],
+            device_id=(above if way == 0 else under, me_s),
+            device_id_type=MESH,
+        )
+
+    tcopy(0).start()
+    tcopy(1).start()
 
     def hcopy(way):
         return pltpu.make_async_remote_copy(
@@ -76,38 +119,79 @@
     hcopy(0).start()
     hcopy(1).start()
 
-    for i in range(3):
+    for i in range(3, 7):
         loads[i].wait()
-    eye = lax.broadcasted_iota(jnp.int32, (RY, RY), 0) == lax.broadcasted_iota(
-        jnp.int32, (RY, RY), 1
-    )
-
-    def column(row, mask, n):
-        full = jnp.broadcast_to(row, (n, n))
-        col = jnp.sum(jnp.where(mask, full, 0.0), axis=1, keepdims=True)
-        return jnp.broadcast_to(col, (n, 128))
-
-    stc = [column(st[m : m + 1, :], eye, RY) for m in range(5)]
-    tile_out[0:1, :] = stc[0][0:1]
-    tile_out[1:2, :] = stc[1][0:1]
-    tile_out[2:3, :] = stc[4][RY - 1 : RY]
-    tile_out[3:4, :] = stc[3][RY - 1 : RY]
-    tile_out[4:8, :] = jnp.zeros((4, 128), F32)
-
-    def tcopy(way):
+    slots = owner.shape[1]
+    nn = (((1,), (0,)), ((), ()))
+    own = owner[...]
+    live = lax.broadcasted_iota(jnp.int32, (1, slots), 1) < counts[0]
+    wall_row = jnp.where(live, own >> 3, NW)
+    key_row[0:1, :] = jnp.where(live, (own & 7) * NW + (own >> 3), 512).astype(F32)
+    key_row[1:8, :] = jnp.zeros((7, slots), F32)
+    in_wall = lax.broadcasted_iota(jnp.int32, (NW, slots), 0) == wall_row
+    load = [forces[c : c + 1, :] for c in range(3)] + [cells[...].astype(F32)]
+    for part in range(3):
+        head = [x.astype(jnp.bfloat16).astype(F32) for x in load]
+        load = [x - y for x, y in zip(load, head)]
+        for c in range(4):
+            r0 = (part * 4 + c) * NW
+            left[r0 : r0 + NW, :] = jnp.where(in_wall, head[c], 0.0).astype(jnp.bfloat16)
+
+    lane_f = lax.broadcasted_iota(jnp.int32, (256, 128), 1).astype(F32)
+    sub_f = lax.broadcasted_iota(jnp.int32, (256, 128), 0).astype(F32)
+    lower_tri = [
+        jnp.where(lane_f + 128.0 * b < sub_f, 1.0, 0.0) for b in range(2)
+    ]
+
+    def rank_block(i, carry):
+        at = pl.ds(pl.multiple_of(i * 256, 256), 256)
+        tile = key_row[:, at]
+        col = jnp.broadcast_to(tile.T[:, 0:1], (256, 128))
+        hit = col == lane_f
+        score = jnp.where(hit, carry, 0.0)
+        for b in range(2):
+            same = col == tile[0:1, b * 128 : b * 128 + 128]
+            score = score + jnp.where(same, lower_tri[b], 0.0)
+        rank = jnp.sum(score, axis=1, keepdims=True)
+        place = jnp.broadcast_to(
+            jnp.floor(col[:, 0:1] * (1.0 / NW)) * SLOTS + rank, (256, 128)
+        )
+        for b in range(4):
+            right[at, b * 128 : b * 128 + 128] = jnp.where(
+                place == lane_f + 128.0 * b, 1.0, 0.0
+            ).astype(jnp.bfloat16)
+        return carry + jnp.sum(jnp.where(hit, 1.0, 0.0), axis=0, keepdims=True)
+
+    lax.fori_loop(0, slots // 256, rank_block, jnp.zeros((1, 128), F32), unroll=4)
+    made = lax.dot_general(left[...], right[...], nn, preferred_element_type=F32)
+    made = made[0:64] + made[64:128] + made[128:192]
+    first = lax.broadcasted_iota(jnp.int32, (NW, 128), 1) < SLOTS
+    for k in range(NS):
+        for b in range(2):
+            pair = [
+                made[c * NW : c * NW + NW, k // 2 * 128 : k // 2 * 128 + 128]
+                for c in (2 * b, 2 * b + 1)
+            ]
+            turn = 1 - k % 2
+            pair[turn] = pltpu.roll(pair[turn], SLOTS, 1)
+            pack[b, k * NW : k * NW + NW, :] = jnp.where(first, pair[0], pair[1])
+
+    def p1copy(k):
+        to = lax.rem(me_s + k, NS)
         return pltpu.make_async_remote_copy(
-            src_ref=tile_out,
-            dst_ref=tile_in.at[way],
-            send_sem=ts.at[way],
-            recv_sem=tr.at[way],
-            device_id=(above if way == 0 else under, me_s),
+            src_ref=pack.at[:, pl.ds(pl.multiple_of(to * NW, NW), NW)],
+            dst_ref=recv1.at[:, pl.ds(pl.multiple_of(me_s * NW, NW), NW)],
+            send_sem=p1s.at[0],
+            recv_sem=p1r.at[0],
+            device_id=(me_w, to),
             device_id_type=MESH,
         )
 
-    tcopy(0).start()
-    tcopy(1).start()
-
-    nn = (((1,), (0,)), ((), ()))
+    for k in range(1, NS):
+        p1copy(k).start()
+    mine = pl.ds(pl.multiple_of(me_s * NW, NW), NW)
+    recv1[:, mine, :] = pack[:, mine, :]
+
     lane_i = lax.broadcasted_iota(jnp.int32, (RY, NW * RY), 1)
     in_row = (lane_i & (RY - 1)) == lax.broadcasted_iota(jnp.int32, (RY, NW * RY), 0)
     to_slab = (
@@ -276,8 +360,8 @@
         return pltpu.make_async_remote_copy(
             src_ref=send_a.at[to],
             dst_ref=recv_a.at[me_w],
-            send_sem=as_.at[k],
-            recv_sem=ar.at[k],
+            send_sem=as_.at[0],
+            recv_sem=ar.at[0],
             device_id=(to, me_s),
             device_id_type=MESH,
         )
@@ -286,67 +370,7 @@
         acopy(k).start()
     recv_a[me_w] = send_a[me_w]
 
-    for i in range(3, 7):
-        loads[i].wait()
-    count = counts[0]
-    pack[...] = jnp.zeros((2, NW * NS, 128), F32)
-    up_i = lax.broadcasted_iota(jnp.int32, (256, 256), 0)
-    up_j = lax.broadcasted_iota(jnp.int32, (256, 256), 1)
-    before = (up_i < up_j).astype(F32).astype(jnp.bfloat16)
-    ones = jnp.ones((256, 256), jnp.bfloat16)
-    ids = lax.broadcasted_iota(jnp.int32, (NW * NS, 256), 0)
-    ranks = lax.broadcasted_iota(jnp.int32, (SLOTS, 256), 0).astype(F32)
-    lanes = lax.broadcasted_iota(jnp.int32, (1, 256), 1)
-    nt = (((1,), (1,)), ((), ()))
-
-    def pack_block(i, carry):
-        at = pl.ds(pl.multiple_of(i * 256, 256), 256)
-        own = owner[:, at]
-        key = (own & 7) * NW + (own >> 3)
-        key = jnp.where(lanes + i * 256 < count, key, 512)
-        hit = ids == key
-        hot = jnp.where(hit, 1.0, 0.0)
-        hot_b = hot.astype(jnp.bfloat16)
-        pre = lax.dot_general(hot_b, before, nn, preferred_element_type=F32)
-        tot = lax.dot_general(hot_b, ones, nn, preferred_element_type=F32)
-        rank = jnp.sum(jnp.where(hit, pre + carry, 0.0), axis=0, keepdims=True)
-        place = ranks == rank
-        load = [forces[c : c + 1, at] for c in range(3)] + [cells[:, at].astype(F32)]
-        sums = None
-        for _part in range(3):
-            head = [x.astype(jnp.bfloat16).astype(F32) for x in load]
-            load = [x - y for x, y in zip(load, head)]
-            right = jnp.concatenate(
-                [jnp.where(place, y, 0.0) for y in head], axis=0
-            ).astype(jnp.bfloat16)
-            term = lax.dot_general(hot_b, right, nt, preferred_element_type=F32)
-            sums = term if sums is None else sums + term
-        pack[0] += sums[:, 0:128]
-        pack[1] += sums[:, 128:256]
-        return carry + tot
-
-    lax.fori_loop(
-        0, owner.shape[1] // 256, pack_block, jnp.zeros((NW * NS, 256), F32), unroll=4
-    )
-
-    def p1copy(k):
-        to = lax.rem(me_s + k, NS)
-        return pltpu.make_async_remote_copy(
-            src_ref=pack.at[:, pl.ds(pl.multiple_of(to * NW, NW), NW)],
-            dst_ref=recv1.at[:, pl.ds(pl.multiple_of(me_s * NW, NW), NW)],
-            send_sem=p1s.at[k],
-            recv_sem=p1r.at[k],
-            device_id=(me_w, to),
-            device_id_type=MESH,
-        )
-
-    for k in range(1, NS):
-        p1copy(k).start()
-    mine = pl.ds(pl.multiple_of(me_s * NW, NW), NW)
-    recv1[:, mine, :] = pack[:, mine, :]
-
-    for k in range(1, NS):
-        p1copy(k).wait()
+    wait_all(pack.at[:, pl.ds(0, NW * (NS - 1))], recv1.at[:, pl.ds(0, NW * (NS - 1))], p1s, p1r)
     for w in range(NW):
         for b in range(2):
             pack2[w, b] = recv1[b, pl.ds(w, NS, stride=NW), :]
@@ -356,8 +380,8 @@
         return pltpu.make_async_remote_copy(
             src_ref=pack2.at[to],
             dst_ref=recv2.at[me_w],
-            send_sem=p2s.at[k],
-            recv_sem=p2r.at[k],
+            send_sem=p2s.at[0],
+            recv_sem=p2r.at[0],
             device_id=(to, me_s),
             device_id_type=MESH,
         )
@@ -366,8 +390,7 @@
         p2copy(k).start()
     recv2[me_w] = pack2[me_w]
 
-    for k in range(1, NW):
-        acopy(k).wait()
+    wait_all(send_a.at[pl.ds(0, NW - 1)], recv_a.at[pl.ds(0, NW - 1)], as_, ar)
 
     p = recv_a[0, 0]
     for s in range(1, NW):
@@ -389,8 +412,8 @@
         return pltpu.make_async_remote_copy(
             src_ref=send_f.at[to],
             dst_ref=bound.at[me_w],
-            send_sem=fs.at[k],
-            recv_sem=fr.at[k],
+            send_sem=fs.at[0],
+            recv_sem=fr.at[0],
             device_id=(to, me_s),
             device_id_type=MESH,
         )
@@ -400,8 +423,7 @@
     keep_own = pltpu.make_async_copy(send_f.at[me_w], bound.at[me_w], osem.at[2])
     keep_own.start()
 
-    for k in range(1, NW):
-        p2copy(k).wait()
+    wait_all(pack2.at[pl.ds(0, NW - 1)], recv2.at[pl.ds(0, NW - 1)], p2s, p2r)
     part_t[0:128, :] = recv2[:, 0].reshape(NW * NS, 128).T
     rest = recv2[:, 1].reshape(NW * NS, 128)
     flipped = rest.T
@@ -416,8 +438,7 @@
     keep_rows = pltpu.make_async_copy(rows_v, rows_h, osem.at[4])
     keep_rows.start()
 
-    for k in range(1, NW):
-        fcopy(k).wait()
+    wait_all(send_f.at[pl.ds(0, NW - 1)], bound.at[pl.ds(0, NW - 1)], fs, fr)
     for keep in (keep_coef, keep_halo, keep_own, keep_part, keep_rows):
         keep.wait()
 
@@ -448,6 +469,9 @@
             pltpu.VMEM((8, RY, 128), F32),
             pltpu.VMEM((256, 128), F32),
             pltpu.VMEM((128, 128), jnp.int32),
+            pltpu.VMEM((8, owner.shape[1]), F32),
+            pltpu.VMEM((12 * NW, owner.shape[1]), jnp.bfloat16),
+            pltpu.VMEM((owner.shape[1], NS * SLOTS), jnp.bfloat16),
             pltpu.VMEM((3, RY, SZ, NX), F32),
             pltpu.VMEM((NW, 2, 3, 8, 128), F32),
             pltpu.VMEM((NW, 2, 3, 8, 128), F32),
@@ -470,8 +494,7 @@
             pltpu.VMEM((2, RY + 8, 128), F32),
             pltpu.VMEM((6, NW, 128), F32),
             dma((7,)), dma((5,)), dma((6,)), dma((2,)), dma((2,)), dma((2,)), dma((2,)),
-            dma((NW,)), dma((NW,)), dma((NW,)), dma((NW,)),
-            dma((NS,)), dma((NS,)), dma((NW,)), dma((NW,)),
+            *[dma((1,))] * 8,
         ],
         compiler_params=pltpu.CompilerParams(
             collective_id=0, has_side_effects=True, vmem_limit_bytes=56 << 20

time: 63.9 us -> 57.2 us (0.90)
  Pallas kernels: 62.5 us -> 55.5 us
    pallas_call x1, Pallas kernels: 36.9 us -> 30.5 us  [exchange(): pl.pallas_call(exchange_kernel, out_shape=(jax.ShapeDtypeStruct((2, 3, SZ...]
where the time goes in v4:
time: 57.2 us; the launch traced here: 56.8 us
  Pallas kernels  55.5 us (97%)
  between operations  1.29 us (2%)
    pallas_call x1, Pallas kernels, exchange(): pl.pallas_call(exchange_kernel, out_shape=(jax.ShapeDtypeStruct((2, 3, SZ...  30.5 us
    pallas_call x1, Pallas kernels, local(): pl.pallas_call(local_kernel, out_shape=(jax.ShapeDtypeStruct(whole, F32),...  25 us

profile of v4, /device:TPU:0, one launch (start us, length us, event | category | flops | bytes accessed | tf_op | source)
XLA Modules:
  0.0 56.8 jit_solution(8887192470327346225)
XLA Ops:
  1.3 30.5 %exchange.1 = (f32[2,3,16,1024]{3,2,1,0:T(8,128)}, f32[16,2,3,8,128]{4,3,2,1,0:T(8,128)}, f32[8,32,128]{2,1,0:T(8,128)}, f32[256,128]{1,0:T(8,128)}, s32[128,128]{1,0:T(8,128)}) custom-call(f32[3,32,16,1024]{3,2,1,0:T(8,128)} %vel.3, f32[1,512]{1,0:T(1,128)} %bitcast.8, f32[1,512]{1,0:T(1,128)} %bitcast.9, f32[5,32]{1,0:T(8,128)} %st_h.1, ...), custom_call_target="tpu_custom_call" | custom-call | tf_op jit(solution)/shard_map/exchange/pallas_call | solution.py:449
  31.8 25.0 %local.1 = (f32[3,32,16,1024]{3,2,1,0:T(8,128)}, f32[3,32,16,1024]{3,2,1,0:T(8,128)}) custom-call(f32[3,32,16,1024]{3,2,1,0:T(8,128)} %vel.3, f32[2,3,16,1024]{3,2,1,0:T(8,128)} %get-tuple-element.7.halo_h, f32[16,2,3,8,128]{4,3,2,1,0:T(8,128)} %get-tuple-element.8.bound_h, f32[8,32,128]{2,1,0:T(8,128)} %get-tuple-element.9.coef_h, ...), custom_call_target="tpu_custom_call" | custom-call | tf_op jit(solution)/shard_map/local/pallas_call | solution.py:657

commit v5 on v3

--- a/solution.py
+++ b/solution.py
@@ -18,13 +18,25 @@
     vel, lower_h, upper_h, st_h, forces_h, owner_h, cells_h, counts_h,
     halo_h, bound, coef_h, part_h, rows_h,
     lower, upper, st, forces, owner, cells, counts, halo, coef, part_t, rows_v,
-    vbuf, send_a, recv_a, send_f, elim, pbuf, tile_out, tile_in,
+    key_row, left, right, vbuf, send_a, recv_a, send_f, elim, pbuf, tile_out, tile_in,
     pack, recv1, pack2, recv2,
     lmat, umat, dmat, cmat, ymat, zmat, wmat, wgt, red,
     isem, osem, vsem, hs, hr, ts, tr, as_, ar, fs, fr, p1s, p1r, p2s, p2r,
 ):
     me_w = lax.axis_index("wall")
     me_s = lax.axis_index("span")
+
+    def wait_all(src, dst, sent, got, i=0):
+        group = pltpu.make_async_remote_copy(
+            src_ref=src,
+            dst_ref=dst,
+            send_sem=sent.at[i],
+            recv_sem=got.at[i],
+            device_id=(me_w, me_s),
+            device_id_type=MESH,
+        )
+        group.wait_send()
+        group.wait_recv()
 
     def vcopy(c, h):
         part = (c, slice(None), pl.ds(h * 8, 8), slice(None))
@@ -63,18 +75,18 @@
     above = lax.rem(me_w + 1, NW)
     under = lax.rem(me_w + NW - 1, NW)
 
-    def hcopy(way):
+    def hcopy(way, c):
         return pltpu.make_async_remote_copy(
-            src_ref=vel.at[:, RY - 1] if way == 0 else vel.at[:, 0],
-            dst_ref=halo.at[way],
-            send_sem=hs.at[way],
-            recv_sem=hr.at[way],
+            src_ref=vel.at[c, RY - 1 if way == 0 else 0],
+            dst_ref=halo.at[way, c],
+            send_sem=hs.at[way * 3 + c],
+            recv_sem=hr.at[way * 3 + c],
             device_id=(above if way == 0 else under, me_s),
             device_id_type=MESH,
         )
 
-    hcopy(0).start()
-    hcopy(1).start()
+    hcopy(0, 0).start()
+    hcopy(1, 0).start()
 
     for i in range(3):
         loads[i].wait()
@@ -106,6 +118,10 @@
 
     tcopy(0).start()
     tcopy(1).start()
+    for c in (1, 2):
+        hcopy(0, c).start()
+        hcopy(1, c).start()
+
 
     nn = (((1,), (0,)), ((), ()))
     lane_i = lax.broadcasted_iota(jnp.int32, (RY, NW * RY), 1)
@@ -193,17 +209,11 @@
     keep_coef = pltpu.make_async_copy(coef, coef_h, osem.at[0])
     keep_coef.start()
 
-    tcopy(0).wait()
-    tcopy(1).wait()
     for way, own, scale in ((0, z_own, low_next), (1, y_own, upp_prev)):
         wmat[...] = jnp.zeros((RY + 8, 128), F32)
         for m in range(5):
             wmat[m + 2 : m + 2 + RY, :] += kept[m] * own
         wgt[way] = wmat[...] * (-scale)
-    wgt[0, RY + 2 : RY + 3, :] += tile_in[1, 0:1, :]
-    wgt[0, RY + 3 : RY + 4, :] += tile_in[1, 1:2, :]
-    wgt[1, 5:6, :] += tile_in[0, 2:3, :]
-    wgt[1, 4:5, :] += tile_in[0, 3:4, :]
 
     eye16 = lax.broadcasted_iota(jnp.int32, (NW, NW), 0) == lax.broadcasted_iota(
         jnp.int32, (NW, NW), 1
@@ -234,7 +244,7 @@
         red[5, s : s + 1, :] = q
         q = red[1, s : s + 1, :] * q * c3 - lz1[s : s + 1]
 
-    for c in range(3):
+    def own_rows(c):
         for h in range(2):
             vcopy(c, h).wait()
 
@@ -251,91 +261,130 @@
                         up[b] = wu * u if j == 0 else up[b] + wu * u
                         down[b] = wd * u if j == 0 else down[b] + wd * u
                 for b in range(4):
-                    send_a[h * 8 + x * 4 + b, 0, c] = up[b]
-                    send_a[h * 8 + x * 4 + b, 1, c] = down[b]
-
-    hcopy(0).wait()
-    hcopy(1).wait()
-    keep_halo = pltpu.make_async_copy(halo, halo_h, osem.at[1])
-    keep_halo.start()
-    for h in range(2):
-
-        @pl.loop(0, 8)
-        def _(x):
-            cols = pl.ds(pl.multiple_of(x * 128, 128), 128)
-            for c in range(3):
-                lo = halo[0, c, h * 8 : h * 8 + 8, cols]
-                hi = halo[1, c, h * 8 : h * 8 + 8, cols]
-                for way in range(2):
-                    send_a[h * 8 + x, way, c] += (
-                        wgt[way, 3:4, :] * lo + wgt[way, RY + 4 : RY + 5, :] * hi
-                    )
-
-    def acopy(k):
+                    send_a[c, h * 8 + x * 4 + b, 0] = up[b]
+                    send_a[c, h * 8 + x * 4 + b, 1] = down[b]
+
+    def acopy(c, k):
         to = lax.rem(me_w + k, NW)
         return pltpu.make_async_remote_copy(
-            src_ref=send_a.at[to],
-            dst_ref=recv_a.at[me_w],
-            send_sem=as_.at[k],
-            recv_sem=ar.at[k],
+            src_ref=send_a.at[c, to],
+            dst_ref=recv_a.at[c, me_w],
+            send_sem=as_.at[c],
+            recv_sem=ar.at[c],
             device_id=(to, me_s),
             device_id_type=MESH,
         )
 
-    for k in range(1, NW):
-        acopy(k).start()
-    recv_a[me_w] = send_a[me_w]
+    def add_ends(c):
+        for h in range(2):
+            cells8 = slice(h * 8, h * 8 + 8)
+
+            @pl.loop(0, 8)
+            def _(x):
+                cols = pl.ds(pl.multiple_of(x * 128, 128), 128)
+                ends = (halo[0, c, cells8, cols], halo[1, c, cells8, cols])
+                near = (
+                    (tile_in[1, 0:1, :], RY - 2, tile_in[1, 1:2, :], RY - 1),
+                    (tile_in[0, 2:3, :], 1, tile_in[0, 3:4, :], 0),
+                )
+                for way in range(2):
+                    wa, ja, wb, jb = near[way]
+                    send_a[c, h * 8 + x, way] += (
+                        wgt[way, 3:4, :] * ends[0]
+                        + wgt[way, RY + 4 : RY + 5, :] * ends[1]
+                        + wa * vbuf[c, ja, cells8, cols]
+                        + wb * vbuf[c, jb, cells8, cols]
+                    )
+
+    def send_up(c):
+        hcopy(0, c).wait()
+        hcopy(1, c).wait()
+        add_ends(c)
+        for k in range(1, NW):
+            acopy(c, k).start()
+        recv_a[c, me_w] = send_a[c, me_w]
+
+    own_rows(0)
+    own_rows(1)
+    own_rows(2)
 
     for i in range(3, 7):
         loads[i].wait()
-    count = counts[0]
-    pack[...] = jnp.zeros((2, NW * NS, 128), F32)
-    up_i = lax.broadcasted_iota(jnp.int32, (256, 256), 0)
-    up_j = lax.broadcasted_iota(jnp.int32, (256, 256), 1)
-    before = (up_i < up_j).astype(F32).astype(jnp.bfloat16)
-    ones = jnp.ones((256, 256), jnp.bfloat16)
-    ids = lax.broadcasted_iota(jnp.int32, (NW * NS, 256), 0)
-    ranks = lax.broadcasted_iota(jnp.int32, (SLOTS, 256), 0).astype(F32)
-    lanes = lax.broadcasted_iota(jnp.int32, (1, 256), 1)
-    nt = (((1,), (1,)), ((), ()))
-
-    def pack_block(i, carry):
+    slots = owner.shape[1]
+    own = owner[...]
+    live = lax.broadcasted_iota(jnp.int32, (1, slots), 1) < counts[0]
+    wall_row = jnp.where(live, own >> 3, NW)
+    key_row[0:1, :] = jnp.where(live, (own & 7) * NW + (own >> 3), 512).astype(F32)
+    key_row[1:8, :] = jnp.zeros((7, slots), F32)
+    lane_f = lax.broadcasted_iota(jnp.int32, (256, 128), 1).astype(F32)
+    sub_f = lax.broadcasted_iota(jnp.int32, (256, 128), 0).astype(F32)
+    lower_tri = [
+        jnp.where(lane_f + 128.0 * b < sub_f, 1.0, 0.0) for b in range(2)
+    ]
+
+    ones = jnp.ones((128, 128), jnp.bfloat16)
+    head_row = jnp.where(
+        lax.broadcasted_iota(jnp.int32, (8, 128), 0) == 0, 1.0, 0.0
+    ).astype(jnp.bfloat16)
+
+    def rank_block(i, carry):
         at = pl.ds(pl.multiple_of(i * 256, 256), 256)
-        own = owner[:, at]
-        key = (own & 7) * NW + (own >> 3)
-        key = jnp.where(lanes + i * 256 < count, key, 512)
-        hit = ids == key
-        hot = jnp.where(hit, 1.0, 0.0)
-        hot_b = hot.astype(jnp.bfloat16)
-        pre = lax.dot_general(hot_b, before, nn, preferred_element_type=F32)
-        tot = lax.dot_general(hot_b, ones, nn, preferred_element_type=F32)
-        rank = jnp.sum(jnp.where(hit, pre + carry, 0.0), axis=0, keepdims=True)
-        place = ranks == rank
-        load = [forces[c : c + 1, at] for c in range(3)] + [cells[:, at].astype(F32)]
-        sums = None
-        for _part in range(3):
-            head = [x.astype(jnp.bfloat16).astype(F32) for x in load]
-            load = [x - y for x, y in zip(load, head)]
-            right = jnp.concatenate(
-                [jnp.where(place, y, 0.0) for y in head], axis=0
+        tile = key_row[:, at]
+        col = lax.dot_general(
+            tile.T.astype(jnp.bfloat16), head_row, nn, preferred_element_type=F32
+        )
+        hit = col == lane_f
+        score = jnp.where(hit, carry, 0.0)
+        for b in range(2):
+            same = col == tile[0:1, b * 128 : b * 128 + 128]
+            score = score + jnp.where(same, lower_tri[b], 0.0)
+        rank = lax.dot_general(
+            score.astype(jnp.bfloat16), ones, nn, preferred_element_type=F32
+        )
+        place = jnp.floor(col * (1.0 / NW)) * SLOTS + rank
+        for b in range(4):
+            right[at, b * 128 : b * 128 + 128] = jnp.where(
+                place == lane_f + 128.0 * b, 1.0, 0.0
             ).astype(jnp.bfloat16)
-            term = lax.dot_general(hot_b, right, nt, preferred_element_type=F32)
-            sums = term if sums is None else sums + term
-        pack[0] += sums[:, 0:128]
-        pack[1] += sums[:, 128:256]
-        return carry + tot
-
-    lax.fori_loop(
-        0, owner.shape[1] // 256, pack_block, jnp.zeros((NW * NS, 256), F32), unroll=4
-    )
+        return carry + jnp.sum(jnp.where(hit, 1.0, 0.0), axis=0, keepdims=True)
+
+    blocks = slots // 256
+    carry = lax.fori_loop(
+        0, blocks // 2, rank_block, jnp.zeros((1, 128), F32), unroll=4
+    )
+    tcopy(0).wait()
+    tcopy(1).wait()
+    send_up(0)
+    lax.fori_loop(blocks // 2, blocks, rank_block, carry, unroll=4)
+    in_wall = lax.broadcasted_iota(jnp.int32, (NW, slots), 0) == wall_row
+    load = [forces[c : c + 1, :] for c in range(3)] + [cells[...].astype(F32)]
+    for part in range(3):
+        head = [x.astype(jnp.bfloat16).astype(F32) for x in load]
+        load = [x - y for x, y in zip(load, head)]
+        for c in range(4):
+            r0 = (part * 4 + c) * NW
+            left[r0 : r0 + NW, :] = jnp.where(in_wall, head[c], 0.0).astype(jnp.bfloat16)
+
+    made = lax.dot_general(left[...], right[...], nn, preferred_element_type=F32)
+    made = made[0:64] + made[64:128] + made[128:192]
+    first = lax.broadcasted_iota(jnp.int32, (NW, 128), 1) < SLOTS
+    for k in range(NS):
+        for b in range(2):
+            pair = [
+                made[c * NW : c * NW + NW, k // 2 * 128 : k // 2 * 128 + 128]
+                for c in (2 * b, 2 * b + 1)
+            ]
+            turn = 1 - k % 2
+            pair[turn] = pltpu.roll(pair[turn], SLOTS, 1)
+            pack[b, k * NW : k * NW + NW, :] = jnp.where(first, pair[0], pair[1])
 
     def p1copy(k):
         to = lax.rem(me_s + k, NS)
         return pltpu.make_async_remote_copy(
             src_ref=pack.at[:, pl.ds(pl.multiple_of(to * NW, NW), NW)],
             dst_ref=recv1.at[:, pl.ds(pl.multiple_of(me_s * NW, NW), NW)],
-            send_sem=p1s.at[k],
-            recv_sem=p1r.at[k],
+            send_sem=p1s.at[0],
+            recv_sem=p1r.at[0],
             device_id=(me_w, to),
             device_id_type=MESH,
         )
@@ -345,8 +394,45 @@
     mine = pl.ds(pl.multiple_of(me_s * NW, NW), NW)
     recv1[:, mine, :] = pack[:, mine, :]
 
-    for k in range(1, NS):
-        p1copy(k).wait()
+    send_up(1)
+    send_up(2)
+    keep_halo = pltpu.make_async_copy(halo, halo_h, osem.at[1])
+    keep_halo.start()
+
+    def solve(c):
+        wait_all(send_a.at[c, pl.ds(0, NW - 1)], recv_a.at[c, pl.ds(0, NW - 1)], as_, ar, c)
+        p = recv_a[c, 0, 0]
+        for s in range(1, NW):
+            pbuf[s] = p
+            e = recv_a[c, s, 1] - red[0, s : s + 1, :] * p
+            elim[s] = e
+            if s < NW - 1:
+                p = recv_a[c, s, 0] - red[1, s : s + 1, :] * (
+                    p + red[2, s : s + 1, :] * e
+                )
+        down = jnp.zeros((8, 128), F32)
+        send_f[c, NW - 1, 1] = down
+        for s in range(NW - 1, 0, -1):
+            down = red[3, s : s + 1, :] * elim[s] - red[4, s : s + 1, :] * down
+            send_f[c, s - 1, 1] = down
+            send_f[c, s, 0] = pbuf[s] + red[5, s : s + 1, :] * down
+        send_f[c, 0, 0] = jnp.zeros((8, 128), F32)
+        for k in range(1, NW):
+            fcopy(c, k).start()
+
+    def fcopy(c, k):
+        to = lax.rem(me_w + k, NW)
+        return pltpu.make_async_remote_copy(
+            src_ref=send_f.at[c, to],
+            dst_ref=bound.at[c, me_w],
+            send_sem=fs.at[c],
+            recv_sem=fr.at[c],
+            device_id=(to, me_s),
+            device_id_type=MESH,
+        )
+
+    solve(0)
+    wait_all(pack.at[:, pl.ds(0, NW * (NS - 1))], recv1.at[:, pl.ds(0, NW * (NS - 1))], p1s, p1r)
     for w in range(NW):
         for b in range(2):
             pack2[w, b] = recv1[b, pl.ds(w, NS, stride=NW), :]
@@ -356,8 +442,8 @@
         return pltpu.make_async_remote_copy(
             src_ref=pack2.at[to],
             dst_ref=recv2.at[me_w],
-            send_sem=p2s.at[k],
-            recv_sem=p2r.at[k],
+            send_sem=p2s.at[0],
+            recv_sem=p2r.at[0],
             device_id=(to, me_s),
             device_id_type=MESH,
         )
@@ -366,42 +452,12 @@
         p2copy(k).start()
     recv2[me_w] = pack2[me_w]
 
-    for k in range(1, NW):
-        acopy(k).wait()
-
-    p = recv_a[0, 0]
-    for s in range(1, NW):
-        pbuf[s] = p
-        e = recv_a[s, 1] - red[0, s : s + 1, :] * p
-        elim[s] = e
-        if s < NW - 1:
-            p = recv_a[s, 0] - red[1, s : s + 1, :] * (p + red[2, s : s + 1, :] * e)
-    down = jnp.zeros((3, 8, 128), F32)
-    send_f[NW - 1, 1] = down
-    for s in range(NW - 1, 0, -1):
-        down = red[3, s : s + 1, :] * elim[s] - red[4, s : s + 1, :] * down
-        send_f[s - 1, 1] = down
-        send_f[s, 0] = pbuf[s] + red[5, s : s + 1, :] * down
-    send_f[0, 0] = jnp.zeros((3, 8, 128), F32)
-
-    def fcopy(k):
-        to = lax.rem(me_w + k, NW)
-        return pltpu.make_async_remote_copy(
-            src_ref=send_f.at[to],
-            dst_ref=bound.at[me_w],
-            send_sem=fs.at[k],
-            recv_sem=fr.at[k],
-            device_id=(to, me_s),
-            device_id_type=MESH,
-        )
-
-    for k in range(1, NW):
-        fcopy(k).start()
-    keep_own = pltpu.make_async_copy(send_f.at[me_w], bound.at[me_w], osem.at[2])
+    solve(1)
+    solve(2)
+    keep_own = pltpu.make_async_copy(send_f.at[:, me_w], bound.at[:, me_w], osem.at[2])
     keep_own.start()
 
-    for k in range(1, NW):
-        p2copy(k).wait()
+    wait_all(pack2.at[pl.ds(0, NW - 1)], recv2.at[pl.ds(0, NW - 1)], p2s, p2r)
     part_t[0:128, :] = recv2[:, 0].reshape(NW * NS, 128).T
     rest = recv2[:, 1].reshape(NW * NS, 128)
     flipped = rest.T
@@ -416,8 +472,8 @@
     keep_rows = pltpu.make_async_copy(rows_v, rows_h, osem.at[4])
     keep_rows.start()
 
-    for k in range(1, NW):
-        fcopy(k).wait()
+    for c in range(3):
+        wait_all(send_f.at[c, pl.ds(0, NW - 1)], bound.at[c, pl.ds(0, NW - 1)], fs, fr, c)
     for keep in (keep_coef, keep_halo, keep_own, keep_part, keep_rows):
         keep.wait()
 
@@ -429,7 +485,7 @@
         exchange_kernel,
         out_shape=(
             jax.ShapeDtypeStruct((2, 3, SZ, NX), F32),
-            jax.ShapeDtypeStruct((NW, 2, 3, 8, 128), F32),
+            jax.ShapeDtypeStruct((3, NW, 2, 8, 128), F32),
             jax.ShapeDtypeStruct((8, RY, 128), F32),
             jax.ShapeDtypeStruct((256, 128), F32),
             jax.ShapeDtypeStruct((128, 128), jnp.int32),
@@ -448,12 +504,15 @@
             pltpu.VMEM((8, RY, 128), F32),
             pltpu.VMEM((256, 128), F32),
             pltpu.VMEM((128, 128), jnp.int32),
+            pltpu.VMEM((8, owner.shape[1]), F32),
+            pltpu.VMEM((12 * NW, owner.shape[1]), jnp.bfloat16),
+            pltpu.VMEM((owner.shape[1], NS * SLOTS), jnp.bfloat16),
             pltpu.VMEM((3, RY, SZ, NX), F32),
-            pltpu.VMEM((NW, 2, 3, 8, 128), F32),
-            pltpu.VMEM((NW, 2, 3, 8, 128), F32),
-            pltpu.VMEM((NW, 2, 3, 8, 128), F32),
-            pltpu.VMEM((NW, 3, 8, 128), F32),
-            pltpu.VMEM((NW, 3, 8, 128), F32),
+            pltpu.VMEM((3, NW, 2, 8, 128), F32),
+            pltpu.VMEM((3, NW, 2, 8, 128), F32),
+            pltpu.VMEM((3, NW, 2, 8, 128), F32),
+            pltpu.VMEM((NW, 8, 128), F32),
+            pltpu.VMEM((NW, 8, 128), F32),
             pltpu.VMEM((8, 128), F32),
             pltpu.VMEM((2, 8, 128), F32),
             pltpu.VMEM((2, NW * NS, 128), F32),
@@ -469,9 +528,8 @@
             pltpu.VMEM((RY + 8, 128), F32),
             pltpu.VMEM((2, RY + 8, 128), F32),
             pltpu.VMEM((6, NW, 128), F32),
-            dma((7,)), dma((5,)), dma((6,)), dma((2,)), dma((2,)), dma((2,)), dma((2,)),
-            dma((NW,)), dma((NW,)), dma((NW,)), dma((NW,)),
-            dma((NS,)), dma((NS,)), dma((NW,)), dma((NW,)),
+            dma((7,)), dma((5,)), dma((6,)), dma((6,)), dma((6,)), dma((2,)), dma((2,)),
+            *[dma((3,))] * 4, *[dma((1,))] * 4,
         ],
         compiler_params=pltpu.CompilerParams(
             collective_id=0, has_side_effects=True, vmem_limit_bytes=56 << 20
@@ -486,8 +544,9 @@
     halo, bound, coef, part_t, rows,
     acc0, acc1, acc2, acc3, even, odd, mixed, vbuf, stage, isem, vsem, dsem, fsem,
 ):
-    def take(c):
-        return pltpu.make_async_copy(vel.at[c], vbuf.at[c], vsem.at[c])
+    def take(c, x):
+        part = (c, slice(None), slice(None), pl.ds(pl.multiple_of(x * 512, 512), 512))
+        return pltpu.make_async_copy(vel.at[part], vbuf.at[part], vsem.at[c * 2 + x])
 
     staged = ((coef_h, coef), (bound_h, bound), (halo_h, halo), (part_h, part_t), (rows_h, rows))
     loads = [
@@ -496,71 +555,19 @@
     for i in range(3):
         loads[i].start()
     for c in range(3):
-        take(c).start()
+        for half in range(2):
+            take(c, half).start()
     loads[3].start()
     loads[4].start()
 
     accs = (acc0, acc1, acc2, acc3)
-    zeros = jnp.zeros((128, 128), F32)
+    depth = acc0.shape[0]
 
     @pl.loop(0, 128)
     def _(i):
-        at = pl.ds(pl.multiple_of(i * 128, 128), 128)
+        at = pl.ds(pl.multiple_of(i * (depth // 128), depth // 128), depth // 128)
         for acc in accs:
-            acc[at, :] = zeros
-
-    def put_d(c, x):
-        part = (c, slice(None), slice(None), pl.ds(x * 512, 512))
-        return pltpu.make_async_copy(vbuf.at[part], derivative.at[part], dsem.at[c * 2 + x])
-
-    for i in range(3):
-        loads[i].wait()
-    for c in range(3):
-        take(c).wait()
-        for half in range(2):
-
-            @pl.loop(0, 4)
-            def _(xx):
-                x = half * 4 + xx
-                cols = pl.ds(pl.multiple_of(x * 128, 128), 128)
-
-                def row(i):
-                    if i < -1 or i > RY:
-                        return None
-                    if i == -1:
-                        return halo[0, c, :, cols]
-                    if i == RY:
-                        return halo[1, c, :, cols]
-                    return vbuf[c, i, :, cols]
-
-                def edge(way):
-                    return jnp.concatenate([bound[x, way, c], bound[8 + x, way, c]], axis=0)
-
-                window = [row(i) for i in range(-2, 3)]
-                prev = None
-                for j in range(RY):
-                    total = None
-                    for m in range(5):
-                        if window[m] is None or j + m - 2 == -1 and j == 0:
-                            continue
-                        if j + m - 2 == RY and j == RY - 1:
-                            continue
-                        term = coef[m, j : j + 1, :] * window[m]
-                        total = term if total is None else total + term
-                    if j == 0:
-                        total = total + coef[7, 0:1, :] * edge(0)
-                    if j == RY - 1:
-                        total = total + coef[7, RY - 1 : RY, :] * edge(1)
-                    if j > 0:
-                        total = total - coef[5, j : j + 1, :] * prev
-                    prev = total
-                    window = window[1:] + [row(j + 3)]
-                    vbuf[c, j, :, cols] = total
-                for j in range(RY - 2, -1, -1):
-                    prev = vbuf[c, j, :, cols] - coef[6, j : j + 1, :] * prev
-                    vbuf[c, j, :, cols] = prev
-
-            put_d(c, half).start()
+            acc[at, :] = jnp.zeros((depth // 128, 128), F32)
 
     lane = lax.broadcasted_iota(jnp.int32, (8, 128), 1).astype(F32)
 
@@ -574,11 +581,25 @@
                 f = jnp.take_along_axis(part_t[r0 : r0 + 8, :], pick, axis=1)
                 to[pl.ds(g * 32 + c, 8, stride=4), :] = jnp.where(hit, f, 0.0)
 
-    def add(source, frm):
+    group = 2
+
+    def add(source, frm, steps):
         base = source * 128 + SLOTS
-        for r in range(SLOTS):
-            at = pl.ds(pl.multiple_of(rows[base + r], 4), 4)
-            accs[r % 4][at, :] += frm[r * 4 : r * 4 + 4, :]
+        for r0 in range(0, SLOTS, 4 * group):
+            for k in range(4):
+                slots = [r0 + k + 4 * g for g in range(group)]
+                first = [rows[base + r] for r in slots]
+                at = [pl.ds(pl.multiple_of(f, 4), 4) for f in first]
+                value = [frm[r * 4 : r * 4 + 4, :] for r in slots]
+                held = [accs[k][a, :] for a in at]
+                for g in range(group):
+                    held[g] = held[g] + value[g]
+                    for e in range(g):
+                        held[g] = held[g] + jnp.where(first[e] == first[g], value[e], 0.0)
+                for g in range(group):
+                    accs[k][at[g], :] = held[g]
+                for _step in range(group // 2):
+                    next(steps, None)
 
     even[...] = jnp.zeros((256, 128), F32)
     odd[...] = jnp.zeros((256, 128), F32)
@@ -586,12 +607,73 @@
     loads[4].wait()
     spread(0, even)
 
-    @pl.loop(0, 64)
+    def put_d(c, x):
+        part = (c, slice(None), slice(None), pl.ds(pl.multiple_of(x * 512, 512), 512))
+        return pltpu.make_async_copy(vbuf.at[part], derivative.at[part], dsem.at[c * 2 + x])
+
+    def sweep_steps(c, h, x):
+        here = (pl.ds(pl.multiple_of(h * 8, 8), 8), pl.ds(pl.multiple_of(x * 128, 128), 128))
+
+        def row(i):
+            if i < -1 or i > RY:
+                return None
+            if i == -1:
+                return halo[0, c, *here]
+            if i == RY:
+                return halo[1, c, *here]
+            return vbuf[c, i, *here]
+
+        window = [row(i) for i in range(-2, 3)]
+        prev = None
+        for j in range(RY):
+            total = None
+            for m in range(5):
+                if window[m] is None or j + m - 2 == -1 and j == 0:
+                    continue
+                if j + m - 2 == RY and j == RY - 1:
+                    continue
+                term = coef[m, j : j + 1, :] * window[m]
+                total = term if total is None else total + term
+            if j == 0:
+                total = total + coef[7, 0:1, :] * bound[c, h * 8 + x, 0]
+            if j == RY - 1:
+                total = total + coef[7, RY - 1 : RY, :] * bound[c, h * 8 + x, 1]
+            if j > 0:
+                total = total - coef[5, j : j + 1, :] * prev
+            prev = total
+            window = window[1:] + [row(j + 3)]
+            vbuf[c, j, *here] = total
+            yield
+        for j in range(RY - 2, -1, -1):
+            prev = vbuf[c, j, *here] - coef[6, j : j + 1, :] * prev
+            vbuf[c, j, *here] = prev
+            yield
+
+    def scatter_pair(i, steps):
+        spread(2 * i + 1, odd)
+        add(2 * i, even, steps)
+        spread(jnp.minimum(2 * i + 2, 127), even)
+        add(2 * i + 1, odd, steps)
+        for _rest in steps:
+            pass
+
+    for i in range(3):
+        loads[i].wait()
+
+    @pl.loop(0, 6)
+    def _(q):
+        c, half = q // 2, q % 2
+        take(c, half).wait()
+
+        @pl.loop(0, 8)
+        def _(t):
+            scatter_pair(q * 8 + t, sweep_steps(c, t // 4, half * 4 + t % 4))
+
+        put_d(c, half).start()
+
+    @pl.loop(48, 64)
     def _(i):
-        spread(2 * i + 1, odd)
-        add(2 * i, even)
-        spread(jnp.minimum(2 * i + 2, 127), even)
-        add(2 * i + 1, odd)
+        scatter_pair(i, iter(()))
 
     def put_f(b):
         part = (slice(None), pl.ds(b * 4, 4))
@@ -646,7 +728,7 @@
         + [pltpu.VMEM((depth, 128), F32)] * 4
         + [pltpu.VMEM((256, 128), F32)] * 3
         + [pltpu.VMEM(whole, F32)] * 2
-        + [pltpu.SemaphoreType.DMA((n,)) for n in (5, 3, 6, 8)],
+        + [pltpu.SemaphoreType.DMA((n,)) for n in (5, 6, 6, 8)],
         compiler_params=pltpu.CompilerParams(vmem_limit_bytes=58 << 20),
         name="local",
     )(vel, halo, bound, coef, part_t, rows, inv_vol)

time: 63.9 us -> 55 us (0.86)
  Pallas kernels: 62.5 us -> 53.6 us
    pallas_call x1, Pallas kernels: 36.9 us -> 29 us  [exchange(): pl.pallas_call(exchange_kernel, out_shape=(jax.ShapeDtypeStruct((2, 3, SZ...]
    pallas_call x1, Pallas kernels: 25.6 us -> 24.5 us  [local(): pl.pallas_call(local_kernel, out_shape=(jax.ShapeDtypeStruct(whole, F32),...]
where the time goes in v5:
time: 55 us; the launch traced here: 54.8 us
  Pallas kernels  53.6 us (97%)
  between operations  1.29 us (2%)
    pallas_call x1, Pallas kernels, exchange(): pl.pallas_call(exchange_kernel, out_shape=(jax.ShapeDtypeStruct((2, 3, SZ...  29 us
    pallas_call x1, Pallas kernels, local(): pl.pallas_call(local_kernel, out_shape=(jax.ShapeDtypeStruct(whole, F32),...  24.5 us

profile of v5, /device:TPU:0, one launch (start us, length us, event | category | flops | bytes accessed | tf_op | source)
XLA Modules:
  0.0 54.8 jit_solution(18131338181044226)
XLA Ops:
  1.3 29.0 %exchange.1 = (f32[2,3,16,1024]{3,2,1,0:T(8,128)}, f32[3,16,2,8,128]{4,3,2,1,0:T(8,128)}, f32[8,32,128]{2,1,0:T(8,128)}, f32[256,128]{1,0:T(8,128)}, s32[128,128]{1,0:T(8,128)}) custom-call(f32[3,32,16,1024]{3,2,1,0:T(8,128)} %vel.3, f32[1,512]{1,0:T(1,128)} %bitcast.8, f32[1,512]{1,0:T(1,128)} %bitcast.9, f32[5,32]{1,0:T(8,128)} %st_h.1, ...), custom_call_target="tpu_custom_call" | custom-call | tf_op jit(solution)/shard_map/exchange/pallas_call | solution.py:484
  30.3 24.5 %local.1 = (f32[3,32,16,1024]{3,2,1,0:T(8,128)}, f32[3,32,16,1024]{3,2,1,0:T(8,128)}) custom-call(f32[3,32,16,1024]{3,2,1,0:T(8,128)} %vel.3, f32[2,3,16,1024]{3,2,1,0:T(8,128)} %get-tuple-element.7.halo_h, f32[3,16,2,8,128]{4,3,2,1,0:T(8,128)} %get-tuple-element.8.bound_h, f32[8,32,128]{2,1,0:T(8,128)} %get-tuple-element.9.coef_h, ...), custom_call_target="tpu_custom_call" | custom-call | tf_op jit(solution)/shard_map/local/pallas_call | solution.py:716

commit v6 on v5

--- a/solution.py
+++ b/solution.py
@@ -16,12 +16,12 @@
 
 def exchange_kernel(
     vel, lower_h, upper_h, st_h, forces_h, owner_h, cells_h, counts_h,
-    halo_h, bound, coef_h, part_h, rows_h,
-    lower, upper, st, forces, owner, cells, counts, halo, coef, part_t, rows_v,
+    base_h, bound, edge_h, part_h, rows_h,
+    lower, upper, st, forces, owner, cells, counts, halo, coef, edge, part_t, rows_v,
     key_row, left, right, vbuf, send_a, recv_a, send_f, elim, pbuf, tile_out, tile_in,
     pack, recv1, pack2, recv2,
-    lmat, umat, dmat, cmat, ymat, zmat, wmat, wgt, red,
-    isem, osem, vsem, hs, hr, ts, tr, as_, ar, fs, fr, p1s, p1r, p2s, p2r,
+    lmat, umat, dmat, cmat, ymat, zmat, first_col, last_col, wmat, wgt, red,
+    isem, osem, bsem, vsem, hs, hr, ts, tr, as_, ar, fs, fr, p1s, p1r, p2s, p2r,
 ):
     me_w = lax.axis_index("wall")
     me_s = lax.axis_index("span")
@@ -172,6 +172,16 @@
     for j in range(RY - 2, -1, -1):
         z = -(lmat[j + 1 : j + 2, :] * dmat[j : j + 1, :]) * z
         zmat[j : j + 1, :] = z
+    v = binv[0]
+    first_col[0:1, :] = v
+    for j in range(1, RY):
+        v = -(lmat[j : j + 1, :] * binv[j]) * v
+        first_col[j : j + 1, :] = v
+    v = dmat[RY - 1 : RY, :]
+    last_col[RY - 1 : RY, :] = v
+    for j in range(RY - 2, -1, -1):
+        v = -cmat[j : j + 1, :] * v
+        last_col[j : j + 1, :] = v
 
     lane16 = lax.broadcasted_iota(jnp.int32, (RY, 128), 1)
 
@@ -205,8 +215,9 @@
         coef[m] = kept[m] * inv_own
     coef[5] = jnp.where(row_i == 0, 0.0, low_own * inv_own)
     coef[6] = c_own
-    coef[7] = inv_own
-    keep_coef = pltpu.make_async_copy(coef, coef_h, osem.at[0])
+    edge[0] = at_slab(first_col[...], me_w)
+    edge[1] = at_slab(last_col[...], me_w)
+    keep_coef = pltpu.make_async_copy(edge, edge_h, osem.at[0])
     keep_coef.start()
 
     for way, own, scale in ((0, z_own, low_next), (1, y_own, upp_prev)):
@@ -355,7 +366,6 @@
     tcopy(0).wait()
     tcopy(1).wait()
     send_up(0)
-    lax.fori_loop(blocks // 2, blocks, rank_block, carry, unroll=4)
     in_wall = lax.broadcasted_iota(jnp.int32, (NW, slots), 0) == wall_row
     load = [forces[c : c + 1, :] for c in range(3)] + [cells[...].astype(F32)]
     for part in range(3):
@@ -364,7 +374,10 @@
         for c in range(4):
             r0 = (part * 4 + c) * NW
             left[r0 : r0 + NW, :] = jnp.where(in_wall, head[c], 0.0).astype(jnp.bfloat16)
-
+    carry = lax.fori_loop(blocks // 2, blocks * 3 // 4, rank_block, carry, unroll=4)
+    send_up(1)
+    lax.fori_loop(blocks * 3 // 4, blocks, rank_block, carry, unroll=4)
+    send_up(2)
     made = lax.dot_general(left[...], right[...], nn, preferred_element_type=F32)
     made = made[0:64] + made[64:128] + made[128:192]
     first = lax.broadcasted_iota(jnp.int32, (NW, 128), 1) < SLOTS
@@ -393,11 +406,6 @@
         p1copy(k).start()
     mine = pl.ds(pl.multiple_of(me_s * NW, NW), NW)
     recv1[:, mine, :] = pack[:, mine, :]
-
-    send_up(1)
-    send_up(2)
-    keep_halo = pltpu.make_async_copy(halo, halo_h, osem.at[1])
-    keep_halo.start()
 
     def solve(c):
         wait_all(send_a.at[c, pl.ds(0, NW - 1)], recv_a.at[c, pl.ds(0, NW - 1)], as_, ar, c)
@@ -431,7 +439,57 @@
             device_id_type=MESH,
         )
 
+    def keep_base(c):
+        return pltpu.make_async_copy(vbuf.at[c], base_h.at[c], bsem.at[c])
+
+    def particular(c):
+        @pl.loop(0, 4)
+        def _(xx):
+            tiles = range(2)
+            cols = [
+                pl.ds(pl.multiple_of(xx * 256 + t * 128, 128), 128) for t in tiles
+            ]
+
+            def row(i):
+                if i < -1 or i > RY:
+                    return None
+                if i == -1:
+                    return [halo[0, c, :, cols[t]] for t in tiles]
+                if i == RY:
+                    return [halo[1, c, :, cols[t]] for t in tiles]
+                return [vbuf[c, i, :, cols[t]] for t in tiles]
+
+            window = [row(i) for i in range(-2, 3)]
+            prev = [None, None]
+            for j in range(RY):
+                total = [None, None]
+                for m in range(5):
+                    if window[m] is None or j + m - 2 == -1 and j == 0:
+                        continue
+                    if j + m - 2 == RY and j == RY - 1:
+                        continue
+                    weight = coef[m, j : j + 1, :]
+                    for t in tiles:
+                        term = weight * window[m][t]
+                        total[t] = term if total[t] is None else total[t] + term
+                if j > 0:
+                    for t in tiles:
+                        total[t] = total[t] - coef[5, j : j + 1, :] * prev[t]
+                prev = total
+                window = window[1:] + [row(j + 3)]
+                for t in tiles:
+                    vbuf[c, j, :, cols[t]] = total[t]
+            for j in range(RY - 2, -1, -1):
+                weight = coef[6, j : j + 1, :]
+                for t in tiles:
+                    prev[t] = vbuf[c, j, :, cols[t]] - weight * prev[t]
+                    vbuf[c, j, :, cols[t]] = prev[t]
+
+        keep_base(c).start()
+
     solve(0)
+    particular(0)
+    solve(1)
     wait_all(pack.at[:, pl.ds(0, NW * (NS - 1))], recv1.at[:, pl.ds(0, NW * (NS - 1))], p1s, p1r)
     for w in range(NW):
         for b in range(2):
@@ -452,10 +510,11 @@
         p2copy(k).start()
     recv2[me_w] = pack2[me_w]
 
-    solve(1)
     solve(2)
     keep_own = pltpu.make_async_copy(send_f.at[:, me_w], bound.at[:, me_w], osem.at[2])
     keep_own.start()
+    particular(1)
+    particular(2)
 
     wait_all(pack2.at[pl.ds(0, NW - 1)], recv2.at[pl.ds(0, NW - 1)], p2s, p2r)
     part_t[0:128, :] = recv2[:, 0].reshape(NW * NS, 128).T
@@ -474,7 +533,9 @@
 
     for c in range(3):
         wait_all(send_f.at[c, pl.ds(0, NW - 1)], bound.at[c, pl.ds(0, NW - 1)], fs, fr, c)
-    for keep in (keep_coef, keep_halo, keep_own, keep_part, keep_rows):
+    for c in range(3):
+        keep_base(c).wait()
+    for keep in (keep_coef, keep_own, keep_part, keep_rows):
         keep.wait()
 
 
@@ -484,9 +545,9 @@
     return pl.pallas_call(
         exchange_kernel,
         out_shape=(
-            jax.ShapeDtypeStruct((2, 3, SZ, NX), F32),
+            jax.ShapeDtypeStruct((3, RY, SZ, NX), F32),
             jax.ShapeDtypeStruct((3, NW, 2, 8, 128), F32),
-            jax.ShapeDtypeStruct((8, RY, 128), F32),
+            jax.ShapeDtypeStruct((2, RY, 128), F32),
             jax.ShapeDtypeStruct((256, 128), F32),
             jax.ShapeDtypeStruct((128, 128), jnp.int32),
         ),
@@ -501,7 +562,8 @@
             pltpu.VMEM(cells.shape, jnp.int32),
             pltpu.SMEM((1,), jnp.int32),
             pltpu.VMEM((2, 3, SZ, NX), F32),
-            pltpu.VMEM((8, RY, 128), F32),
+            pltpu.VMEM((7, RY, 128), F32),
+            pltpu.VMEM((2, RY, 128), F32),
             pltpu.VMEM((256, 128), F32),
             pltpu.VMEM((128, 128), jnp.int32),
             pltpu.VMEM((8, owner.shape[1]), F32),
@@ -525,10 +587,12 @@
             pltpu.VMEM((RY, 128), F32),
             pltpu.VMEM((RY, 128), F32),
             pltpu.VMEM((RY, 128), F32),
+            pltpu.VMEM((RY, 128), F32),
+            pltpu.VMEM((RY, 128), F32),
             pltpu.VMEM((RY + 8, 128), F32),
             pltpu.VMEM((2, RY + 8, 128), F32),
             pltpu.VMEM((6, NW, 128), F32),
-            dma((7,)), dma((5,)), dma((6,)), dma((6,)), dma((6,)), dma((2,)), dma((2,)),
+            dma((7,)), dma((5,)), dma((3,)), dma((6,)), dma((6,)), dma((6,)), dma((2,)), dma((2,)),
             *[dma((3,))] * 4, *[dma((1,))] * 4,
         ],
         compiler_params=pltpu.CompilerParams(
@@ -539,26 +603,24 @@
 
 
 def local_kernel(
-    vel, halo_h, bound_h, coef_h, part_h, rows_h, inv_vol,
+    base, bound_h, edge_h, part_h, rows_h, inv_vol,
     derivative, forcing,
-    halo, bound, coef, part_t, rows,
+    bound, edge, part_t, rows,
     acc0, acc1, acc2, acc3, even, odd, mixed, vbuf, stage, isem, vsem, dsem, fsem,
 ):
     def take(c, x):
         part = (c, slice(None), slice(None), pl.ds(pl.multiple_of(x * 512, 512), 512))
-        return pltpu.make_async_copy(vel.at[part], vbuf.at[part], vsem.at[c * 2 + x])
-
-    staged = ((coef_h, coef), (bound_h, bound), (halo_h, halo), (part_h, part_t), (rows_h, rows))
+        return pltpu.make_async_copy(base.at[part], vbuf.at[part], vsem.at[c * 2 + x])
+
+    staged = ((edge_h, edge), (bound_h, bound), (part_h, part_t), (rows_h, rows))
     loads = [
         pltpu.make_async_copy(src, dst, isem.at[i]) for i, (src, dst) in enumerate(staged)
     ]
-    for i in range(3):
-        loads[i].start()
+    for load in loads:
+        load.start()
     for c in range(3):
         for half in range(2):
             take(c, half).start()
-    loads[3].start()
-    loads[4].start()
 
     accs = (acc0, acc1, acc2, acc3)
     depth = acc0.shape[0]
@@ -598,55 +660,26 @@
                         held[g] = held[g] + jnp.where(first[e] == first[g], value[e], 0.0)
                 for g in range(group):
                     accs[k][at[g], :] = held[g]
-                for _step in range(group // 2):
+                if k % 2 == 1:
                     next(steps, None)
 
     even[...] = jnp.zeros((256, 128), F32)
     odd[...] = jnp.zeros((256, 128), F32)
-    loads[3].wait()
-    loads[4].wait()
+    for load in loads:
+        load.wait()
     spread(0, even)
 
     def put_d(c, x):
         part = (c, slice(None), slice(None), pl.ds(pl.multiple_of(x * 512, 512), 512))
         return pltpu.make_async_copy(vbuf.at[part], derivative.at[part], dsem.at[c * 2 + x])
 
-    def sweep_steps(c, h, x):
+    def join_steps(c, h, x):
         here = (pl.ds(pl.multiple_of(h * 8, 8), 8), pl.ds(pl.multiple_of(x * 128, 128), 128))
-
-        def row(i):
-            if i < -1 or i > RY:
-                return None
-            if i == -1:
-                return halo[0, c, *here]
-            if i == RY:
-                return halo[1, c, *here]
-            return vbuf[c, i, *here]
-
-        window = [row(i) for i in range(-2, 3)]
-        prev = None
+        under, above = bound[c, h * 8 + x, 0], bound[c, h * 8 + x, 1]
         for j in range(RY):
-            total = None
-            for m in range(5):
-                if window[m] is None or j + m - 2 == -1 and j == 0:
-                    continue
-                if j + m - 2 == RY and j == RY - 1:
-                    continue
-                term = coef[m, j : j + 1, :] * window[m]
-                total = term if total is None else total + term
-            if j == 0:
-                total = total + coef[7, 0:1, :] * bound[c, h * 8 + x, 0]
-            if j == RY - 1:
-                total = total + coef[7, RY - 1 : RY, :] * bound[c, h * 8 + x, 1]
-            if j > 0:
-                total = total - coef[5, j : j + 1, :] * prev
-            prev = total
-            window = window[1:] + [row(j + 3)]
-            vbuf[c, j, *here] = total
-            yield
-        for j in range(RY - 2, -1, -1):
-            prev = vbuf[c, j, *here] - coef[6, j : j + 1, :] * prev
-            vbuf[c, j, *here] = prev
+            vbuf[c, j, *here] = vbuf[c, j, *here] + (
+                edge[0, j : j + 1, :] * under + edge[1, j : j + 1, :] * above
+            )
             yield
 
     def scatter_pair(i, steps):
@@ -657,9 +690,6 @@
         for _rest in steps:
             pass
 
-    for i in range(3):
-        loads[i].wait()
-
     @pl.loop(0, 6)
     def _(q):
         c, half = q // 2, q % 2
@@ -667,7 +697,7 @@
 
         @pl.loop(0, 8)
         def _(t):
-            scatter_pair(q * 8 + t, sweep_steps(c, t // 4, half * 4 + t % 4))
+            scatter_pair(q * 8 + t, join_steps(c, t // 4, half * 4 + t % 4))
 
         put_d(c, half).start()
 
@@ -708,7 +738,7 @@
         put_f(b).wait()
 
 
-def local(vel, halo, bound, coef, part_t, rows, inv_vol):
+def local(base, bound, edge, part_t, rows, inv_vol):
     sm = pl.BlockSpec(memory_space=pltpu.SMEM)
     hbm = pl.BlockSpec(memory_space=pl.ANY)
     depth = RY * SZ * NX // 128 * 4
@@ -716,32 +746,29 @@
     return pl.pallas_call(
         local_kernel,
         out_shape=(jax.ShapeDtypeStruct(whole, F32), jax.ShapeDtypeStruct(whole, F32)),
-        in_specs=[hbm] * 6 + [sm],
+        in_specs=[hbm] * 5 + [sm],
         out_specs=(hbm, hbm),
         scratch_shapes=[
-            pltpu.VMEM(halo.shape, F32),
             pltpu.VMEM(bound.shape, F32),
-            pltpu.VMEM(coef.shape, F32),
+            pltpu.VMEM(edge.shape, F32),
             pltpu.VMEM(part_t.shape, F32),
             pltpu.SMEM(rows.shape, jnp.int32),
         ]
         + [pltpu.VMEM((depth, 128), F32)] * 4
         + [pltpu.VMEM((256, 128), F32)] * 3
         + [pltpu.VMEM(whole, F32)] * 2
-        + [pltpu.SemaphoreType.DMA((n,)) for n in (5, 6, 6, 8)],
+        + [pltpu.SemaphoreType.DMA((n,)) for n in (4, 6, 6, 8)],
         compiler_params=pltpu.CompilerParams(vmem_limit_bytes=58 << 20),
         name="local",
-    )(vel, halo, bound, coef, part_t, rows, inv_vol)
+    )(base, bound, edge, part_t, rows, inv_vol)
 
 
 def body(velocity, lower, upper, stencil, inv_volume, forces, owner, cells, counts):
-    halo, bound, coef, part_t, rows = exchange(
+    base, bound, edge, part_t, rows = exchange(
         velocity, lower.reshape(1, -1), upper.reshape(1, -1), stencil, forces,
         owner.reshape(1, -1), cells.reshape(1, -1), counts,
     )
-    derivative, forcing = local(
-        velocity, halo, bound, coef, part_t, rows.reshape(-1), inv_volume
-    )
+    derivative, forcing = local(base, bound, edge, part_t, rows.reshape(-1), inv_volume)
     return derivative, forcing
 
 

time: 55 us -> 51.7 us (0.940)
  Pallas kernels: 53.6 us -> 50.3 us
    pallas_call x1, Pallas kernels: 24.5 us -> 21.6 us  [local(): pl.pallas_call(local_kernel, out_shape=(jax.ShapeDtypeStruct(whole, F32),...]
where the time goes in v6:
time: 51.7 us; the launch traced here: 51.6 us
  Pallas kernels  50.3 us (97%)
  between operations  1.29 us (2%)
    pallas_call x1, Pallas kernels, exchange(): pl.pallas_call(exchange_kernel, out_shape=(jax.ShapeDtypeStruct((3, RY, S...  28.7 us
    pallas_call x1, Pallas kernels, local(): pl.pallas_call(local_kernel, out_shape=(jax.ShapeDtypeStruct(whole, F32),...  21.6 us

profile of v6, /device:TPU:0, one launch (start us, length us, event | category | flops | bytes accessed | tf_op | source)
XLA Modules:
  0.0 51.6 jit_solution(13942613458984531165)
XLA Ops:
  1.3 28.7 %exchange.1 = (f32[3,32,16,1024]{3,2,1,0:T(8,128)}, f32[3,16,2,8,128]{4,3,2,1,0:T(8,128)}, f32[2,32,128]{2,1,0:T(8,128)}, f32[256,128]{1,0:T(8,128)}, s32[128,128]{1,0:T(8,128)}) custom-call(f32[3,32,16,1024]{3,2,1,0:T(8,128)} %vel.1, f32[1,512]{1,0:T(1,128)} %bitcast.8, f32[1,512]{1,0:T(1,128)} %bitcast.9, f32[5,32]{1,0:T(8,128)} %st_h.1, ...), custom_call_target="tpu_custom_call" | custom-call | tf_op jit(solution)/shard_map/exchange/pallas_call | solution.py:545
  29.9 21.6 %local.1 = (f32[3,32,16,1024]{3,2,1,0:T(8,128)}, f32[3,32,16,1024]{3,2,1,0:T(8,128)}) custom-call(f32[3,32,16,1024]{3,2,1,0:T(8,128)} %get-tuple-element.7.base, f32[3,16,2,8,128]{4,3,2,1,0:T(8,128)} %get-tuple-element.8.bound_h, f32[2,32,128]{2,1,0:T(8,128)} %get-tuple-element.9.edge_h, f32[256,128]{1,0:T(8,128)} %get-tuple-element.10.part_h, ...), custom_call_target="tpu_custom_call" | custom-call | tf_op jit(solution)/shard_map/local/pallas_call | solution.py:746

commit v7 on v6

--- a/solution.py
+++ b/solution.py
@@ -374,10 +374,10 @@
         for c in range(4):
             r0 = (part * 4 + c) * NW
             left[r0 : r0 + NW, :] = jnp.where(in_wall, head[c], 0.0).astype(jnp.bfloat16)
+    send_up(1)
     carry = lax.fori_loop(blocks // 2, blocks * 3 // 4, rank_block, carry, unroll=4)
-    send_up(1)
+    send_up(2)
     lax.fori_loop(blocks * 3 // 4, blocks, rank_block, carry, unroll=4)
-    send_up(2)
     made = lax.dot_general(left[...], right[...], nn, preferred_element_type=F32)
     made = made[0:64] + made[64:128] + made[128:192]
     first = lax.broadcasted_iota(jnp.int32, (NW, 128), 1) < SLOTS
@@ -425,6 +425,8 @@
             send_f[c, s - 1, 1] = down
             send_f[c, s, 0] = pbuf[s] + red[5, s : s + 1, :] * down
         send_f[c, 0, 0] = jnp.zeros((8, 128), F32)
+
+    def send_down(c):
         for k in range(1, NW):
             fcopy(c, k).start()
 
@@ -487,9 +489,12 @@
 
         keep_base(c).start()
 
+    particular(0)
     solve(0)
-    particular(0)
+    send_down(0)
     solve(1)
+    send_down(1)
+    solve(2)
     wait_all(pack.at[:, pl.ds(0, NW * (NS - 1))], recv1.at[:, pl.ds(0, NW * (NS - 1))], p1s, p1r)
     for w in range(NW):
         for b in range(2):
@@ -510,7 +515,7 @@
         p2copy(k).start()
     recv2[me_w] = pack2[me_w]
 
-    solve(2)
+    send_down(2)
     keep_own = pltpu.make_async_copy(send_f.at[:, me_w], bound.at[:, me_w], osem.at[2])
     keep_own.start()
     particular(1)
@@ -706,14 +711,14 @@
         scatter_pair(i, iter(()))
 
     def put_f(b):
-        part = (slice(None), pl.ds(b * 4, 4))
+        part = (slice(None), pl.ds(b * 2, 2))
         return pltpu.make_async_copy(stage.at[part], forcing.at[part], fsem.at[b])
 
-    @pl.loop(0, 8)
+    @pl.loop(0, 16)
     def _(b):
-        @pl.loop(0, 8)
+        @pl.loop(0, 4)
         def _(jh):
-            j, h = b * 4 + jh // 2, jh % 2
+            j, h = b * 2 + jh // 2, jh % 2
             scale = -inv_vol[j]
             cells = pl.ds(pl.multiple_of(h * 8, 8), 8)
             for x in range(8):
@@ -733,7 +738,7 @@
         for half in range(2):
             put_d(c, half).wait()
 
-    @pl.loop(0, 8)
+    @pl.loop(0, 16)
     def _(b):
         put_f(b).wait()
 
@@ -757,7 +762,7 @@
         + [pltpu.VMEM((depth, 128), F32)] * 4
         + [pltpu.VMEM((256, 128), F32)] * 3
         + [pltpu.VMEM(whole, F32)] * 2
-        + [pltpu.SemaphoreType.DMA((n,)) for n in (4, 6, 6, 8)],
+        + [pltpu.SemaphoreType.DMA((n,)) for n in (4, 6, 6, 16)],
         compiler_params=pltpu.CompilerParams(vmem_limit_bytes=58 << 20),
         name="local",
     )(base, bound, edge, part_t, rows, inv_vol)

time: 51.7 us -> 52.4 us (1.014)
  no operation moved by 1% of the time
where the time goes in v7:
time: 52.4 us; the launch traced here: 52.1 us
  Pallas kernels  50.8 us (97%)
  between operations  1.29 us (2%)
    pallas_call x1, Pallas kernels, exchange(): pl.pallas_call(exchange_kernel, out_shape=(jax.ShapeDtypeStruct((3, RY, S...  29.2 us
    pallas_call x1, Pallas kernels, local(): pl.pallas_call(local_kernel, out_shape=(jax.ShapeDtypeStruct(whole, F32),...  21.6 us

profile of v7, /device:TPU:0, one launch (start us, length us, event | category | flops | bytes accessed | tf_op | source)
XLA Modules:
  0.0 52.1 jit_solution(6470233754213282710)
XLA Ops:
  1.3 29.2 %exchange.1 = (f32[3,32,16,1024]{3,2,1,0:T(8,128)}, f32[3,16,2,8,128]{4,3,2,1,0:T(8,128)}, f32[2,32,128]{2,1,0:T(8,128)}, f32[256,128]{1,0:T(8,128)}, s32[128,128]{1,0:T(8,128)}) custom-call(f32[3,32,16,1024]{3,2,1,0:T(8,128)} %vel.1, f32[1,512]{1,0:T(1,128)} %bitcast.8, f32[1,512]{1,0:T(1,128)} %bitcast.9, f32[5,32]{1,0:T(8,128)} %st_h.1, ...), custom_call_target="tpu_custom_call" | custom-call | tf_op jit(solution)/shard_map/exchange/pallas_call | solution.py:550
  30.4 21.6 %local.1 = (f32[3,32,16,1024]{3,2,1,0:T(8,128)}, f32[3,32,16,1024]{3,2,1,0:T(8,128)}) custom-call(f32[3,32,16,1024]{3,2,1,0:T(8,128)} %get-tuple-element.7.base, f32[3,16,2,8,128]{4,3,2,1,0:T(8,128)} %get-tuple-element.8.bound_h, f32[2,32,128]{2,1,0:T(8,128)} %get-tuple-element.9.edge_h, f32[256,128]{1,0:T(8,128)} %get-tuple-element.10.part_h, ...), custom_call_target="tpu_custom_call" | custom-call | tf_op jit(solution)/shard_map/local/pallas_call | solution.py:751

commit v8 on v7

--- a/solution.py
+++ b/solution.py
@@ -18,7 +18,7 @@
     vel, lower_h, upper_h, st_h, forces_h, owner_h, cells_h, counts_h,
     base_h, bound, edge_h, part_h, rows_h,
     lower, upper, st, forces, owner, cells, counts, halo, coef, edge, part_t, rows_v,
-    key_row, left, right, vbuf, send_a, recv_a, send_f, elim, pbuf, tile_out, tile_in,
+    key_row, left, right, vbuf, send_a, recv_a, send_f, land, elim, pbuf, tile_out, tile_in,
     pack, recv1, pack2, recv2,
     lmat, umat, dmat, cmat, ymat, zmat, first_col, last_col, wmat, wgt, red,
     isem, osem, bsem, vsem, hs, hr, ts, tr, as_, ar, fs, fr, p1s, p1r, p2s, p2r,
@@ -434,7 +434,7 @@
         to = lax.rem(me_w + k, NW)
         return pltpu.make_async_remote_copy(
             src_ref=send_f.at[c, to],
-            dst_ref=bound.at[c, me_w],
+            dst_ref=land.at[c, me_w] if c < 2 else bound.at[me_w],
             send_sem=fs.at[c],
             recv_sem=fr.at[c],
             device_id=(to, me_s),
@@ -487,6 +487,21 @@
                     prev[t] = vbuf[c, j, :, cols[t]] - weight * prev[t]
                     vbuf[c, j, :, cols[t]] = prev[t]
 
+    def join(c):
+        most = pl.ds(0, NW - 1)
+        wait_all(send_f.at[c, most], land.at[c, most], fs, fr, c)
+        land[c, me_w] = send_f[c, me_w]
+
+        @pl.loop(0, 8)
+        def _(x):
+            cols = pl.ds(pl.multiple_of(x * 128, 128), 128)
+            ends = [[land[c, h * 8 + x, way] for way in range(2)] for h in range(2)]
+            for j in range(RY):
+                first, last = edge[0, j : j + 1, :], edge[1, j : j + 1, :]
+                for h in range(2):
+                    here = (c, j, slice(h * 8, h * 8 + 8), cols)
+                    vbuf[here] = vbuf[here] + (first * ends[h][0] + last * ends[h][1])
+
         keep_base(c).start()
 
     particular(0)
@@ -516,10 +531,13 @@
     recv2[me_w] = pack2[me_w]
 
     send_down(2)
-    keep_own = pltpu.make_async_copy(send_f.at[:, me_w], bound.at[:, me_w], osem.at[2])
+    keep_own = pltpu.make_async_copy(send_f.at[2, me_w], bound.at[me_w], osem.at[2])
     keep_own.start()
     particular(1)
     particular(2)
+    keep_base(2).start()
+    join(0)
+    join(1)
 
     wait_all(pack2.at[pl.ds(0, NW - 1)], recv2.at[pl.ds(0, NW - 1)], p2s, p2r)
     part_t[0:128, :] = recv2[:, 0].reshape(NW * NS, 128).T
@@ -536,8 +554,7 @@
     keep_rows = pltpu.make_async_copy(rows_v, rows_h, osem.at[4])
     keep_rows.start()
 
-    for c in range(3):
-        wait_all(send_f.at[c, pl.ds(0, NW - 1)], bound.at[c, pl.ds(0, NW - 1)], fs, fr, c)
+    wait_all(send_f.at[2, pl.ds(0, NW - 1)], bound.at[pl.ds(0, NW - 1)], fs, fr, 2)
     for c in range(3):
         keep_base(c).wait()
     for keep in (keep_coef, keep_own, keep_part, keep_rows):
@@ -551,7 +568,7 @@
         exchange_kernel,
         out_shape=(
             jax.ShapeDtypeStruct((3, RY, SZ, NX), F32),
-            jax.ShapeDtypeStruct((3, NW, 2, 8, 128), F32),
+            jax.ShapeDtypeStruct((NW, 2, 8, 128), F32),
             jax.ShapeDtypeStruct((2, RY, 128), F32),
             jax.ShapeDtypeStruct((256, 128), F32),
             jax.ShapeDtypeStruct((128, 128), jnp.int32),
@@ -578,6 +595,7 @@
             pltpu.VMEM((3, NW, 2, 8, 128), F32),
             pltpu.VMEM((3, NW, 2, 8, 128), F32),
             pltpu.VMEM((3, NW, 2, 8, 128), F32),
+            pltpu.VMEM((2, NW, 2, 8, 128), F32),
             pltpu.VMEM((NW, 8, 128), F32),
             pltpu.VMEM((NW, 8, 128), F32),
             pltpu.VMEM((8, 128), F32),
@@ -611,21 +629,23 @@
     base, bound_h, edge_h, part_h, rows_h, inv_vol,
     derivative, forcing,
     bound, edge, part_t, rows,
-    acc0, acc1, acc2, acc3, even, odd, mixed, vbuf, stage, isem, vsem, dsem, fsem,
+    acc0, acc1, acc2, acc3, even, odd, mixed, vbuf, stage, isem, vsem, dsem, fsem, csem,
 ):
-    def take(c, x):
-        part = (c, slice(None), slice(None), pl.ds(pl.multiple_of(x * 512, 512), 512))
-        return pltpu.make_async_copy(base.at[part], vbuf.at[part], vsem.at[c * 2 + x])
+    def take(x):
+        part = (2, slice(None), slice(None), pl.ds(pl.multiple_of(x * 512, 512), 512))
+        return pltpu.make_async_copy(base.at[part], vbuf.at[part[1:]], vsem.at[x])
 
     staged = ((edge_h, edge), (bound_h, bound), (part_h, part_t), (rows_h, rows))
     loads = [
         pltpu.make_async_copy(src, dst, isem.at[i]) for i, (src, dst) in enumerate(staged)
     ]
+    done = pl.ds(0, 2)
+    whole = pltpu.make_async_copy(base.at[done], derivative.at[done], csem.at[0])
     for load in loads:
         load.start()
-    for c in range(3):
-        for half in range(2):
-            take(c, half).start()
+    for half in range(2):
+        take(half).start()
+    whole.start()
 
     accs = (acc0, acc1, acc2, acc3)
     depth = acc0.shape[0]
@@ -674,15 +694,15 @@
         load.wait()
     spread(0, even)
 
-    def put_d(c, x):
-        part = (c, slice(None), slice(None), pl.ds(pl.multiple_of(x * 512, 512), 512))
-        return pltpu.make_async_copy(vbuf.at[part], derivative.at[part], dsem.at[c * 2 + x])
-
-    def join_steps(c, h, x):
+    def put_d(x):
+        part = (2, slice(None), slice(None), pl.ds(pl.multiple_of(x * 512, 512), 512))
+        return pltpu.make_async_copy(vbuf.at[part[1:]], derivative.at[part], dsem.at[x])
+
+    def join_steps(h, x):
         here = (pl.ds(pl.multiple_of(h * 8, 8), 8), pl.ds(pl.multiple_of(x * 128, 128), 128))
-        under, above = bound[c, h * 8 + x, 0], bound[c, h * 8 + x, 1]
+        under, above = bound[h * 8 + x, 0], bound[h * 8 + x, 1]
         for j in range(RY):
-            vbuf[c, j, *here] = vbuf[c, j, *here] + (
+            vbuf[j, *here] = vbuf[j, *here] + (
                 edge[0, j : j + 1, :] * under + edge[1, j : j + 1, :] * above
             )
             yield
@@ -695,18 +715,17 @@
         for _rest in steps:
             pass
 
-    @pl.loop(0, 6)
-    def _(q):
-        c, half = q // 2, q % 2
-        take(c, half).wait()
+    @pl.loop(0, 2)
+    def _(half):
+        take(half).wait()
 
         @pl.loop(0, 8)
         def _(t):
-            scatter_pair(q * 8 + t, join_steps(c, t // 4, half * 4 + t % 4))
-
-        put_d(c, half).start()
-
-    @pl.loop(48, 64)
+            scatter_pair(half * 8 + t, join_steps(t // 4, half * 4 + t % 4))
+
+        put_d(half).start()
+
+    @pl.loop(16, 64)
     def _(i):
         scatter_pair(i, iter(()))
 
@@ -734,9 +753,9 @@
 
         put_f(b).start()
 
-    for c in range(3):
-        for half in range(2):
-            put_d(c, half).wait()
+    whole.wait()
+    for half in range(2):
+        put_d(half).wait()
 
     @pl.loop(0, 16)
     def _(b):
@@ -761,8 +780,8 @@
         ]
         + [pltpu.VMEM((depth, 128), F32)] * 4
         + [pltpu.VMEM((256, 128), F32)] * 3
-        + [pltpu.VMEM(whole, F32)] * 2
-        + [pltpu.SemaphoreType.DMA((n,)) for n in (4, 6, 6, 16)],
+        + [pltpu.VMEM(whole[1:], F32), pltpu.VMEM(whole, F32)]
+        + [pltpu.SemaphoreType.DMA((n,)) for n in (4, 2, 2, 16, 1)],
         compiler_params=pltpu.CompilerParams(vmem_limit_bytes=58 << 20),
         name="local",
     )(base, bound, edge, part_t, rows, inv_vol)

time: 52.4 us -> 160 us (3.05)
  Pallas kernels: 50.8 us -> 158 us
    pallas_call x1, Pallas kernels: 21.6 us -> 129 us  [local(): pl.pallas_call(local_kernel, out_shape=(jax.ShapeDtypeStruct(whole, F32),...]
where the time goes in v8:
time: 160 us
  Pallas kernels  158 us (99%)
    pallas_call x1, Pallas kernels, local(): pl.pallas_call(local_kernel, out_shape=(jax.ShapeDtypeStruct(whole, F32),...  129 us
    pallas_call x1, Pallas kernels, exchange(): pl.pallas_call(exchange_kernel, out_shape=(jax.ShapeDtypeStruct((3, RY, S...  29.2 us

profile of v8, /device:TPU:0, one launch (start us, length us, event | category | flops | bytes accessed | tf_op | source)
XLA Modules:
  0.0 159.6 jit_solution(1839609071926051193)
XLA Ops:
  1.3 29.2 %exchange.1 = (f32[3,32,16,1024]{3,2,1,0:T(8,128)}, f32[16,2,8,128]{3,2,1,0:T(8,128)}, f32[2,32,128]{2,1,0:T(8,128)}, f32[256,128]{1,0:T(8,128)}, s32[128,128]{1,0:T(8,128)}) custom-call(f32[3,32,16,1024]{3,2,1,0:T(8,128)} %vel.1, f32[1,512]{1,0:T(1,128)} %bitcast.8, f32[1,512]{1,0:T(1,128)} %bitcast.9, f32[5,32]{1,0:T(8,128)} %st_h.1, f32[3,4096]{1,0:T(4,128)} %forces_h.1, ...), custom_call_target="tpu_custom_call" | custom-call | tf_op jit(solution)/shard_map/exchange/pallas_call | solution.py:567
  30.4 129.1 %local.1 = (f32[3,32,16,1024]{3,2,1,0:T(8,128)}, f32[3,32,16,1024]{3,2,1,0:T(8,128)}) custom-call(f32[3,32,16,1024]{3,2,1,0:T(8,128)} %get-tuple-element.7.base, f32[16,2,8,128]{3,2,1,0:T(8,128)} %get-tuple-element.8.bound_h, f32[2,32,128]{2,1,0:T(8,128)} %get-tuple-element.9.edge_h, f32[256,128]{1,0:T(8,128)} %get-tuple-element.10.part_h, s32[16384]{0:T(1024)} %bitcast.5, ...), custom_call_target="tpu_custom_call" | custom-call | tf_op jit(solution)/shard_map/local/pallas_call | solution.py:770

commit v9 on v8

--- a/solution.py
+++ b/solution.py
@@ -629,7 +629,7 @@
     base, bound_h, edge_h, part_h, rows_h, inv_vol,
     derivative, forcing,
     bound, edge, part_t, rows,
-    acc0, acc1, acc2, acc3, even, odd, mixed, vbuf, stage, isem, vsem, dsem, fsem, csem,
+    acc0, acc1, acc2, acc3, even, odd, mixed, vbuf, through, stage, isem, vsem, dsem, fsem, csem,
 ):
     def take(x):
         part = (2, slice(None), slice(None), pl.ds(pl.multiple_of(x * 512, 512), 512))
@@ -640,12 +640,13 @@
         pltpu.make_async_copy(src, dst, isem.at[i]) for i, (src, dst) in enumerate(staged)
     ]
     done = pl.ds(0, 2)
-    whole = pltpu.make_async_copy(base.at[done], derivative.at[done], csem.at[0])
+    whole_in = pltpu.make_async_copy(base.at[done], through, csem.at[0])
+    whole = pltpu.make_async_copy(through, derivative.at[done], csem.at[1])
     for load in loads:
         load.start()
     for half in range(2):
         take(half).start()
-    whole.start()
+    whole_in.start()
 
     accs = (acc0, acc1, acc2, acc3)
     depth = acc0.shape[0]
@@ -724,6 +725,9 @@
             scatter_pair(half * 8 + t, join_steps(t // 4, half * 4 + t % 4))
 
         put_d(half).start()
+
+    whole_in.wait()
+    whole.start()
 
     @pl.loop(16, 64)
     def _(i):
@@ -780,8 +784,12 @@
         ]
         + [pltpu.VMEM((depth, 128), F32)] * 4
         + [pltpu.VMEM((256, 128), F32)] * 3
-        + [pltpu.VMEM(whole[1:], F32), pltpu.VMEM(whole, F32)]
-        + [pltpu.SemaphoreType.DMA((n,)) for n in (4, 2, 2, 16, 1)],
+        + [
+            pltpu.VMEM(whole[1:], F32),
+            pltpu.VMEM((2, *whole[1:]), F32),
+            pltpu.VMEM(whole, F32),
+        ]
+        + [pltpu.SemaphoreType.DMA((n,)) for n in (4, 2, 2, 16, 2)],
         compiler_params=pltpu.CompilerParams(vmem_limit_bytes=58 << 20),
         name="local",
     )(base, bound, edge, part_t, rows, inv_vol)

time: 160 us -> 51 us (0.32)
  Pallas kernels: 158 us -> 49.5 us
    pallas_call x1, Pallas kernels: 129 us -> 20.3 us  [local(): pl.pallas_call(local_kernel, out_shape=(jax.ShapeDtypeStruct(whole, F32),...]
where the time goes in v9:
time: 51 us; the launch traced here: 50.8 us
  Pallas kernels  49.5 us (97%)
  between operations  1.29 us (3%)
    pallas_call x1, Pallas kernels, exchange(): pl.pallas_call(exchange_kernel, out_shape=(jax.ShapeDtypeStruct((3, RY, S...  29.2 us
    pallas_call x1, Pallas kernels, local(): pl.pallas_call(local_kernel, out_shape=(jax.ShapeDtypeStruct(whole, F32),...  20.3 us

profile of v9, /device:TPU:0, one launch (start us, length us, event | category | flops | bytes accessed | tf_op | source)
XLA Modules:
  0.0 50.8 jit_solution(2675728634210116662)
XLA Ops:
  1.3 29.2 %exchange.1 = (f32[3,32,16,1024]{3,2,1,0:T(8,128)}, f32[16,2,8,128]{3,2,1,0:T(8,128)}, f32[2,32,128]{2,1,0:T(8,128)}, f32[256,128]{1,0:T(8,128)}, s32[128,128]{1,0:T(8,128)}) custom-call(f32[3,32,16,1024]{3,2,1,0:T(8,128)} %vel.1, f32[1,512]{1,0:T(1,128)} %bitcast.8, f32[1,512]{1,0:T(1,128)} %bitcast.9, f32[5,32]{1,0:T(8,128)} %st_h.1, f32[3,4096]{1,0:T(4,128)} %forces_h.1, ...), custom_call_target="tpu_custom_call" | custom-call | tf_op jit(solution)/shard_map/exchange/pallas_call | solution.py:567
  30.4 20.3 %local.1 = (f32[3,32,16,1024]{3,2,1,0:T(8,128)}, f32[3,32,16,1024]{3,2,1,0:T(8,128)}) custom-call(f32[3,32,16,1024]{3,2,1,0:T(8,128)} %get-tuple-element.7.base, f32[16,2,8,128]{3,2,1,0:T(8,128)} %get-tuple-element.8.bound_h, f32[2,32,128]{2,1,0:T(8,128)} %get-tuple-element.9.edge_h, f32[256,128]{1,0:T(8,128)} %get-tuple-element.10.part_h, s32[16384]{0:T(1024)} %bitcast.5, ...), custom_call_target="tpu_custom_call" | custom-call | tf_op jit(solution)/shard_map/local/pallas_call | solution.py:774
